TPU v7x, 32 devices: a whole 2x2x4 slice. The times are simulated.
32 devices in a mesh: dp: 4 (over y, x), fsdp: 8 (over z, core).
Axes of the slice: x: 2, y: 2, z: 4, core: 2. Of those that a mesh axis runs over, the one named last changes fastest.
Arguments:
- tokens: bfloat16 [32768, 768], P(('dp', 'fsdp')), may hold values from -6 to 6
- cotangent: bfloat16 [32768, 768], P(('dp', 'fsdp')), may hold values from -6 to 6
- tie_map: int32 [12], replicated, may hold values from 0 to 3, as said below
- first_length: int32 [32], P(('dp', 'fsdp')), may hold values from 512 to 1024, as said below
- gain_attend: bfloat16 [4, 768], P(None, ('dp', 'fsdp')), may hold values from 0.5 to 1.5
- shift_attend: bfloat16 [4, 768], P(None, ('dp', 'fsdp')), may hold values from -3 to 3
- heads_weight: bfloat16 [4, 768, 2304], P(None, ('dp', 'fsdp')), may hold values from -0.21875 to 0.21875
- query_bias: bfloat16 [4, 768], P(None, ('dp', 'fsdp')), may hold values from -3 to 3
- value_bias: bfloat16 [4, 768], P(None, ('dp', 'fsdp')), may hold values from -3 to 3
- mixing_weight: bfloat16 [4, 768, 768], P(None, ('dp', 'fsdp')), may hold values from -0.625 to 0.625
- mixing_bias: bfloat16 [4, 768], P(None, ('dp', 'fsdp')), may hold values from -3 to 3
- gain_feed: bfloat16 [4, 768], P(None, ('dp', 'fsdp')), may hold values from 0.5 to 1.5
- shift_feed: bfloat16 [4, 768], P(None, ('dp', 'fsdp')), may hold values from -3 to 3
- expand_weight: bfloat16 [4, 768, 3072], P(None, ('dp', 'fsdp')), may hold values from -0.21875 to 0.21875
- expand_bias: bfloat16 [4, 3072], P(None, ('dp', 'fsdp')), may hold values from -3 to 3
- shrink_weight: bfloat16 [4, 3072, 768], P(None, ('dp', 'fsdp')), may hold values from -0.109375 to 0.109375
- shrink_bias: bfloat16 [4, 768], P(None, ('dp', 'fsdp')), may hold values from -3 to 3
Outputs:
- block_output: bfloat16 [32768, 768], P(('dp', 'fsdp'))
- tokens_grad: bfloat16 [32768, 768], P(('dp', 'fsdp'))
- dgain_attend: float32 [4, 768], P(None, ('dp', 'fsdp'))
- dshift_attend: float32 [4, 768], P(None, ('dp', 'fsdp'))
- dheads_weight: float32 [4, 768, 2304], P(None, ('dp', 'fsdp'))
- dquery_bias: float32 [4, 768], P(None, ('dp', 'fsdp'))
- dvalue_bias: float32 [4, 768], P(None, ('dp', 'fsdp'))
- dmixing_weight: float32 [4, 768, 768], P(None, ('dp', 'fsdp'))
- dmixing_bias: float32 [4, 768], P(None, ('dp', 'fsdp'))
- dgain_feed: float32 [4, 768], P(None, ('dp', 'fsdp'))
- dshift_feed: float32 [4, 768], P(None, ('dp', 'fsdp'))
- dexpand_weight: float32 [4, 768, 3072], P(None, ('dp', 'fsdp'))
- dexpand_bias: float32 [4, 3072], P(None, ('dp', 'fsdp'))
- dshrink_weight: float32 [4, 3072, 768], P(None, ('dp', 'fsdp'))
- dshrink_bias: float32 [4, 768], P(None, ('dp', 'fsdp'))
Inputs may be any that keep to these rules, and one draw needn't show every extreme that they name: `tie_map`: the first 2 entries name distinct sources; the others name sources too. `first_length`: each entry is 512 or 1024; both occur in every draw.
All inputs are finite; a program needn't handle non-finite values.
Results may differ from a plain program's by a relative error of at most 0.013.
Values may be sent and summed in bfloat16 or wider, within the bound.
A program may use at most 256 MiB of HBM per device.

v0:
```python
import jax
import jax.numpy as jnp
from jax import lax
from jax.sharding import PartitionSpec as P

HEADS = 12
HD = 64
LAYERS = 2
UNIQUE = 4


norm_eps = 1e-05
masked_score = -1000000000.0


def layer_norm(values, gain, shift):
    centre = values - jnp.mean(values, axis=-1, keepdims=True)
    spread = jnp.mean(centre * centre, axis=-1, keepdims=True)
    return centre * lax.rsqrt(spread + norm_eps) * gain + shift


def inner_rows(left, right):
    return lax.dot_general(
        left, right, (((0,), (0,)), ((), ())), preferred_element_type=jnp.float32
    )


def times_transposed(left, right):
    return lax.dot_general(
        left, right, (((1,), (1,)), ((), ())), preferred_element_type=jnp.float32
    )


def column_sums(values):
    return jnp.sum(values.astype(jnp.float32), axis=0)


def block_mask(first_len, block_start, query_count, key_count):
    query_place = block_start + lax.iota(jnp.int32, query_count)
    key_place = lax.iota(jnp.int32, key_count)
    query_part = query_place[None, :] >= first_len[:, None]
    key_part = key_place[None, :] >= first_len[:, None]
    causal = key_place[None, None, :] <= query_place[None, :, None]
    return causal & (query_part[:, :, None] == key_part[:, None, :])


def heads_to_rows(stacked):
    return jnp.moveaxis(stacked, 0, 2).reshape(-1, HEADS * HD)


def attend_forward(queries, keys, values, first_len):
    block_rows = queries.shape[1] // 2
    score_scale = HD ** (-0.5)

    def one_head(head_index):
        query_head = lax.dynamic_slice_in_dim(queries, head_index * HD, HD, 2)
        key_head = lax.dynamic_slice_in_dim(keys, head_index * HD, HD, 2)
        value_head = lax.dynamic_slice_in_dim(values, head_index * HD, HD, 2)
        outputs = []
        totals = []
        for block_index in range(2):
            block_start = block_index * block_rows
            key_count = block_start + block_rows
            query_block = query_head[:, block_start : block_start + block_rows]
            scores = (
                jnp.einsum(
                    "rqd,rkd->rqk",
                    query_block,
                    key_head[:, :key_count],
                    preferred_element_type=jnp.float32,
                )
                * score_scale
            )
            scores = jnp.where(
                block_mask(first_len, block_start, block_rows, key_count), scores, masked_score
            )
            highest = jnp.max(scores, axis=-1, keepdims=True)
            weights = jnp.exp(scores - highest)
            weight_sum = jnp.sum(weights, axis=-1, keepdims=True)
            probs = (weights / weight_sum).astype(jnp.bfloat16)
            outputs.append(
                jnp.einsum(
                    "rqk,rkd->rqd",
                    probs,
                    value_head[:, :key_count],
                    preferred_element_type=jnp.float32,
                )
            )
            totals.append(highest[..., 0] + jnp.log(weight_sum[..., 0]))
        return (
            jnp.concatenate(outputs, axis=1).astype(jnp.bfloat16),
            jnp.concatenate(totals, axis=1),
        )

    head_out, head_lse = lax.map(one_head, lax.iota(jnp.int32, HEADS))
    return (heads_to_rows(head_out), head_lse)


def attend_backward(queries, keys, values, out_grad, head_lse, first_len):
    length = queries.shape[1]
    block_rows = length // 2
    score_scale = HD ** (-0.5)

    def one_head(packed):
        head_index, lse_head = packed
        query_head = lax.dynamic_slice_in_dim(queries, head_index * HD, HD, 2)
        key_head = lax.dynamic_slice_in_dim(keys, head_index * HD, HD, 2)
        value_head = lax.dynamic_slice_in_dim(values, head_index * HD, HD, 2)
        grad_head = lax.dynamic_slice_in_dim(out_grad, head_index * HD, HD, 2)
        query_parts = []
        key_grad = jnp.zeros(key_head.shape, jnp.float32)
        value_grad = jnp.zeros(value_head.shape, jnp.float32)
        for block_index in range(2):
            block_start = block_index * block_rows
            key_count = block_start + block_rows
            query_block = query_head[:, block_start : block_start + block_rows]
            grad_block = grad_head[:, block_start : block_start + block_rows]
            key_block = key_head[:, :key_count]
            value_block = value_head[:, :key_count]
            scores = (
                jnp.einsum(
                    "rqd,rkd->rqk", query_block, key_block, preferred_element_type=jnp.float32
                )
                * score_scale
            )
            scores = jnp.where(
                block_mask(first_len, block_start, block_rows, key_count), scores, masked_score
            )
            probs = jnp.exp(scores - lse_head[:, block_start : block_start + block_rows, None])
            probs_low = probs.astype(jnp.bfloat16)
            prob_grad = jnp.einsum(
                "rqd,rkd->rqk", grad_block, value_block, preferred_element_type=jnp.float32
            )
            centre_term = jnp.sum(probs * prob_grad, axis=-1, keepdims=True)
            score_grad = (probs * (prob_grad - centre_term)).astype(jnp.bfloat16)
            query_parts.append(
                jnp.einsum(
                    "rqk,rkd->rqd", score_grad, key_block, preferred_element_type=jnp.float32
                )
                * score_scale
            )
            key_part = (
                jnp.einsum(
                    "rqk,rqd->rkd", score_grad, query_block, preferred_element_type=jnp.float32
                )
                * score_scale
            )
            value_part = jnp.einsum(
                "rqk,rqd->rkd", probs_low, grad_block, preferred_element_type=jnp.float32
            )
            padding = ((0, 0), (0, length - key_count), (0, 0))
            key_grad = key_grad + jnp.pad(key_part, padding)
            value_grad = value_grad + jnp.pad(value_part, padding)
        return (jnp.concatenate(query_parts, axis=1), key_grad, value_grad)

    query_grad, key_grad, value_grad = lax.map(one_head, (lax.iota(jnp.int32, HEADS), head_lse))
    return jnp.concatenate(
        [heads_to_rows(query_grad), heads_to_rows(key_grad), heads_to_rows(value_grad)], axis=1
    )


def forward_use(hidden, params, first_len):
    (
        gain_a,
        shift_a,
        heads_w,
        query_b,
        value_b,
        mix_w,
        mix_b,
        gain_f,
        shift_f,
        expand_w,
        expand_b,
        shrink_w,
        shrink_b,
    ) = params
    row_count = first_len.shape[0]
    width = heads_w.shape[0]
    normed_low = layer_norm(hidden, gain_a.astype(jnp.float32), shift_a.astype(jnp.float32)).astype(
        jnp.bfloat16
    )
    query_f = query_b.astype(jnp.float32)
    bias = jnp.concatenate([query_f, jnp.zeros_like(query_f), value_b.astype(jnp.float32)])
    projected = (jnp.dot(normed_low, heads_w, preferred_element_type=jnp.float32) + bias).astype(
        jnp.bfloat16
    )
    queries = projected[:, :width].reshape(row_count, -1, width)
    keys = projected[:, width : 2 * width].reshape(row_count, -1, width)
    values = projected[:, 2 * width :].reshape(row_count, -1, width)
    attended, head_lse = attend_forward(queries, keys, values, first_len)
    middle = (
        hidden
        + jnp.dot(attended, mix_w, preferred_element_type=jnp.float32)
        + mix_b.astype(jnp.float32)
    )
    normed_two = layer_norm(middle, gain_f.astype(jnp.float32), shift_f.astype(jnp.float32)).astype(
        jnp.bfloat16
    )
    expanded = jnp.dot(normed_two, expand_w, preferred_element_type=jnp.float32) + expand_b.astype(
        jnp.float32
    )
    activated = jax.nn.gelu(expanded, approximate=True).astype(jnp.bfloat16)
    result = (
        middle
        + jnp.dot(activated, shrink_w, preferred_element_type=jnp.float32)
        + shrink_b.astype(jnp.float32)
    )
    kept = (
        hidden,
        normed_low,
        projected,
        attended,
        head_lse,
        middle,
        normed_two,
        expanded,
        activated,
    )
    return (result, kept)


def backward_use(grad_out, kept, params, first_len):
    (
        gain_a,
        shift_a,
        heads_w,
        query_b,
        value_b,
        mix_w,
        mix_b,
        gain_f,
        shift_f,
        expand_w,
        expand_b,
        shrink_w,
        shrink_b,
    ) = params
    hidden, normed_low, projected, attended, head_lse, middle, normed_two, expanded, activated = (
        kept
    )
    row_count = first_len.shape[0]
    width = heads_w.shape[0]
    grad_low = grad_out.astype(jnp.bfloat16)
    shrink_w_term = inner_rows(activated, grad_low)
    shrink_b_term = column_sums(grad_low)
    activated_grad = times_transposed(grad_low, shrink_w)
    unused, gelu_back = jax.vjp(lambda inputs: jax.nn.gelu(inputs, approximate=True), expanded)
    expand_grad = gelu_back(activated_grad)[0].astype(jnp.bfloat16)
    expand_w_term = inner_rows(normed_two, expand_grad)
    expand_b_term = column_sums(expand_grad)
    normed_grad = times_transposed(expand_grad, expand_w)
    unused, norm_back = jax.vjp(
        layer_norm, middle, gain_f.astype(jnp.float32), shift_f.astype(jnp.float32)
    )
    middle_norm, gain_f_term, shift_f_term = norm_back(normed_grad)
    middle_grad = grad_out + middle_norm
    middle_low = middle_grad.astype(jnp.bfloat16)
    mix_w_term = inner_rows(attended, middle_low)
    mix_b_term = column_sums(middle_low)
    attended_grad = times_transposed(middle_low, mix_w).astype(jnp.bfloat16)
    queries = projected[:, :width].reshape(row_count, -1, width)
    keys = projected[:, width : 2 * width].reshape(row_count, -1, width)
    values = projected[:, 2 * width :].reshape(row_count, -1, width)
    grad_rows = attended_grad.reshape(row_count, -1, width)
    projected_grad = attend_backward(queries, keys, values, grad_rows, head_lse, first_len).astype(
        jnp.bfloat16
    )
    heads_w_term = inner_rows(normed_low, projected_grad)
    query_b_term = column_sums(projected_grad[:, :width])
    value_b_term = column_sums(projected_grad[:, 2 * width :])
    first_grad = times_transposed(projected_grad, heads_w)
    unused, first_back = jax.vjp(
        layer_norm, hidden, gain_a.astype(jnp.float32), shift_a.astype(jnp.float32)
    )
    hidden_norm, gain_a_term, shift_a_term = first_back(first_grad)
    terms = (
        gain_a_term,
        shift_a_term,
        heads_w_term,
        query_b_term,
        value_b_term,
        mix_w_term,
        mix_b_term,
        gain_f_term,
        shift_f_term,
        expand_w_term,
        expand_b_term,
        shrink_w_term,
        shrink_b_term,
    )
    return (middle_grad + hidden_norm, terms)


def gather_forward(local):
    return (
        lax.all_gather(local[0], ("dp", "fsdp"), axis=0, tiled=True),
        lax.all_gather(local[1], ("dp", "fsdp"), axis=0, tiled=True),
        lax.all_gather(local[2], ("dp", "fsdp"), axis=0, tiled=True),
        lax.all_gather(local[3], ("dp", "fsdp"), axis=0, tiled=True),
        lax.all_gather(local[4], ("dp", "fsdp"), axis=0, tiled=True),
        lax.all_gather(local[5], ("dp", "fsdp"), axis=0, tiled=True),
        lax.all_gather(local[6], ("dp", "fsdp"), axis=0, tiled=True),
        lax.all_gather(local[7], ("dp", "fsdp"), axis=0, tiled=True),
        lax.all_gather(local[8], ("dp", "fsdp"), axis=0, tiled=True),
        lax.all_gather(local[9], ("dp", "fsdp"), axis=0, tiled=True),
        lax.all_gather(local[10], ("dp", "fsdp"), axis=0, tiled=True),
        lax.all_gather(local[11], ("dp", "fsdp"), axis=0, tiled=True),
        lax.all_gather(local[12], ("dp", "fsdp"), axis=0, tiled=True),
    )


def gather_backward(local):
    return (
        lax.all_gather(local[0], ("dp", "fsdp"), axis=0, tiled=True),
        lax.all_gather(local[1], ("dp", "fsdp"), axis=0, tiled=True),
        lax.all_gather(local[2], ("dp", "fsdp"), axis=0, tiled=True),
        lax.all_gather(local[3], ("dp", "fsdp"), axis=0, tiled=True),
        lax.all_gather(local[4], ("dp", "fsdp"), axis=0, tiled=True),
        lax.all_gather(local[5], ("dp", "fsdp"), axis=0, tiled=True),
        lax.all_gather(local[6], ("dp", "fsdp"), axis=0, tiled=True),
        lax.all_gather(local[7], ("dp", "fsdp"), axis=0, tiled=True),
        lax.all_gather(local[8], ("dp", "fsdp"), axis=0, tiled=True),
        lax.all_gather(local[9], ("dp", "fsdp"), axis=0, tiled=True),
        lax.all_gather(local[10], ("dp", "fsdp"), axis=0, tiled=True),
        lax.all_gather(local[11], ("dp", "fsdp"), axis=0, tiled=True),
        lax.all_gather(local[12], ("dp", "fsdp"), axis=0, tiled=True),
    )


def sum_terms(terms):
    return (
        lax.psum_scatter(terms[0], ("dp", "fsdp"), scatter_dimension=0, tiled=True),
        lax.psum_scatter(terms[1], ("dp", "fsdp"), scatter_dimension=0, tiled=True),
        lax.psum_scatter(terms[2], ("dp", "fsdp"), scatter_dimension=0, tiled=True),
        lax.psum_scatter(terms[3], ("dp", "fsdp"), scatter_dimension=0, tiled=True),
        lax.psum_scatter(terms[4], ("dp", "fsdp"), scatter_dimension=0, tiled=True),
        lax.psum_scatter(terms[5], ("dp", "fsdp"), scatter_dimension=0, tiled=True),
        lax.psum_scatter(terms[6], ("dp", "fsdp"), scatter_dimension=0, tiled=True),
        lax.psum_scatter(terms[7], ("dp", "fsdp"), scatter_dimension=0, tiled=True),
        lax.psum_scatter(terms[8], ("dp", "fsdp"), scatter_dimension=0, tiled=True),
        lax.psum_scatter(terms[9], ("dp", "fsdp"), scatter_dimension=0, tiled=True),
        lax.psum_scatter(terms[10], ("dp", "fsdp"), scatter_dimension=0, tiled=True),
        lax.psum_scatter(terms[11], ("dp", "fsdp"), scatter_dimension=0, tiled=True),
        lax.psum_scatter(terms[12], ("dp", "fsdp"), scatter_dimension=0, tiled=True),
    )


def pick_shards(stacks, source):
    return tuple((lax.dynamic_index_in_dim(stack, source, 0, keepdims=False) for stack in stacks))


def place_source(source, values):
    chosen = (lax.iota(jnp.int32, UNIQUE) == source).astype(jnp.float32)
    return tuple((chosen.reshape((UNIQUE,) + (1,) * item.ndim) * item[None] for item in values))


def body(
    tokens,
    cotangent,
    tie_map,
    first_length,
    gain_attend,
    shift_attend,
    heads_weight,
    query_bias,
    value_bias,
    mixing_weight,
    mixing_bias,
    gain_feed,
    shift_feed,
    expand_weight,
    expand_bias,
    shrink_weight,
    shrink_bias,
):
    stacks = (
        gain_attend,
        shift_attend,
        heads_weight,
        query_bias,
        value_bias,
        mixing_weight,
        mixing_bias,
        gain_feed,
        shift_feed,
        expand_weight,
        expand_bias,
        shrink_weight,
        shrink_bias,
    )
    hidden = tokens.astype(jnp.float32)
    kept_uses = []
    for layer_index in range(LAYERS):
        source = tie_map[layer_index]
        gathered = gather_forward(pick_shards(stacks, source))
        hidden, kept = forward_use(hidden, gathered, first_length)
        kept_uses.append(kept)
    block_output = hidden.astype(jnp.bfloat16)
    grad_hidden = cotangent.astype(jnp.float32)
    totals = tuple((jnp.zeros(stack.shape, jnp.float32) for stack in stacks))
    for layer_index in reversed(range(LAYERS)):
        source = tie_map[layer_index]
        gathered = gather_backward(pick_shards(stacks, source))
        grad_hidden, terms = backward_use(
            grad_hidden, kept_uses[layer_index], gathered, first_length
        )
        shares = sum_terms(terms)
        totals = tuple((total + item for total, item in zip(totals, place_source(source, shares))))
    return (
        block_output,
        grad_hidden.astype(jnp.bfloat16),
        totals[0],
        totals[1],
        totals[2],
        totals[3],
        totals[4],
        totals[5],
        totals[6],
        totals[7],
        totals[8],
        totals[9],
        totals[10],
        totals[11],
        totals[12],
    )


def solution(mesh):
    return jax.shard_map(
        body,
        mesh=mesh,
        in_specs=(
            P(("dp", "fsdp"), None),
            P(("dp", "fsdp"), None),
            P(),
            P(("dp", "fsdp")),
            P(None, ("dp", "fsdp")),
            P(None, ("dp", "fsdp")),
            P(None, ("dp", "fsdp"), None),
            P(None, ("dp", "fsdp")),
            P(None, ("dp", "fsdp")),
            P(None, ("dp", "fsdp"), None),
            P(None, ("dp", "fsdp")),
            P(None, ("dp", "fsdp")),
            P(None, ("dp", "fsdp")),
            P(None, ("dp", "fsdp"), None),
            P(None, ("dp", "fsdp")),
            P(None, ("dp", "fsdp"), None),
            P(None, ("dp", "fsdp")),
        ),
        out_specs=(
            P(("dp", "fsdp"), None),
            P(("dp", "fsdp"), None),
            P(None, ("dp", "fsdp")),
            P(None, ("dp", "fsdp")),
            P(None, ("dp", "fsdp"), None),
            P(None, ("dp", "fsdp")),
            P(None, ("dp", "fsdp")),
            P(None, ("dp", "fsdp"), None),
            P(None, ("dp", "fsdp")),
            P(None, ("dp", "fsdp")),
            P(None, ("dp", "fsdp")),
            P(None, ("dp", "fsdp"), None),
            P(None, ("dp", "fsdp")),
            P(None, ("dp", "fsdp"), None),
            P(None, ("dp", "fsdp")),
        ),
        check_vma=False,
    )
```

profile of v0, /device:TPU:0, one launch (start us, length us, event | category | flops | bytes accessed | tf_op | source)
XLA Modules:
  0.0 2255.2 jit_solution(4374493837738662019)
XLA Ops:
  29.7 44.5 %all-reduce.41 = (bf16[768]{0:T(1024)(128)(2,1)S(1)}, bf16[768]{0:T(1024)(128)(2,1)S(1)}, bf16[768]{0:T(1024)(128)(2,1)S(1)}, bf16[768]{0:T(1024)(128)(2,1)S(1)}...) all-reduce(bf16[768]{0:T(1024)(128)(2,1)S(1)} %dynamic-update-slice, ...), channel_id=6, replica_groups=mesh['dp'=4,'fsdp'=8] {'dp','fsdp'}, use_global_device_ids=true, to_apply=%add.7 | all-reduce | flops 18432 | bytes 73728
  88.5 99.8 %while.56 = (s32[]{:T(128)}, bf16[12,1,1024,64]{2,3,1,0:T(8,128)(2,1)}, f32[12,1,1024]{2,1,0:T(1,128)S(1)}, s32[1]{0:T(128)}, s32[12]{0:T(128)S(1)}, /*index=5*/...) while((s32[]{:T(128)}, ...), condition=%wide.region_7.8_spmd, body=%wide.region_2.7_spmd.sunk | while | flops 210308096 | bytes 10931927 | solution.py:95
  199.4 11.6 fusion.139
  211.0 53.9 %all-gather.41.cloned.1.call-done = bf16[1,3072,768]{2,1,0:T(8,128)(2,1)} async-done(((bf16[1,96,768]{2,1,0:T(8,128)(2,1)}), bf16[1,3072,768]{2,1,0:T(8,128)(2,1)}) %all-gather.41.cloned.1.call-update) | async-done | bytes 4718608 | tf_op jit(solution)/shard_map/all_gather | solution.py:308
  264.9 11.1 fusion.222
  278.1 48.0 %all-gather.43.cloned.1.call-done = bf16[1,768,2304]{2,1,0:T(8,128)(2,1)} async-done(((bf16[1,24,2304]{2,1,0:T(8,128)(2,1)}), bf16[1,768,2304]{2,1,0:T(8,128)(2,1)}) %all-gather.43.cloned.1.call-update) | async-done | bytes 3538960 | tf_op jit(solution)/shard_map/all_gather | solution.py:299
  336.1 97.8 %while.57 = (s32[]{:T(128)}, bf16[12,1,1024,64]{2,3,1,0:T(8,128)(2,1)}, f32[12,1,1024]{2,1,0:T(1,128)S(1)}, s32[1]{0:T(128)}, s32[12]{0:T(128)S(1)}, /*index=5*/...) while((s32[]{:T(128)}, ...), condition=%wide.region_17.18_spmd, body=%wide.region_12.17_spmd.sunk | while | flops 210308096 | bytes 10931927 | solution.py:95
  448.3 10.6 fusion.131
  458.9 55.0 %all-gather.49.cloned.1.call-done = bf16[1,3072,768]{2,1,0:T(8,128)(2,1)} async-done(((bf16[1,96,768]{2,1,0:T(8,128)(2,1)}), bf16[1,3072,768]{2,1,0:T(8,128)(2,1)}) %all-gather.49.cloned.1.call-update) | async-done | bytes 4718608 | tf_op jit(solution)/shard_map/all_gather | solution.py:308
  513.9 17.8 convert_reduce_fusion.1
  556.2 210.2 %while.58 = (s32[]{:T(128)}, bf16[12,1,1024,64]{2,3,1,0:T(8,128)(2,1)}, bf16[12,1,1024,64]{2,3,1,0:T(8,128)(2,1)}, bf16[12,1,1024,64]{2,3,1,0:T(8,128)(2,1)}, s3...) while((s32[]{:T(128)}, ...), condition=%wide.region_25.26_spmd, body=%wide.region_22.25_spmd.sunk | while | flops 513378304 | bytes 27307272 | solution.py:156
  771.1 8.6 fusion.225
  791.1 18.4 convert_reduce_fusion
  809.4 9.0 fusion.226
  835.5 218.0 %while.59 = (s32[]{:T(128)}, bf16[12,1,1024,64]{2,3,1,0:T(8,128)(2,1)}, bf16[12,1,1024,64]{2,3,1,0:T(8,128)(2,1)}, bf16[12,1,1024,64]{2,3,1,0:T(8,128)(2,1)}, s3...) while((s32[]{:T(128)}, ...), condition=%wide.region_33.34_spmd, body=%wide.region_30.33_spmd.sunk | while | flops 513378304 | bytes 27307272 | solution.py:156
  1058.2 8.6 fusion.224
  1085.5 10.2 fusion.159
  1096.4 8.8 fusion.158
  1105.5 14.6 fusion.200
  1121.5 12.9 fusion.208
  1135.1 10.5 fusion.207
  1146.3 10.5 fusion.206
  1165.7 11.3 add_convert_fusion.3
  1178.5 44.8 %all-reduce.44.cloned.1.call-done = (f32[768]{0:T(1024)}, f32[768]{0:T(1024)}, f32[768]{0:T(1024)}, f32[768]{0:T(1024)}, f32[768]{0:T(1024)}, /*index=5*/f32[768...) async-done(((f32[768]{0:T(1024)}, f32[768]{0:T(1024)}, ...) | async-done | bytes 73744
  1238.2 91.8 %reduce-scatter.15.cloned.1.call-done = f32[24,768]{1,0:T(8,128)} async-done(((f32[768,768]{1,0:T(8,128)}), f32[24,768]{1,0:T(8,128)}) %reduce-scatter.15.cloned.1.call-update) | async-done | bytes 73744 | tf_op jit(solution)/shard_map/reduce_scatter | solution.py:338
  1329.9 103.9 %reduce-scatter.13.cloned.1.call-done = f32[24,768]{1,0:T(8,128)} async-done(((f32[768,768]{1,0:T(8,128)}), f32[24,768]{1,0:T(8,128)}) %reduce-scatter.13.cloned.1.call-update) | async-done | bytes 73744 | tf_op jit(solution)/shard_map/reduce_scatter | solution.py:338
  1435.6 122.3 %reduce-scatter.9.cloned.1.call-done = f32[24,2304]{1,0:T(8,128)} async-done(((f32[768,2304]{1,0:T(8,128)}), f32[24,2304]{1,0:T(8,128)}) %reduce-scatter.9.cloned.1.call-update) | async-done | bytes 221200 | tf_op jit(solution)/shard_map/reduce_scatter | solution.py:335
  1557.9 124.2 %reduce-scatter.11.cloned.1.call-done = f32[24,2304]{1,0:T(8,128)} async-done(((f32[768,2304]{1,0:T(8,128)}), f32[24,2304]{1,0:T(8,128)}) %reduce-scatter.11.cloned.1.call-update) | async-done | bytes 221200 | tf_op jit(solution)/shard_map/reduce_scatter | solution.py:335
  1684.2 139.2 %reduce-scatter.23.cloned.1.call-done = f32[96,768]{1,0:T(8,128)} async-done(((f32[3072,768]{1,0:T(8,128)}), f32[96,768]{1,0:T(8,128)}) %reduce-scatter.23.cloned.1.call-update) | async-done | bytes 294928 | tf_op jit(solution)/shard_map/reduce_scatter | solution.py:344
  1823.3 140.9 %reduce-scatter.21.cloned.1.call-done = f32[96,768]{1,0:T(8,128)} async-done(((f32[3072,768]{1,0:T(8,128)}), f32[96,768]{1,0:T(8,128)}) %reduce-scatter.21.cloned.1.call-update) | async-done | bytes 294928 | tf_op jit(solution)/shard_map/reduce_scatter | solution.py:344
  1966.6 138.7 %reduce-scatter.17.cloned.1.call-done = f32[24,3072]{1,0:T(8,128)} async-done(((f32[768,3072]{1,0:T(8,128)}), f32[24,3072]{1,0:T(8,128)}) %reduce-scatter.17.cloned.1.call-update) | async-done | bytes 294928 | tf_op jit(solution)/shard_map/reduce_scatter | solution.py:342
  2105.2 140.9 %reduce-scatter.19.cloned.1.call-done = f32[24,3072]{1,0:T(8,128)} async-done(((f32[768,3072]{1,0:T(8,128)}), f32[24,3072]{1,0:T(8,128)}) %reduce-scatter.19.cloned.1.call-update) | async-done | bytes 294928 | tf_op jit(solution)/shard_map/reduce_scatter | solution.py:342
  (1152 shorter events, 779.0 us)
Async XLA Ops:
  7.2 67.0 %copy-start.27 = (bf16[1024,768]{1,0:T(8,128)(2,1)S(1)}, bf16[1024,768]{1,0:T(8,128)(2,1)}, u32[]{:S(2)}) copy-start(bf16[1024,768]{1,0:T(8,128)(2,1)} %param.25) | copy-start | bytes 4718596
  7.2 71.5 %all-gather.35.cloned.1.call-start = ((), (), s32[]{:S(2)}) async-start(), calls=%async_computation.16 | async-start | bytes 3649536 | tf_op jit(solution)/shard_map/all_gather | solution.py:299
  14.2 174.1 %all-gather.37.cloned.1.call-start = ((), (), s32[]{:S(2)}) async-start(), calls=%async_computation.17 | async-start | bytes 1216512 | tf_op jit(solution)/shard_map/all_gather | solution.py:302
  15.7 183.7 %all-gather.39.cloned.1.call-start = ((), (), s32[]{:S(2)}) async-start(), calls=%async_computation.18 | async-start | bytes 4866048 | tf_op jit(solution)/shard_map/all_gather | solution.py:306
  17.5 247.5 %all-gather.41.cloned.1.call-start = ((), (), s32[]{:S(2)}) async-start(), calls=%async_computation.19 | async-start | bytes 4866048 | tf_op jit(solution)/shard_map/all_gather | solution.py:308
  19.2 306.9 %all-gather.43.cloned.1.call-start = ((), (), s32[]{:S(2)}) async-start(), calls=%async_computation.20 | async-start | bytes 3649536 | tf_op jit(solution)/shard_map/all_gather | solution.py:299
  19.8 414.1 %all-gather.45.cloned.1.call-start = ((), (), s32[]{:S(2)}) async-start(), calls=%async_computation.21 | async-start | bytes 1216512 | tf_op jit(solution)/shard_map/all_gather | solution.py:302
  20.4 427.9 %all-gather.47.cloned.1.call-start = ((), (), s32[]{:S(2)}) async-start(), calls=%async_computation.22 | async-start | bytes 4866048 | tf_op jit(solution)/shard_map/all_gather | solution.py:306
  21.2 492.7 %all-gather.49.cloned.1.call-start = ((), (), s32[]{:S(2)}) async-start(), calls=%async_computation.23 | async-start | bytes 4866048 | tf_op jit(solution)/shard_map/all_gather | solution.py:308
  21.9 1201.4 %all-reduce.44.cloned.1.call-start = ((), (), s32[]{:S(2)}) async-start(), calls=%async_computation.24 | async-start | bytes 180224
  75.0 113.3 %copy-start = (bf16[1024,768]{0,1:T(8,128)(2,1)}, bf16[1024,768]{0,1:T(8,128)(2,1)S(1)}, u32[]{:S(2)}) copy-start(bf16[1024,768]{0,1:T(8,128)(2,1)S(1)} %copy.46) | copy-start | bytes 4718596
  76.3 123.1 %copy-start.38 = (f32[768]{0:T(1024)}, f32[768]{0:T(1024)S(1)}, u32[]{:S(2)}) copy-start(f32[768]{0:T(1024)S(1)} %convert_element_type.340) | copy-start | bytes 9220
  76.3 123.1 %copy-start.46 = (f32[768]{0:T(1024)}, f32[768]{0:T(1024)S(1)}, u32[]{:S(2)}) copy-start(f32[768]{0:T(1024)S(1)} %convert_element_type.341) | copy-start | bytes 9220
  76.3 188.6 %copy-start.65 = (f32[3072]{0:T(1024)}, f32[3072]{0:T(1024)S(1)}, u32[]{:S(2)}) copy-start(f32[3072]{0:T(1024)S(1)} %convert_element_type.342) | copy-start | bytes 36868
  76.4 249.8 %copy-start.69 = (f32[768]{0:T(1024)}, f32[768]{0:T(1024)S(1)}, u32[]{:S(2)}) copy-start(f32[768]{0:T(1024)S(1)} %convert_element_type.345) | copy-start | bytes 9220
  76.4 469.8 %copy-start.40 = (f32[768]{0:T(1024)}, f32[768]{0:T(1024)S(1)}, u32[]{:S(2)}) copy-start(f32[768]{0:T(1024)S(1)} %convert_element_type.349) | copy-start | bytes 9220
  76.4 371.9 %copy-start.48 = (f32[768]{0:T(1024)}, f32[768]{0:T(1024)S(1)}, u32[]{:S(2)}) copy-start(f32[768]{0:T(1024)S(1)} %convert_element_type.350) | copy-start | bytes 9220
  77.0 436.9 %copy-start.63 = (f32[3072]{0:T(1024)}, f32[3072]{0:T(1024)S(1)}, u32[]{:S(2)}) copy-start(f32[3072]{0:T(1024)S(1)} %convert_element_type.351) | copy-start | bytes 36868
  194.5 70.4 %copy-start.3 = (f32[1024,768]{0,1:T(8,128)S(1)}, f32[1024,768]{0,1:T(8,128)}, u32[]{:S(2)}) copy-start(f32[1024,768]{0,1:T(8,128)} %copy-done.2) | copy-start | bytes 9437188
  278.1 55.1 %copy-start.61 = (f32[1024]{0:T(1024)}, f32[1024]{0:T(1024)S(1)}, u32[]{:S(2)}) copy-start(f32[1024]{0:T(1024)S(1)} %multiply_reduce_fusion.11) | copy-start | bytes 12292
  439.8 106.4 %copy-start.5 = (f32[1024,768]{0,1:T(8,128)}, f32[1024,768]{0,1:T(8,128)S(1)}, u32[]{:S(2)}) copy-start(f32[1024,768]{0,1:T(8,128)S(1)} %get-tuple-element.629) | copy-start | bytes 9437188
  439.8 106.4 %copy-start.36 = (f32[1024]{0:T(1024)}, f32[1024]{0:T(1024)S(1)}, u32[]{:S(2)}) copy-start(f32[1024]{0:T(1024)S(1)} %broadcast_multiply_fusion) | copy-start | bytes 12292
  440.2 106.0 %copy-start.44 = (f32[1024]{0:T(1024)}, f32[1024]{0:T(1024)S(1)}, u32[]{:S(2)}) copy-start(f32[1024]{0:T(1024)S(1)} %fusion.177) | copy-start | bytes 12292
  788.6 20.8 slice-start
  1075.3 254.6 %reduce-scatter.15.cloned.1.call-start = ((), (), s32[]{:S(2)}) async-start(), calls=%async_computation.11 | async-start | bytes 2433024 | tf_op jit(solution)/shard_map/reduce_scatter | solution.py:338
  1080.6 353.3 %reduce-scatter.13.cloned.1.call-start = ((), (), s32[]{:S(2)}) async-start(), calls=%async_computation.10 | async-start | bytes 2433024 | tf_op jit(solution)/shard_map/reduce_scatter | solution.py:338
  1085.5 472.4 %reduce-scatter.9.cloned.1.call-start = ((), (), s32[]{:S(2)}) async-start(), calls=%async_computation.8 | async-start | bytes 7299072 | tf_op jit(solution)/shard_map/reduce_scatter | solution.py:335
  1095.8 586.3 %reduce-scatter.11.cloned.1.call-start = ((), (), s32[]{:S(2)}) async-start(), calls=%async_computation.9 | async-start | bytes 7299072 | tf_op jit(solution)/shard_map/reduce_scatter | solution.py:335
  1105.3 718.1 %reduce-scatter.23.cloned.1.call-start = ((), (), s32[]{:S(2)}) async-start(), calls=%async_computation.15 | async-start | bytes 9732096 | tf_op jit(solution)/shard_map/reduce_scatter | solution.py:344
  1120.2 844.1 %reduce-scatter.21.cloned.1.call-start = ((), (), s32[]{:S(2)}) async-start(), calls=%async_computation.14 | async-start | bytes 9732096 | tf_op jit(solution)/shard_map/reduce_scatter | solution.py:344
  1134.4 970.8 %reduce-scatter.17.cloned.1.call-start = ((), (), s32[]{:S(2)}) async-start(), calls=%async_computation.12 | async-start | bytes 9732096 | tf_op jit(solution)/shard_map/reduce_scatter | solution.py:342
  1145.6 1100.6 %reduce-scatter.19.cloned.1.call-start = ((), (), s32[]{:S(2)}) async-start(), calls=%async_computation.13 | async-start | bytes 9732096 | tf_op jit(solution)/shard_map/reduce_scatter | solution.py:342
  (64 other events, 282.6 us)
Sparse Core Ops, SparseCore 0:
  14.3 62.9 all-gather.34
  80.3 52.9 all-gather.36
  136.8 62.4 all-gather.38
  202.8 62.0 all-gather.40
  267.8 58.3 all-gather.42
  329.0 52.9 all-gather.44
  385.6 62.6 all-gather.46
  451.9 61.9 all-gather.48
  1075.5 147.7 all-reduce.43
  1228.4 101.4 reduce-scatter.14
  1335.2 98.6 reduce-scatter.12
  1439.4 118.4 reduce-scatter.8
  1563.5 118.4 reduce-scatter.10
  1687.8 135.4 reduce-scatter.22
  1829.1 135.1 reduce-scatter.20
  1970.0 135.1 reduce-scatter.16
  2111.0 135.1 reduce-scatter.18
where the time goes:
time: 2270 us; the launch traced here: 2260 us
  waiting for transfers between devices  1220 us (54%)
  matrix products  648 us (29%)
  other arithmetic  175 us (8%)
  local copies, waits for them, and re-layouts  114 us (5%)
  blocking collectives  44.5 us (2%)
  loops' own time  34.8 us (2%)
    reduce_scatter x2, waiting for transfers between devices, sum_terms(): lax.psum_scatter(terms[11], ('dp', 'fsdp'), scatter_dimension=0, tiled=True)  280 us
    reduce_scatter x2, waiting for transfers between devices, sum_terms(): lax.psum_scatter(terms[9], ('dp', 'fsdp'), scatter_dimension=0, tiled=True)  280 us
    reduce_scatter x2, waiting for transfers between devices, sum_terms(): lax.psum_scatter(terms[2], ('dp', 'fsdp'), scatter_dimension=0, tiled=True)  246 us
    reduce_scatter x2, waiting for transfers between devices, sum_terms(): lax.psum_scatter(terms[5], ('dp', 'fsdp'), scatter_dimension=0, tiled=True)  196 us
    all_gather x2, waiting for transfers between devices, gather_forward(): lax.all_gather(local[11], ('dp', 'fsdp'), axis=0, tiled=True)  109 us
    dot_general x48, matrix products, one_head(): jnp.einsum('rqd,rkd->rqk', query_block, key_block, preferred_element_type...  83.3 us
    dot_general x48, matrix products, one_head(): jnp.einsum('rqk,rqd->rkd', score_grad, query_block, preferred_element_typ...  77.8 us
    dot_general x48, matrix products, one_head(): jnp.einsum('rqk,rqd->rkd', probs_low, grad_block, preferred_element_type=...  77.5 us
  transfers between devices with their start and end apart: 17, of which 14 were waited for; matrix products, arithmetic and copies ran while one was open for 17% of the time, Pallas kernels for 0%

commit v1 on v0

v1 whole, which is shorter than its diff:
```python
import functools

import jax
import jax.numpy as jnp
from jax import lax
from jax.experimental import pallas as pl
from jax.experimental.pallas import tpu as pltpu
from jax.sharding import PartitionSpec as P

LAYERS = 2
UNIQUE = 4
F32 = jnp.float32
BF = jnp.bfloat16
AX = ("dp", "fsdp")
LANES = 128
EPS = 1e-05

NEG=-1e9
def nt(a,b): return lax.dot_general(a,b,(((1,),(1,)),((),())),preferred_element_type=F32)
def nn(a,b): return lax.dot_general(a,b,(((1,),(0,)),((),())),preferred_element_type=F32)
def halves(x):
    lane=lax.broadcasted_iota(jnp.int32,x.shape,1)
    z=jnp.zeros_like(x)
    return jnp.where(lane<64,x,z), jnp.where(lane<64,z,x)

def fwd_kernel(fl_ref,q_ref,k_ref,v_ref,o_ref,lse_ref,*,bq):
    L=q_ref.shape[0]; half=L//2
    second=fl_ref[pl.program_id(0)]<L
    shut=jnp.where(second,F32(1e9),F32(0.))
    q=q_ref[...]*BF(0.125); k=k_ref[...]; vT=v_ref[...].T
    sub=lax.broadcasted_iota(jnp.int32,vT.shape,0)
    zero=jnp.zeros_like(vT)
    vTs=(jnp.where(sub<64,vT,zero),jnp.where(sub<64,zero,vT))
    qs=halves(q)
    tri=lax.broadcasted_iota(jnp.int32,(bq,bq),0)<=lax.broadcasted_iota(jnp.int32,(bq,bq),1)
    for j in range(L//bq):
        lo=j*bq; hi=lo+bq
        acc=jnp.zeros((128,bq),F32)
        for h in range(2):
            qh=qs[h][lo:hi]
            s=nt(k[:hi],qh)
            parts=[]
            if lo>0 : parts.append((0,min(lo,half),s[:min(lo,half)]))
            if lo>half: parts.append((half,lo,s[half:lo]))
            diag=jnp.where(tri,s[lo:],NEG)
            m=jnp.max(diag,axis=0,keepdims=True)
            for a,b,t in parts:
                mt=jnp.max(t,axis=0,keepdims=True)
                if lo>=half and a==0: mt=mt-shut
                m=jnp.maximum(m,mt)
            ps=[]; l=0.
            for a,b,t in parts+[(lo,hi,diag)]:
                mm=m+shut if (lo>=half and a==0) else m
                p=jnp.exp(t-mm)
                l=l+jnp.sum(p,axis=0,keepdims=True)
                ps.append(p.astype(BF))
            p=jnp.concatenate(ps,axis=0) if len(ps)>1 else ps[0]
            oh=nn(vTs[h][:,:hi],p)
            acc=acc+oh*(1.0/l)
            lse_ref[0,h:h+1,lo:hi]=m+jnp.log(l)
        o_ref[lo:hi,:]=acc.T.astype(BF)

def attend_fwd(qkv,fl,bq=256):
    N,C=qkv.shape; R=fl.shape[0]; L=N//R; D=C//3; G=D//128
    return pl.pallas_call(functools.partial(fwd_kernel,bq=bq),
        grid_spec=pltpu.PrefetchScalarGridSpec(num_scalar_prefetch=1,grid=(R,G),
          in_specs=[pl.BlockSpec((L,128),lambda r,g,fl:(r,g)),
                    pl.BlockSpec((L,128),lambda r,g,fl:(r,G+g)),
                    pl.BlockSpec((L,128),lambda r,g,fl:(r,2*G+g))],
          out_specs=[pl.BlockSpec((L,128),lambda r,g,fl:(r,g)),
                     pl.BlockSpec((1,2,L),lambda r,g,fl:(r*G+g,0,0))]),
        out_shape=[jax.ShapeDtypeStruct((N,D),BF),jax.ShapeDtypeStruct((R*G,2,L),F32)],
        compiler_params=pltpu.CompilerParams(vmem_limit_bytes=48<<20),
        cost_estimate=pl.CostEstimate(flops=2*2*R*L*L*D*2,bytes_accessed=N*D*8,transcendentals=R*L*L*12//2),
        name="attend_fwd")(fl,qkv,qkv,qkv)

def bwd_kernel(fl_ref,q_ref,k_ref,v_ref,do_ref,lse_ref,dq_ref,dk_ref,dv_ref,dk_acc,dv_acc,*,bq):
    L=q_ref.shape[0]; half=L//2
    second=fl_ref[pl.program_id(0)]<L
    shut=jnp.where(second,F32(1e9),F32(0.))
    q=q_ref[...]*BF(0.125); k=k_ref[...]; v=v_ref[...]; do=do_ref[...]
    kT=k.T
    sub=lax.broadcasted_iota(jnp.int32,kT.shape,0); zero=jnp.zeros_like(kT)
    kTs=(jnp.where(sub<64,kT,zero),jnp.where(sub<64,zero,kT))
    qs=halves(q); dos=halves(do)
    tri=lax.broadcasted_iota(jnp.int32,(bq,bq),0)<=lax.broadcasted_iota(jnp.int32,(bq,bq),1)
    nb=L//bq
    for j in reversed(range(nb)):
        lo=j*bq; hi=lo+bq
        dqT=jnp.zeros((128,bq),F32)
        dkp=None; dvp=None
        for h in range(2):
            qh=qs[h][lo:hi]; doh=dos[h][lo:hi]
            lse=lse_ref[0,h:h+1,lo:hi]
            s=nt(k[:hi],qh)
            dp=nt(v[:hi],doh)
            ps=[];
            cuts=[]
            if lo>0: cuts.append((0,min(lo,half)))
            if lo>half: cuts.append((half,lo))
            cuts.append((lo,hi))
            for a,b in cuts:
                ll=lse+shut if (lo>=half and b<=half) else lse
                t=s[a:b]-ll
                if a==lo: t=jnp.where(tri,t,NEG)
                ps.append(jnp.exp(t))
            p=jnp.concatenate(ps,axis=0) if len(ps)>1 else ps[0]
            delta=jnp.sum(p*dp,axis=0,keepdims=True)
            ds=(p*(dp-delta)).astype(BF)
            pb=p.astype(BF)
            dv_=nn(pb,doh); dk_=nn(ds,qh)
            dvp=dv_ if dvp is None else dvp+dv_
            dkp=dk_ if dkp is None else dkp+dk_
            dqT=dqT+nn(kTs[h][:,:hi],ds)
        if j==nb-1:
            dk_acc[...]=dkp; dv_acc[...]=dvp
        else:
            dk_acc[:hi]+=dkp; dv_acc[:hi]+=dvp
        dq_ref[lo:hi,:]=(dqT.T*0.125).astype(BF)
    dk_ref[...]=dk_acc[...].astype(BF); dv_ref[...]=dv_acc[...].astype(BF)

def attend_bwd(qkv,do,lse,fl,bq=256):
    N,C=qkv.shape; R=fl.shape[0]; L=N//R; D=C//3; G=D//128
    blk=lambda off: pl.BlockSpec((L,128),lambda r,g,fl:(r,off*G+g))
    return pl.pallas_call(functools.partial(bwd_kernel,bq=bq),
        grid_spec=pltpu.PrefetchScalarGridSpec(num_scalar_prefetch=1,grid=(R,G),
          in_specs=[blk(0),blk(1),blk(2),blk(0),pl.BlockSpec((1,2,L),lambda r,g,fl:(r*G+g,0,0))],
          out_specs=[blk(0),blk(0),blk(0)],
          scratch_shapes=[pltpu.VMEM((L,128),F32),pltpu.VMEM((L,128),F32)]),
        out_shape=[jax.ShapeDtypeStruct((N,D),BF)]*3,
        compiler_params=pltpu.CompilerParams(vmem_limit_bytes=48<<20),
        cost_estimate=pl.CostEstimate(flops=5*2*R*L*L*D*2,bytes_accessed=N*D*16,transcendentals=R*L*L*12//2),
        name="attend_bwd")(fl,qkv,qkv,qkv,do,lse)


def swap(x, mask):
    count = lax.axis_size(AX)
    return lax.ppermute(x, AX, [(i, i ^ mask) for i in range(count)])


def block_mesh():
    return lax.axis_size("dp") == 4 and lax.axis_size("fsdp") == 8


CORE, ZLO, ZHI, XBIT, YBIT = 1, 2, 4, 8, 16


def place_column(own, others):
    z = lax.rem(lax.axis_index("fsdp") // 2, 4)
    parts = [own] + others
    rows = []
    for k in range(4):
        pick = parts[k]
        for j in range(1, 4):
            pick = jnp.where(z == j, parts[k ^ j], pick)
        rows.append(pick)
    return jnp.stack(rows)


def assemble_kernel(*refs, cuts):
    n = 8
    ins = refs[:n]
    outs = refs[n : n + len(cuts)]
    sem = refs[-1]
    dp = lax.axis_index("dp")
    core = lax.rem(lax.axis_index("fsdp"), 2)
    copies = []
    for index in range(n):
        rel_dp, rel_core = index % 4, index // 4
        to_dp = (dp + rel_dp) - 2 * (dp & rel_dp)
        to_core = core if rel_core == 0 else 1 - core
        for at, (start, width) in enumerate(cuts):
            src = ins[index]
            if len(cuts) > 1:
                src = src.at[:, :, pl.ds(start, width)]
            copies.append(
                pltpu.make_async_copy(src, outs[at].at[to_dp, :, to_core], sem.at[index, at])
            )
    for c in copies:
        c.start()
    for c in copies:
        c.wait()


def assemble(parts, widths):
    r = parts[0].shape[1]
    cuts = []
    start = 0
    for width in widths:
        cuts.append((start, width))
        start += width
    outs = pl.pallas_call(
        functools.partial(assemble_kernel, cuts=cuts),
        in_specs=[pl.BlockSpec(memory_space=pl.ANY)] * 8,
        out_specs=[pl.BlockSpec(memory_space=pltpu.VMEM)] * len(widths),
        out_shape=[jax.ShapeDtypeStruct((4, 4, 2, r, w), BF) for w in widths],
        scratch_shapes=[pltpu.SemaphoreType.DMA((8, len(widths)))],
        cost_estimate=pl.CostEstimate(flops=0, bytes_accessed=4 * 32 * r * start, transcendentals=0),
        name="assemble",
    )(*parts)
    return [o.reshape(32 * r, o.shape[-1]) for o in outs]


def gather_rows(shard, first, widths):
    if not block_mesh():
        whole = lax.all_gather(shard, AX, axis=0, tiled=True)
        out = []
        start = 0
        for width in widths:
            out.append(whole[:, start : start + width])
            start += width
        return out
    second = XBIT + YBIT - first
    column = place_column(shard, [swap(shard, 2 * j) for j in range(1, 4)])
    near = swap(column, first)
    far = [swap(column, second), swap(near, second)]
    if first == XBIT:
        mine = [column, near, far[0], far[1]]
    else:
        mine = [column, far[0], near, far[1]]
    theirs = [swap(part, CORE) for part in mine]
    return assemble(mine + theirs, widths)


def scatter_rows(term, first):
    rows = term.shape[0]
    count = lax.axis_size(AX)
    r = rows // count
    if not block_mesh():
        return lax.psum_scatter(term.astype(F32), AX, scatter_dimension=0, tiled=True)
    width = term.shape[1]
    f = lax.axis_index("fsdp")
    d = lax.axis_index("dp")
    core, z = lax.rem(f, 2), f // 2
    xbit, ybit = lax.rem(d, 2), d // 2

    def fold(value, axis, bit, mask):
        kept = lax.dynamic_index_in_dim(value, bit, axis, keepdims=False)
        sent = lax.dynamic_index_in_dim(value, 1 - bit, axis, keepdims=False)
        return (kept.astype(F32) + swap(sent, mask).astype(F32)).astype(BF)

    value = term.reshape(2, 2, 4, 2, r, width)
    value = fold(value, 3, core, CORE)
    if first == XBIT:
        value = fold(value, 0, ybit, YBIT)
        value = fold(value, 0, xbit, XBIT)
    else:
        value = fold(value, 1, xbit, XBIT)
        value = fold(value, 0, ybit, YBIT)
    total = lax.dynamic_index_in_dim(value, z, 0, keepdims=False).astype(F32)
    for j in range(1, 4):
        other = lax.dynamic_index_in_dim(value, z ^ j, 0, keepdims=False)
        total = total + swap(other, 2 * j).astype(F32)
    return total


def layer_norm(values, gain, shift):
    centre = values - jnp.mean(values, axis=-1, keepdims=True)
    spread = jnp.mean(centre * centre, axis=-1, keepdims=True)
    return centre * lax.rsqrt(spread + EPS) * gain + shift


def inner_rows(left, right):
    return lax.dot_general(left, right, (((0,), (0,)), ((), ())), preferred_element_type=F32)


def times_transposed(left, right):
    return lax.dot_general(left, right, (((1,), (1,)), ((), ())), preferred_element_type=F32)


def column_sums(values):
    return jnp.sum(values.astype(F32), axis=0)


def gelu_pair(z):
    c = 0.7978845608028654
    t = jnp.tanh(c * (z + 0.044715 * z * z * z))
    value = 0.5 * z * (1.0 + t)
    slope = 0.5 * (1.0 + t) + 0.5 * z * (1.0 - t * t) * c * (1.0 + 3 * 0.044715 * z * z)
    return value.astype(BF), slope.astype(BF)


def pack_columns(vectors, wide, count):
    length = vectors[0].shape[0]
    ways = wide.shape[0] // length
    per = length // count
    spread = wide.reshape(count, ways, per).transpose(0, 2, 1).reshape(length, ways)
    block = jnp.concatenate([jnp.stack(vectors, axis=1), spread], axis=1)
    return jnp.pad(block, ((0, 0), (0, LANES - block.shape[1])))


def unpack_columns(block, vector_count, ways, count):
    length = block.shape[0]
    turned = block[:, : vector_count + ways].T
    wide = turned[vector_count:].reshape(ways, count, length // count).transpose(1, 0, 2).reshape(-1)
    return [turned[i] for i in range(vector_count)], wide


def gather_use(local, layer):
    (ga, sa, hw, qb, vb, mw, mb, gf, sf, ew, eb, sw, sb) = local
    small = pack_columns([ga, sa, qb, vb, mb, gf, sf, sb], eb, 1)
    width = hw.shape[1]
    if layer == 0:
        half = width // 2
        wa, sm = gather_rows(jnp.concatenate([hw[:, :half], small], axis=1), XBIT, [half, LANES])
        (wb,) = gather_rows(hw[:, half:], YBIT, [width - half])
        heads = jnp.concatenate([wa, wb], axis=1)
    else:
        heads, sm = gather_rows(jnp.concatenate([hw, small], axis=1), XBIT, [width, LANES])
    (mix,) = gather_rows(mw, YBIT, [mw.shape[1]])
    (expand,) = gather_rows(ew, XBIT, [ew.shape[1]])
    (shrink,) = gather_rows(sw, YBIT, [sw.shape[1]])
    vecs, wide = unpack_columns(sm, 8, eb.shape[0] // ga.shape[0], lax.axis_size(AX))
    vecs = [v.astype(F32) for v in vecs]
    return dict(zip(("ga", "sa", "qb", "vb", "mb", "gf", "sf", "sb"), vecs), eb=wide.astype(F32),
                heads=heads, mix=mix, expand=expand, shrink=shrink)


def forward_use(hidden, w, first_len):
    normed = layer_norm(hidden, w["ga"], w["sa"]).astype(BF)
    bias = jnp.concatenate([w["qb"], jnp.zeros_like(w["qb"]), w["vb"]])
    qkv = (jnp.dot(normed, w["heads"], preferred_element_type=F32) + bias).astype(BF)
    attended, lse = attend_fwd(qkv, first_len)
    middle = hidden + jnp.dot(attended, w["mix"], preferred_element_type=F32) + w["mb"]
    normed_two = layer_norm(middle, w["gf"], w["sf"]).astype(BF)
    expanded = jnp.dot(normed_two, w["expand"], preferred_element_type=F32) + w["eb"]
    activated, slope = gelu_pair(expanded)
    result = middle + jnp.dot(activated, w["shrink"], preferred_element_type=F32) + w["sb"]
    return result, (hidden, normed, qkv, attended, lse, middle, normed_two, activated, slope)


def backward_use(grad_out, kept, w, first_len):
    hidden, normed, qkv, attended, lse, middle, normed_two, activated, slope = kept
    width = hidden.shape[1]
    count = lax.axis_size(AX)
    grad_low = grad_out.astype(BF)
    shrink_term = inner_rows(activated, grad_low).astype(BF)
    shrink_share = scatter_rows(shrink_term, YBIT)
    sb = column_sums(grad_low)
    dz = (times_transposed(grad_low, w["shrink"]) * slope.astype(F32)).astype(BF)
    expand_share = scatter_rows(inner_rows(normed_two, dz).astype(BF), XBIT)
    eb = column_sums(dz)
    dc = times_transposed(dz, w["expand"])
    unused, norm_back = jax.vjp(layer_norm, middle, w["gf"], w["sf"])
    middle_norm, gf, sf = norm_back(dc)
    dm = grad_out + middle_norm
    dmb = dm.astype(BF)
    mix_share = scatter_rows(inner_rows(attended, dmb).astype(BF), YBIT)
    mb = column_sums(dmb)
    do = times_transposed(dmb, w["mix"]).astype(BF)
    dq, dk, dv = attend_bwd(qkv, do, lse, first_len)
    dqkv = jnp.concatenate([dq, dk, dv], axis=1)
    heads_term = inner_rows(normed, dqkv).astype(BF)
    qb = column_sums(dq)
    vb = column_sums(dv)
    da = times_transposed(dqkv, w["heads"])
    unused, first_back = jax.vjp(layer_norm, hidden, w["ga"], w["sa"])
    hidden_norm, ga, sa = first_back(da)
    small = pack_columns([ga, sa, qb, vb, mb, gf, sf, sb], eb, count).astype(BF)
    heads_share = scatter_rows(jnp.concatenate([heads_term, small], axis=1), XBIT)
    vecs, wide = unpack_columns(heads_share[:, 3 * width :], 8, eb.shape[0] // width, 1)
    ga, sa, qb, vb, mb, gf, sf, sb = vecs
    return dm + hidden_norm, (
        ga, sa, heads_share[:, : 3 * width], qb, vb, mix_share, mb, gf, sf, expand_share, wide,
        shrink_share, sb,
    )


def pick_shards(stacks, source):
    return tuple(lax.dynamic_index_in_dim(stack, source, 0, keepdims=False) for stack in stacks)


def place_terms(sources, shares):
    ids = lax.iota(jnp.int32, UNIQUE)
    out = []
    for items in zip(*shares):
        total = 0.0
        for source, item in zip(sources, items):
            chosen = (ids == source).reshape((UNIQUE,) + (1,) * item.ndim)
            total = total + jnp.where(chosen, item[None], 0.0)
        out.append(total)
    return out


def body(tokens, cotangent, tie_map, first_length, *stacks):
    hidden = tokens.astype(F32)
    sources = [tie_map[i] for i in range(LAYERS)]
    weights = [gather_use(pick_shards(stacks, s), i) for i, s in enumerate(sources)]
    kept = []
    for i in range(LAYERS):
        hidden, saved = forward_use(hidden, weights[i], first_length)
        kept.append(saved)
    grad = cotangent.astype(F32)
    shares = [None] * LAYERS
    for i in reversed(range(LAYERS)):
        grad, shares[i] = backward_use(grad, kept[i], weights[i], first_length)
    return (hidden.astype(BF), grad.astype(BF), *place_terms(sources, shares))


def solution(mesh):
    rows = P(AX, None)
    flat = P(None, AX)
    deep = P(None, AX, None)
    weights = (flat, flat, deep, flat, flat, deep, flat, flat, flat, deep, flat, deep, flat)
    return jax.shard_map(
        body,
        mesh=mesh,
        in_specs=(rows, rows, P(), P(AX)) + weights,
        out_specs=(rows, rows) + weights,
        check_vma=False,
    )
```

time: 2270 us -> 833 us (0.37)
  waiting for transfers between devices: 1220 us -> 176 us
  matrix products: 648 us -> 181 us
  starting transfers between devices: 1.48 us -> 147 us
  Pallas kernels: 0 us -> 139 us
  other arithmetic: 175 us -> 71.1 us
  blocking collectives: 44.5 us -> 0 us
  loops' own time: 34.8 us -> 0 us
    reduce_scatter x8 -> x0, waiting for transfers between devices: 1000 us -> none  [the longest x2 280 us: sum_terms(): lax.psum_scatter(terms[11], ('dp', 'fsdp'), scatter_dimension=0, tiled=True)]
    dot_general x344 -> x8, matrix products: 496 us -> 60.1 us  [the longest x2 21.3 us: forward_use(): jnp.dot(activated, w['shrink'], preferred_element_type=F32)]
    ppermute x0 -> x138, waiting for transfers between devices: none -> 176 us  [swap(): return lax.ppermute(x, AX, [(i, i ^ mask) for i in range(count)])]
    all_gather x8 -> x0, waiting for transfers between devices: 170 us -> none  [the longest x2 109 us: gather_forward(): lax.all_gather(local[11], ('dp', 'fsdp'), axis=0, tiled=True)]
    ppermute x0 -> x138, starting transfers between devices: none -> 147 us  [swap(): return lax.ppermute(x, AX, [(i, i ^ mask) for i in range(count)])]
    pallas_call x0 -> x13, Pallas kernels: none -> 139 us  [the longest x2 54.9 us: attend_bwd(): pl.pallas_call(functools.partial(bwd_kernel, bq=bq), grid_spec=pltpu.Pref...]
    ge x96 -> x0, other arithmetic: 62.6 us -> none  [the longest x48 31.3 us: block_mask(): query_part = query_place[None, :] >= first_len[:, None]]
    unnamed x18 -> x0, waiting for transfers between devices: 47.4 us -> none
  transfers between devices with their start and end apart: 17 -> 138, of which waited for: 14 -> 42; matrix products, arithmetic and copies ran while one was open for 17% -> 22% of each run, Pallas kernels for 0% -> 10%
where the time goes in v1:
time: 833 us; the launch traced here: 829 us
  matrix products  181 us (22%)
  waiting for transfers between devices  176 us (21%)
  starting transfers between devices  147 us (18%)
  Pallas kernels  139 us (17%)
  local copies, waits for them, and re-layouts  107 us (13%)
  other arithmetic  71.1 us (9%)
    ppermute x138, waiting for transfers between devices, swap(): return lax.ppermute(x, AX, [(i, i ^ mask) for i in range(count)])  176 us
    ppermute x138, starting transfers between devices, swap(): return lax.ppermute(x, AX, [(i, i ^ mask) for i in range(count)])  147 us
    dot_general x8, matrix products, times_transposed(): lax.dot_general(left, right, (((1,), (1,)), ((), ())), preferred_element_...  66.9 us
    pallas_call x2, Pallas kernels, attend_bwd(): pl.pallas_call(functools.partial(bwd_kernel, bq=bq), grid_spec=pltpu.Pref...  54.9 us
    dot_general x8, matrix products, inner_rows(): lax.dot_general(left, right, (((0,), (0,)), ((), ())), preferred_element_...  53.5 us
    pallas_call x2, Pallas kernels, attend_fwd(): pl.pallas_call(functools.partial(fwd_kernel, bq=bq), grid_spec=pltpu.Pref...  51.2 us
    pallas_call x9, Pallas kernels, assemble(): pl.pallas_call(functools.partial(assemble_kernel, cuts=cuts), in_specs=[p...  32.9 us
    unnamed x296, local copies, waits for them, and re-layouts  28.6 us
  transfers between devices with their start and end apart: 138, of which 42 were waited for; matrix products, arithmetic and copies ran while one was open for 22% of the time, Pallas kernels for 10%

profile of v1, /device:TPU:0, one launch (start us, length us, event | category | flops | bytes accessed | tf_op | source)
XLA Modules:
  0.0 828.5 jit_solution(3952216014142649560)
XLA Ops:
  81.7 7.7 collective-permute-done.1
  94.0 6.0 collective-permute-start.81
  100.0 5.9 collective-permute-done.31
  105.9 8.4 %collective-permute-start.41 = (bf16[96,768]{1,0:T(8,128)(2,1)S(1)}, bf16[96,768]{1,0:T(8,128)(2,1)S(1)}, u32[]{:S(2)}, u32[]{:S(2)}) collective-permute-start(bf16[96,768]{1,0:T(8,128)(2,1)S(1)} %get-tuple-element.201), channel_id=1, source_target_pairs={{0,4},{1,5},{2,6},{3,7},{4,0},{5,1},{6,2},{7,3},{8,12},{9,13},{10,... | collective-permute-start | bytes 442376 | tf_op jit(solution)/shard_map/ppermute | solution.py:138
  115.9 6.4 collective-permute-done.81
  201.4 8.1 add_convert_fusion.1.q_ref.k_ref.v_ref
  209.5 25.6 %attend_fwd.2 = (bf16[1024,768]{1,0:T(8,128)(2,1)S(1)}, f32[6,2,1024]{2,1,0:T(2,128)S(1)}) custom-call(s32[1]{0:T(128)S(6)} %copy.286.fl_ref, bf16[1024,2304]{1,0:T(8,128)(2,1)} %add_convert_fusion.1.q_ref.k_ref.v_ref, bf16[1024,2304]{1,0:T(8,128)(2,1)} %add_convert_fusion.1.q_ref.k_ref.v_ref, bf16[1024,2304]{1,0:T(8,128)(2,1)} %add_convert_fusion.1.q_ref.k_ref.v_ref), custom_call_target="tpu_custom_call" | custom-call | flops 6442450944 | bytes 6291456 | tf_op jit(solution)/shard_map/attend_fwd/pallas_call | solution.py:65
  240.8 13.9 %collective-permute-done.45.refs_3_ = bf16[4,96,768]{2,1,0:T(8,128)(2,1)S(1)} collective-permute-done((bf16[4,96,768]{2,1,0:T(8,128)(2,1)}, bf16[4,96,768]{2,1,0:T(8,128)(2,1)S(1)}, u32[]{:S(2)}, u32[]{:S(2)}) %collective-permute-start.45) | collective-permute-done | bytes 589856 | tf_op jit(solution)/shard_map/ppermute | solution.py:138
  261.3 11.2 %fusion.124 = f32[1024,3072]{1,0:T(8,128)} fusion(bf16[768,3072]{1,0:T(8,128)(2,1)} %bitcast.395, f32[1024,768]{0,1:T(8,128)} %copy-done.4, f32[768]{0:T(1024)S(1)} %get-tuple-element.136, f32[768]{0:T(1024)S(1)} %get-tuple-element.134, f32[1024]{0:T(1024)S(1)} %fusion.80, f32[1024]{0:T(1024)S(1)} %broadcast_multiply_fusion.2), kind=kOutput, calls=%fused_computation.399 | convolution fusion | flops 4835770368 | bytes 20461568 | tf_op jit(solution)/shard_map/dot_general | solution.py:326
  281.7 11.8 %fusion.138 = (f32[1024]{0:T(1024)S(1)}, f32[1024,768]{0,1:T(8,128)S(1)}) fusion(f32[768]{0:T(1024)S(1)} %get-tuple-element.135, f32[1024,768]{0,1:T(8,128)} %copy-done.4, bf16[3072,768]{1,0:T(8,128)(2,1)} %bitcast.421, f32[1024,3072]{1,0:T(8,128)} %fusion.124, f32[3072]{0:T(1024)S(1)} %reshape.443), kind=kOutput, calls=%fused_computation.411 | convolution fusion | flops 4865653760 | bytes 23612416 | tf_op jit(solution)/shard_map/dot_general | solution.py:328
  299.9 25.6 %attend_fwd.3 = (bf16[1024,768]{1,0:T(8,128)(2,1)S(1)}, f32[6,2,1024]{2,1,0:T(2,128)S(1)}) custom-call(s32[1]{0:T(128)S(6)} %copy.286.fl_ref, bf16[1024,2304]{1,0:T(8,128)(2,1)} %add_convert_fusion.q_ref.k_ref.v_ref, bf16[1024,2304]{1,0:T(8,128)(2,1)} %add_convert_fusion.q_ref.k_ref.v_ref, bf16[1024,2304]{1,0:T(8,128)(2,1)} %add_convert_fusion.q_ref.k_ref.v_ref), custom_call_target="tpu_custom_call" | custom-call | flops 6442450944 | bytes 6291456 | tf_op jit(solution)/shard_map/attend_fwd/pallas_call | solution.py:65
  329.2 14.0 %collective-permute-done.85.refs_3_ = bf16[4,96,768]{2,1,0:T(8,128)(2,1)} collective-permute-done((bf16[4,96,768]{2,1,0:T(8,128)(2,1)}, bf16[4,96,768]{2,1,0:T(8,128)(2,1)}, u32[]{:S(2)}, u32[]{:S(2)}) %collective-permute-start.85) | collective-permute-done | bytes 589856 | tf_op jit(solution)/shard_map/ppermute | solution.py:138
  348.5 8.8 %fusion.125 = f32[1024,3072]{1,0:T(8,128)S(1)} fusion(bf16[768,3072]{1,0:T(8,128)(2,1)} %bitcast.399, f32[1024,768]{0,1:T(8,128)} %copy-done.7, f32[768]{0:T(1024)S(1)} %get-tuple-element.128, f32[768]{0:T(1024)S(1)} %get-tuple-element.126, f32[1024]{0:T(1024)S(1)} %fusion.82, f32[1024]{0:T(1024)S(1)} %broadcast_multiply_fusion), kind=kOutput, calls=%fused_computation.400 | convolution fusion | flops 4835770368 | bytes 20461568 | tf_op jit(solution)/shard_map/dot_general | solution.py:326
  357.3 9.5 %convolution_convert_fusion = bf16[3072,768]{1,0:T(8,128)(2,1)} fusion(bf16[1024,768]{1,0:T(8,128)(2,1)S(1)} %copy-done.38, f32[1024,3072]{1,0:T(8,128)S(1)} %fusion.125, f32[3072]{0:T(1024)S(1)} %reshape.452), kind=kOutput, calls=%fused_computation.26 | convolution fusion | flops 4865654784 | bytes 18886656 | tf_op jit(solution)/shard_map/dot_general | solution.py:264
  372.1 17.0 %fusion.142 = (bf16[3072]{0:T(1024)(128)(2,1)}, bf16[1024,3072]{1,0:T(8,128)(2,1)S(1)}) fusion(f32[1024,3072]{1,0:T(8,128)} %copy-done.31, f32[3072]{0:T(1024)S(1)} %reshape.452, bf16[3072,768]{1,0:T(8,128)(2,1)} %bitcast.425, bf16[1024,768]{1,0:T(8,128)(2,1)} %param.18), kind=kOutput, calls=%fused_computation.415 | convolution fusion | flops 4904186880 | bytes 25184256 | tf_op jit(solution)/shard_map/dot_general | solution.py:268
  389.1 9.8 %fusion.141 = (bf16[768]{0:T(1024)(128)(2,1)}, f32[1024,768]{1,0:T(8,128)}) fusion(bf16[1024,3072]{1,0:T(8,128)(2,1)S(1)} %get-tuple-element.286, bf16[768,3072]{1,0:T(8,128)(2,1)} %bitcast.400), kind=kOutput, calls=%fused_computation.414 | convolution fusion | flops 4832623616 | bytes 14157312 | tf_op jit(solution)/shard_map/dot_general | solution.py:268
  398.9 7.1 convolution_convert_fusion.2
  422.1 27.4 %attend_bwd.2 = (bf16[1024,768]{1,0:T(8,128)(2,1)S(1)}, bf16[1024,768]{1,0:T(8,128)(2,1)S(1)}, bf16[1024,768]{1,0:T(8,128)(2,1)S(1)}) custom-call(s32[1]{0:T(128)S(6)} %copy.286.fl_ref, bf16[1024,2304]{1,0:T(8,128)(2,1)} %add_convert_fusion.q_ref.k_ref.v_ref, bf16[1024,2304]{1,0:T(8,128)(2,1)} %add_convert_fusion.q_ref.k_ref.v_ref, ...), custom_call_target="tpu_custom_call" | custom-call | flops 16106127360 | bytes 12582912 | tf_op jit(solution)/shard_map/attend_bwd/pallas_call | solution.py:125
  475.6 16.9 %fusion.145 = (bf16[3072]{0:T(1024)(128)(2,1)S(1)}, bf16[1024,3072]{1,0:T(8,128)(2,1)}) fusion(f32[1024,3072]{1,0:T(8,128)} %fusion.124, f32[3072]{0:T(1024)S(1)} %reshape.443, bf16[3072,768]{1,0:T(8,128)(2,1)S(1)} %bitcast.424, f32[1024,768]{0,1:T(8,128)S(1)} %get-tuple-element.161), kind=kOutput, calls=%fused_computation.418 | convolution fusion | flops 4904973312 | bytes 26757120 | tf_op jit(solution)/shard_map/dot_general | solution.py:268
  492.5 13.4 %convolution_convert_fusion.1 = bf16[3072,768]{1,0:T(8,128)(2,1)} fusion(f32[1024,768]{0,1:T(8,128)S(1)} %get-tuple-element.161, f32[1024,3072]{1,0:T(8,128)} %fusion.124, f32[3072]{0:T(1024)S(1)} %reshape.443), kind=kOutput, calls=%fused_computation.27 | convolution fusion | flops 4866441216 | bytes 20459520 | tf_op jit(solution)/shard_map/dot_general | solution.py:264
  506.1 6.9 fusion.144
  512.9 7.1 convolution_convert_fusion.3
  537.0 27.4 %attend_bwd.3 = (bf16[1024,768]{1,0:T(8,128)(2,1)S(1)}, bf16[1024,768]{1,0:T(8,128)(2,1)S(1)}, bf16[1024,768]{1,0:T(8,128)(2,1)S(1)}) custom-call(s32[1]{0:T(128)S(6)} %copy.286.fl_ref, bf16[1024,2304]{1,0:T(8,128)(2,1)} %add_convert_fusion.1.q_ref.k_ref.v_ref, bf16[1024,2304]{1,0:T(8,128)(2,1)} %add_convert_fusion.1.q_ref.k_ref.v_ref, ...), custom_call_target="tpu_custom_call" | custom-call | flops 16106127360 | bytes 12582912 | tf_op jit(solution)/shard_map/attend_bwd/pallas_call | solution.py:125
  578.3 9.5 %add_convert_fusion.3 = bf16[1024,768]{0,1:T(8,128)(2,1)S(1)} fusion(f32[1024,768]{0,1:T(8,128)S(1)} %copy-done.10, bf16[3072,768]{1,0:T(8,128)(2,1)S(1)} %bitcast.428, f32[768]{0:T(1024)S(1)} %copy-done.124, f32[1024,3072]{1,0:T(8,128)} %copy-done.31, f32[3072]{0:T(1024)S(1)} %copy-done.117), kind=kOutput, calls=%fused_computation.76 | convolution fusion | flops 4865654784 | bytes 22035456 | tf_op jit(solution)/shard_map/dot_general | solution.py:328
  633.3 6.2 collective-permute-done.109
  678.9 11.4 %collective-permute-done.97 = bf16[2,4,24,2432]{3,2,1,0:T(8,128)(2,1)} collective-permute-done((bf16[2,4,24,2432]{3,2,1,0:T(8,128)(2,1)}, bf16[2,4,24,2432]{3,2,1,0:T(8,128)(2,1)}, u32[]{:S(2)}, u32[]{:S(2)}) %collective-permute-start.97) | collective-permute-done | bytes 933920 | tf_op jit(solution)/shard_map/ppermute | solution.py:138
  692.7 17.6 %collective-permute-done.91 = bf16[2,4,24,2432]{3,2,1,0:T(8,128)(2,1)} collective-permute-done((bf16[2,4,24,2432]{3,2,1,0:T(8,128)(2,1)}, bf16[2,4,24,2432]{3,2,1,0:T(8,128)(2,1)}, u32[]{:S(2)}, u32[]{:S(2)}) %collective-permute-start.91) | collective-permute-done | bytes 933920 | tf_op jit(solution)/shard_map/ppermute | solution.py:138
  715.8 6.6 collective-permute-done.92
  727.0 6.9 collective-permute-done.100
  768.4 9.3 %collective-permute-done.134 = bf16[4,96,768]{2,1,0:T(8,128)(2,1)S(1)} collective-permute-done((bf16[4,96,768]{2,1,0:T(8,128)(2,1)S(1)}, bf16[4,96,768]{2,1,0:T(8,128)(2,1)S(1)}, u32[]{:S(2)}, u32[]{:S(2)}) %collective-permute-start.134) | collective-permute-done | bytes 589856 | tf_op jit(solution)/shard_map/ppermute | solution.py:138
  793.9 8.3 %collective-permute-start.129 = (bf16[96,768]{1,0:T(8,128)(2,1)S(1)}, bf16[96,768]{1,0:T(8,128)(2,1)S(1)}, u32[]{:S(2)}, u32[]{:S(2)}) collective-permute-start(bf16[96,768]{1,0:T(8,128)(2,1)S(1)} %get-tuple-element.178), channel_id=1, source_target_pairs={{0,2},{1,3},{2,0},{3,1},{4,6},{5,7},{6,4},{7,5},{8,10},{9,11},{10,... | collective-permute-start | bytes 442376 | tf_op jit(solution)/shard_map/ppermute | solution.py:138
  816.9 7.0 collective-permute-done.130
  (802 shorter events, 441.9 us)
Async XLA Ops:
  7.3 48.4 %collective-permute-start.62 = (bf16[24,768]{1,0:T(8,128)(2,1)}, bf16[24,768]{1,0:T(8,128)(2,1)}, u32[]{:S(2)}, u32[]{:S(2)}) collective-permute-start(bf16[24,768]{1,0:T(8,128)(2,1)} %get-tuple-element.240), channel_id=1, source_target_pairs={{0,2},{1,3},{2,0},{3,1},{4,6},{5,7},{6,4},{7,5},{8,10},{9,11},{10,... | collective-permute-start | bytes 110600 | tf_op jit(solution)/shard_map/ppermute | solution.py:138
  10.3 45.4 %collective-permute-start.61 = (bf16[24,768]{1,0:T(8,128)(2,1)}, bf16[24,768]{1,0:T(8,128)(2,1)}, u32[]{:S(2)}, u32[]{:S(2)}) collective-permute-start(bf16[24,768]{1,0:T(8,128)(2,1)} %get-tuple-element.240), channel_id=1, source_target_pairs={{0,4},{1,5},{2,6},{3,7},{4,0},{5,1},{6,2},{7,3},{8,12},{9,13},{10,... | collective-permute-start | bytes 110600 | tf_op jit(solution)/shard_map/ppermute | solution.py:138
  12.9 43.4 %collective-permute-start.60 = (bf16[24,768]{1,0:T(8,128)(2,1)}, bf16[24,768]{1,0:T(8,128)(2,1)}, u32[]{:S(2)}, u32[]{:S(2)}) collective-permute-start(bf16[24,768]{1,0:T(8,128)(2,1)} %get-tuple-element.240), channel_id=1, source_target_pairs={{0,6},{1,7},{2,4},{3,5},{4,2},{5,3},{6,0},{7,1},{8,14},{9,15},{10,... | collective-permute-start | bytes 110600 | tf_op jit(solution)/shard_map/ppermute | solution.py:138
  12.9 48.1 %collective-permute-start.22 = (bf16[24,768]{1,0:T(8,128)(2,1)S(1)}, bf16[24,768]{1,0:T(8,128)(2,1)}, u32[]{:S(2)}, u32[]{:S(2)}) collective-permute-start(bf16[24,768]{1,0:T(8,128)(2,1)S(1)} %get-tuple-element.241), channel_id=1, source_target_pairs={{0,2},{1,3},{2,0},{3,1},{4,6},{5,7},{6,4},{7,5},{8,10},{9,11},{10,... | collective-permute-start | bytes 110600 | tf_op jit(solution)/shard_map/ppermute | solution.py:138
  13.8 47.3 %collective-permute-start.21 = (bf16[24,768]{1,0:T(8,128)(2,1)S(1)}, bf16[24,768]{1,0:T(8,128)(2,1)}, u32[]{:S(2)}, u32[]{:S(2)}) collective-permute-start(bf16[24,768]{1,0:T(8,128)(2,1)S(1)} %get-tuple-element.241), channel_id=1, source_target_pairs={{0,4},{1,5},{2,6},{3,7},{4,0},{5,1},{6,2},{7,3},{8,12},{9,13},{10,... | collective-permute-start | bytes 110600 | tf_op jit(solution)/shard_map/ppermute | solution.py:138
  66.5 25.9 %collective-permute-start.72 = (bf16[24,3072]{1,0:T(8,128)(2,1)}, bf16[24,3072]{1,0:T(8,128)(2,1)S(1)}, u32[]{:S(2)}, u32[]{:S(2)}) collective-permute-start(bf16[24,3072]{1,0:T(8,128)(2,1)} %get-tuple-element.194), channel_id=1, source_target_pairs={{0,2},{1,3},{2,0},{3,1},{4,6},{5,7},{6,4},{7,5},{8,10},{9,11},{10,... | collective-permute-start | bytes 442376 | tf_op jit(solution)/shard_map/ppermute | solution.py:138
  67.1 26.8 %collective-permute-start.71 = (bf16[24,3072]{1,0:T(8,128)(2,1)}, bf16[24,3072]{1,0:T(8,128)(2,1)S(1)}, u32[]{:S(2)}, u32[]{:S(2)}) collective-permute-start(bf16[24,3072]{1,0:T(8,128)(2,1)} %get-tuple-element.194), channel_id=1, source_target_pairs={{0,4},{1,5},{2,6},{3,7},{4,0},{5,1},{6,2},{7,3},{8,12},{9,13},{10,... | collective-permute-start | bytes 442376 | tf_op jit(solution)/shard_map/ppermute | solution.py:138
  94.0 28.3 %collective-permute-start.81 = (bf16[96,768]{1,0:T(8,128)(2,1)S(1)}, bf16[96,768]{1,0:T(8,128)(2,1)S(1)}, u32[]{:S(2)}, u32[]{:S(2)}) collective-permute-start(bf16[96,768]{1,0:T(8,128)(2,1)S(1)} %copy-done.63), channel_id=1, source_target_pairs={{0,4},{1,5},{2,6},{3,7},{4,0},{5,1},{6,2},{7,3},{8,12},{9,13},{10,... | collective-permute-start | bytes 442376 | tf_op jit(solution)/shard_map/ppermute | solution.py:138
  190.8 47.8 %collective-permute-start.44 = (bf16[4,96,768]{2,1,0:T(8,128)(2,1)}, bf16[4,96,768]{2,1,0:T(8,128)(2,1)}, u32[]{:S(2)}, u32[]{:S(2)}) collective-permute-start(bf16[4,96,768]{2,1,0:T(8,128)(2,1)} %pad_maximum_fusion.4.refs_0_), channel_id=1, source_target_pairs={{0,16},{1,17},{2,18},{3,19},{4,20},{5,21},{6,22},{7,23},{8,24},{9,... | collective-permute-start | bytes 1769480 | tf_op jit(solution)/shard_map/ppermute | solution.py:138
  192.0 46.7 %collective-permute-start.43 = (bf16[4,96,768]{2,1,0:T(8,128)(2,1)}, bf16[4,96,768]{2,1,0:T(8,128)(2,1)}, u32[]{:S(2)}, u32[]{:S(2)}) collective-permute-start(bf16[4,96,768]{2,1,0:T(8,128)(2,1)} %pad_maximum_fusion.4.refs_0_), channel_id=1, source_target_pairs={{0,8},{1,9},{2,10},{3,11},{4,12},{5,13},{6,14},{7,15},{8,0},{9,1},... | collective-permute-start | bytes 1769480 | tf_op jit(solution)/shard_map/ppermute | solution.py:138
  193.5 47.2 %collective-permute-start.36 = (bf16[4,24,3072]{2,1,0:T(8,128)(2,1)}, bf16[4,24,3072]{2,1,0:T(8,128)(2,1)}, u32[]{:S(2)}, u32[]{:S(2)}) collective-permute-start(bf16[4,24,3072]{2,1,0:T(8,128)(2,1)} %pad_maximum_fusion.3.refs_0_), channel_id=1, source_target_pairs={{0,1},{1,0},{2,3},{3,2},{4,5},{5,4},{6,7},{7,6},{8,9},{9,8},{10,11... | collective-permute-start | bytes 1769480 | tf_op jit(solution)/shard_map/ppermute | solution.py:138
  193.5 45.8 %collective-permute-start.34 = (bf16[4,24,3072]{2,1,0:T(8,128)(2,1)}, bf16[4,24,3072]{2,1,0:T(8,128)(2,1)}, u32[]{:S(2)}, u32[]{:S(2)}) collective-permute-start(bf16[4,24,3072]{2,1,0:T(8,128)(2,1)} %pad_maximum_fusion.3.refs_0_), channel_id=1, source_target_pairs={{0,16},{1,17},{2,18},{3,19},{4,20},{5,21},{6,22},{7,23},{8,24},{9,... | collective-permute-start | bytes 1769480 | tf_op jit(solution)/shard_map/ppermute | solution.py:138
  194.5 44.9 %collective-permute-start.35 = (bf16[4,24,3072]{2,1,0:T(8,128)(2,1)}, bf16[4,24,3072]{2,1,0:T(8,128)(2,1)}, u32[]{:S(2)}, u32[]{:S(2)}) collective-permute-start(bf16[4,24,3072]{2,1,0:T(8,128)(2,1)} %collective-permute-done.33.refs_1_), channel_id=1, source_target_pairs={{0,16},{1,17},{2,18},{3,19},{4,20},{5,21},{6,22},{7,23},{8,24},{9,... | collective-permute-start | bytes 1769480 | tf_op jit(solution)/shard_map/ppermute | solution.py:138
  240.7 31.9 %collective-permute-start.46 = (bf16[4,96,768]{2,1,0:T(8,128)(2,1)}, bf16[4,96,768]{2,1,0:T(8,128)(2,1)S(1)}, u32[]{:S(2)}, u32[]{:S(2)}) collective-permute-start(bf16[4,96,768]{2,1,0:T(8,128)(2,1)} %pad_maximum_fusion.4.refs_0_), channel_id=1, source_target_pairs={{0,1},{1,0},{2,3},{3,2},{4,5},{5,4},{6,7},{7,6},{8,9},{9,8},{10,11... | collective-permute-start | bytes 1769480 | tf_op jit(solution)/shard_map/ppermute | solution.py:138
  272.6 54.5 %collective-permute-start.84 = (bf16[4,96,768]{2,1,0:T(8,128)(2,1)S(1)}, bf16[4,96,768]{2,1,0:T(8,128)(2,1)}, u32[]{:S(2)}, u32[]{:S(2)}) collective-permute-start(bf16[4,96,768]{2,1,0:T(8,128)(2,1)S(1)} %copy-done.40), channel_id=1, source_target_pairs={{0,16},{1,17},{2,18},{3,19},{4,20},{5,21},{6,22},{7,23},{8,24},{9,... | collective-permute-start | bytes 1769480 | tf_op jit(solution)/shard_map/ppermute | solution.py:138
  273.6 53.6 %collective-permute-start.83 = (bf16[4,96,768]{2,1,0:T(8,128)(2,1)S(1)}, bf16[4,96,768]{2,1,0:T(8,128)(2,1)}, u32[]{:S(2)}, u32[]{:S(2)}) collective-permute-start(bf16[4,96,768]{2,1,0:T(8,128)(2,1)S(1)} %copy-done.40), channel_id=1, source_target_pairs={{0,8},{1,9},{2,10},{3,11},{4,12},{5,13},{6,14},{7,15},{8,0},{9,1},... | collective-permute-start | bytes 1769480 | tf_op jit(solution)/shard_map/ppermute | solution.py:138
  275.1 54.1 %collective-permute-start.76 = (bf16[4,24,3072]{2,1,0:T(8,128)(2,1)S(1)}, bf16[4,24,3072]{2,1,0:T(8,128)(2,1)}, u32[]{:S(2)}, u32[]{:S(2)}) collective-permute-start(bf16[4,24,3072]{2,1,0:T(8,128)(2,1)S(1)} %copy-done.39), channel_id=1, source_target_pairs={{0,1},{1,0},{2,3},{3,2},{4,5},{5,4},{6,7},{7,6},{8,9},{9,8},{10,11... | collective-permute-start | bytes 1769480 | tf_op jit(solution)/shard_map/ppermute | solution.py:138
  275.1 52.7 %collective-permute-start.74 = (bf16[4,24,3072]{2,1,0:T(8,128)(2,1)S(1)}, bf16[4,24,3072]{2,1,0:T(8,128)(2,1)}, u32[]{:S(2)}, u32[]{:S(2)}) collective-permute-start(bf16[4,24,3072]{2,1,0:T(8,128)(2,1)S(1)} %copy-done.39), channel_id=1, source_target_pairs={{0,16},{1,17},{2,18},{3,19},{4,20},{5,21},{6,22},{7,23},{8,24},{9,... | collective-permute-start | bytes 1769480 | tf_op jit(solution)/shard_map/ppermute | solution.py:138
  276.3 51.7 %collective-permute-start.75 = (bf16[4,24,3072]{2,1,0:T(8,128)(2,1)}, bf16[4,24,3072]{2,1,0:T(8,128)(2,1)}, u32[]{:S(2)}, u32[]{:S(2)}) collective-permute-start(bf16[4,24,3072]{2,1,0:T(8,128)(2,1)} %collective-permute-done.73.refs_1_), channel_id=1, source_target_pairs={{0,16},{1,17},{2,18},{3,19},{4,20},{5,21},{6,22},{7,23},{8,24},{9,... | collective-permute-start | bytes 1769480 | tf_op jit(solution)/shard_map/ppermute | solution.py:138
  329.2 37.6 %collective-permute-start.86 = (bf16[4,96,768]{2,1,0:T(8,128)(2,1)S(1)}, bf16[4,96,768]{2,1,0:T(8,128)(2,1)S(1)}, u32[]{:S(2)}, u32[]{:S(2)}) collective-permute-start(bf16[4,96,768]{2,1,0:T(8,128)(2,1)S(1)} %copy-done.40), channel_id=1, source_target_pairs={{0,1},{1,0},{2,3},{3,2},{4,5},{5,4},{6,7},{7,6},{8,9},{9,8},{10,11... | collective-permute-start | bytes 1769480 | tf_op jit(solution)/shard_map/ppermute | solution.py:138
  591.7 36.2 %collective-permute-start.108 = (bf16[2,2,4,24,768]{4,3,2,1,0:T(8,128)(2,1)}, bf16[2,2,4,24,768]{4,3,2,1,0:T(8,128)(2,1)}, u32[]{:S(2)}, u32[]{:S(2)}) collective-permute-start(bf16[2,2,4,24,768]{4,3,2,1,0:T(8,128)(2,1)} %dynamic-slice_bitcast_fusion.16), channel_id=1, source_target_pairs={{0,1},{1,0},{2,3},{3,2},{4,5},{5,4},{6,7},{7,6},{8,9},{9,8},{10,11... | collective-permute-start | bytes 1769480 | tf_op jit(solution)/shard_map/ppermute | solution.py:138
  599.6 62.9 %collective-permute-start.96 = (bf16[2,2,4,24,2432]{4,3,2,1,0:T(8,128)(2,1)}, bf16[2,2,4,24,2432]{4,3,2,1,0:T(8,128)(2,1)}, u32[]{:S(2)}, u32[]{:S(2)}) collective-permute-start(bf16[2,2,4,24,2432]{4,3,2,1,0:T(8,128)(2,1)} %dynamic-slice_bitcast_fusion.4), channel_id=1, source_target_pairs={{0,1},{1,0},{2,3},{3,2},{4,5},{5,4},{6,7},{7,6},{8,9},{9,8},{10,11... | collective-permute-start | bytes 5603336 | tf_op jit(solution)/shard_map/ppermute | solution.py:138
  601.2 28.9 %collective-permute-start.102 = (bf16[2,2,4,24,768]{4,3,2,1,0:T(8,128)(2,1)}, bf16[2,2,4,24,768]{4,3,2,1,0:T(8,128)(2,1)}, u32[]{:S(2)}, u32[]{:S(2)}) collective-permute-start(bf16[2,2,4,24,768]{4,3,2,1,0:T(8,128)(2,1)} %dynamic-slice_bitcast_fusion.17), channel_id=1, source_target_pairs={{0,1},{1,0},{2,3},{3,2},{4,5},{5,4},{6,7},{7,6},{8,9},{9,8},{10,11... | collective-permute-start | bytes 1769480 | tf_op jit(solution)/shard_map/ppermute | solution.py:138
  625.4 41.0 %collective-permute-start.90 = (bf16[2,2,4,24,2432]{4,3,2,1,0:T(8,128)(2,1)}, bf16[2,2,4,24,2432]{4,3,2,1,0:T(8,128)(2,1)S(1)}, u32[]{:S(2)}, u32[]{:S(2)}) collective-permute-start(bf16[2,2,4,24,2432]{4,3,2,1,0:T(8,128)(2,1)} %dynamic-slice_bitcast_fusion.5), channel_id=1, source_target_pairs={{0,1},{1,0},{2,3},{3,2},{4,5},{5,4},{6,7},{7,6},{8,9},{9,8},{10,11... | collective-permute-start | bytes 5603336 | tf_op jit(solution)/shard_map/ppermute | solution.py:138
  668.4 41.9 %collective-permute-start.91 = (bf16[2,4,24,2432]{3,2,1,0:T(8,128)(2,1)}, bf16[2,4,24,2432]{3,2,1,0:T(8,128)(2,1)}, u32[]{:S(2)}, u32[]{:S(2)}) collective-permute-start(bf16[2,4,24,2432]{3,2,1,0:T(8,128)(2,1)} %dynamic-slice_bitcast_fusion.11), channel_id=1, source_target_pairs={{0,16},{1,17},{2,18},{3,19},{4,20},{5,21},{6,22},{7,23},{8,24},{9,... | collective-permute-start | bytes 2801672 | tf_op jit(solution)/shard_map/ppermute | solution.py:138
  671.8 80.7 %collective-permute-start.133 = (bf16[2,4,96,768]{3,2,1,0:T(8,128)(2,1)}, bf16[2,4,96,768]{3,2,1,0:T(8,128)(2,1)}, u32[]{:S(2)}, u32[]{:S(2)}) collective-permute-start(bf16[2,4,96,768]{3,2,1,0:T(8,128)(2,1)} %dynamic-slice_bitcast_fusion.6), channel_id=1, source_target_pairs={{0,8},{1,9},{2,10},{3,11},{4,12},{5,13},{6,14},{7,15},{8,0},{9,1},... | collective-permute-start | bytes 3538952 | tf_op jit(solution)/shard_map/ppermute | solution.py:138
  674.8 80.8 %collective-permute-start.121 = (bf16[2,4,24,3072]{3,2,1,0:T(8,128)(2,1)}, bf16[2,4,24,3072]{3,2,1,0:T(8,128)(2,1)}, u32[]{:S(2)}, u32[]{:S(2)}) collective-permute-start(bf16[2,4,24,3072]{3,2,1,0:T(8,128)(2,1)} %dynamic-slice_bitcast_fusion.8), channel_id=1, source_target_pairs={{0,16},{1,17},{2,18},{3,19},{4,20},{5,21},{6,22},{7,23},{8,24},{9,... | collective-permute-start | bytes 3538952 | tf_op jit(solution)/shard_map/ppermute | solution.py:138
  736.2 28.9 %collective-permute-start.115 = (bf16[2,4,24,3072]{3,2,1,0:T(8,128)(2,1)S(1)}, bf16[2,4,24,3072]{3,2,1,0:T(8,128)(2,1)}, u32[]{:S(2)}, u32[]{:S(2)}) collective-permute-start(bf16[2,4,24,3072]{3,2,1,0:T(8,128)(2,1)S(1)} %dynamic-slice_bitcast_fusion.9), channel_id=1, source_target_pairs={{0,16},{1,17},{2,18},{3,19},{4,20},{5,21},{6,22},{7,23},{8,24},{9,... | collective-permute-start | bytes 3538952 | tf_op jit(solution)/shard_map/ppermute | solution.py:138
  757.2 24.9 %collective-permute-start.122 = (bf16[4,24,3072]{2,1,0:T(8,128)(2,1)S(1)}, bf16[4,24,3072]{2,1,0:T(8,128)(2,1)S(1)}, u32[]{:S(2)}, u32[]{:S(2)}) collective-permute-start(bf16[4,24,3072]{2,1,0:T(8,128)(2,1)S(1)} %dynamic-slice_bitcast_fusion.14), channel_id=1, source_target_pairs={{0,8},{1,9},{2,10},{3,11},{4,12},{5,13},{6,14},{7,15},{8,0},{9,1},... | collective-permute-start | bytes 1769480 | tf_op jit(solution)/shard_map/ppermute | solution.py:138
  759.5 25.4 %collective-permute-start.128 = (bf16[4,96,768]{2,1,0:T(8,128)(2,1)S(1)}, bf16[4,96,768]{2,1,0:T(8,128)(2,1)S(1)}, u32[]{:S(2)}, u32[]{:S(2)}) collective-permute-start(bf16[4,96,768]{2,1,0:T(8,128)(2,1)S(1)} %dynamic-slice_bitcast_fusion.13), channel_id=1, source_target_pairs={{0,16},{1,17},{2,18},{3,19},{4,20},{5,21},{6,22},{7,23},{8,24},{9,... | collective-permute-start | bytes 1769480 | tf_op jit(solution)/shard_map/ppermute | solution.py:138
  777.9 29.4 %collective-permute-start.135 = (bf16[96,768]{1,0:T(8,128)(2,1)S(1)}, bf16[96,768]{1,0:T(8,128)(2,1)S(1)}, u32[]{:S(2)}, u32[]{:S(2)}) collective-permute-start(bf16[96,768]{1,0:T(8,128)(2,1)S(1)} %get-tuple-element.181), channel_id=1, source_target_pairs={{0,2},{1,3},{2,0},{3,1},{4,6},{5,7},{6,4},{7,5},{8,10},{9,11},{10,... | collective-permute-start | bytes 442376 | tf_op jit(solution)/shard_map/ppermute | solution.py:138
  779.1 28.2 %collective-permute-start.137 = (bf16[96,768]{1,0:T(8,128)(2,1)S(1)}, bf16[96,768]{1,0:T(8,128)(2,1)S(1)}, u32[]{:S(2)}, u32[]{:S(2)}) collective-permute-start(bf16[96,768]{1,0:T(8,128)(2,1)S(1)} %get-tuple-element.182), channel_id=1, source_target_pairs={{0,6},{1,7},{2,4},{3,5},{4,2},{5,3},{6,0},{7,1},{8,14},{9,15},{10,... | collective-permute-start | bytes 442376 | tf_op jit(solution)/shard_map/ppermute | solution.py:138
  (250 other events, 3775.3 us)

commit v2 on v1

--- a/solution.py
+++ b/solution.py
@@ -133,125 +133,231 @@
         name="attend_bwd")(fl,qkv,qkv,qkv,do,lse)
 
 
-def swap(x, mask):
-    count = lax.axis_size(AX)
-    return lax.ppermute(x, AX, [(i, i ^ mask) for i in range(count)])
+MESH = pl.DeviceIdType.MESH
 
 
 def block_mesh():
     return lax.axis_size("dp") == 4 and lax.axis_size("fsdp") == 8
 
 
-CORE, ZLO, ZHI, XBIT, YBIT = 1, 2, 4, 8, 16
-
-
-def place_column(own, others):
-    z = lax.rem(lax.axis_index("fsdp") // 2, 4)
-    parts = [own] + others
-    rows = []
-    for k in range(4):
-        pick = parts[k]
-        for j in range(1, 4):
-            pick = jnp.where(z == j, parts[k ^ j], pick)
-        rows.append(pick)
-    return jnp.stack(rows)
-
-
-def assemble_kernel(*refs, cuts):
-    n = 8
-    ins = refs[:n]
-    outs = refs[n : n + len(cuts)]
-    sem = refs[-1]
-    dp = lax.axis_index("dp")
-    core = lax.rem(lax.axis_index("fsdp"), 2)
-    copies = []
-    for index in range(n):
-        rel_dp, rel_core = index % 4, index // 4
-        to_dp = (dp + rel_dp) - 2 * (dp & rel_dp)
-        to_core = core if rel_core == 0 else 1 - core
-        for at, (start, width) in enumerate(cuts):
-            src = ins[index]
-            if len(cuts) > 1:
-                src = src.at[:, :, pl.ds(start, width)]
-            copies.append(
-                pltpu.make_async_copy(src, outs[at].at[to_dp, :, to_core], sem.at[index, at])
-            )
-    for c in copies:
-        c.start()
-    for c in copies:
-        c.wait()
-
-
-def assemble(parts, widths):
-    r = parts[0].shape[1]
-    cuts = []
-    start = 0
-    for width in widths:
-        cuts.append((start, width))
-        start += width
-    outs = pl.pallas_call(
-        functools.partial(assemble_kernel, cuts=cuts),
-        in_specs=[pl.BlockSpec(memory_space=pl.ANY)] * 8,
-        out_specs=[pl.BlockSpec(memory_space=pltpu.VMEM)] * len(widths),
-        out_shape=[jax.ShapeDtypeStruct((4, 4, 2, r, w), BF) for w in widths],
-        scratch_shapes=[pltpu.SemaphoreType.DMA((8, len(widths)))],
-        cost_estimate=pl.CostEstimate(flops=0, bytes_accessed=4 * 32 * r * start, transcendentals=0),
-        name="assemble",
-    )(*parts)
-    return [o.reshape(32 * r, o.shape[-1]) for o in outs]
-
-
-def gather_rows(shard, first, widths):
+class Place:
+    def __init__(self):
+        d = lax.axis_index("dp")
+        f = lax.axis_index("fsdp")
+        self.y, self.x = lax.div(d, 2), lax.rem(d, 2)
+        self.z, self.c = lax.div(f, 2), lax.rem(f, 2)
+        self.zs = [self.z + 1 - 2 * lax.rem(self.z, 2), lax.rem(self.z + 2, 4), 3 - self.z]
+        self.to_core = (d, 2 * self.z + 1 - self.c)
+        self.to_x = (2 * self.y + 1 - self.x, f)
+        self.to_y = (2 * (1 - self.y) + self.x, f)
+        self.to_z = [(d, 2 * zz + self.c) for zz in self.zs]
+
+    def greet(self):
+        barrier = pltpu.get_barrier_semaphore()
+        peers = [self.to_core, self.to_x, self.to_y] + self.to_z
+        for peer in peers:
+            pl.semaphore_signal(barrier, inc=1, device_id=peer, device_id_type=MESH)
+        pl.semaphore_wait(barrier, len(peers))
+
+
+ALL = slice(None)
+
+
+class Gather:
+    COPIES = 12
+    STEPS = 5
+
+    def __init__(self, me, shard, out, send, recv, local):
+        self.me, self.shard, self.out, self.send, self.recv = me, shard, out, send, recv
+        self.width = shard.shape[-1]
+        self.cut = (self.width // 256 + self.width // 128 % 2) * 128
+        y, x, z, c = me.y, me.x, me.z, me.c
+        left, right = pl.ds(0, self.cut), pl.ds(self.cut, self.width - self.cut)
+        self.own = pltpu.make_async_copy(shard, out.at[y, x, z, c], local)
+        o = out.at
+        self.plan = [(None, me.to_z[j], out.at[y, x, z, c]) for j in range(3)] + [
+            (None, me.to_x, o[y, x, ALL, c, ALL, left]),
+            (None, me.to_y, o[y, x, ALL, c, ALL, right]),
+            (None, me.to_core, o[y, x, ALL, c]),
+            (None, me.to_y, o[y, ALL, ALL, c, ALL, left]),
+            (None, me.to_x, o[ALL, x, ALL, c, ALL, right]),
+            (None, me.to_core, o[y, 1 - x, ALL, c, ALL, left]),
+            (None, me.to_core, o[1 - y, x, ALL, c, ALL, right]),
+            (None, me.to_core, o[1 - y, ALL, ALL, c, ALL, left]),
+            (None, me.to_core, o[ALL, 1 - x, ALL, c, ALL, right]),
+        ]
+
+    def copy(self, k):
+        peer, ref = self.plan[k][1:]
+        return pltpu.make_async_remote_copy(
+            src_ref=self.shard if k < 3 else ref, dst_ref=ref, send_sem=self.send.at[k],
+            recv_sem=self.recv.at[k], device_id=peer, device_id_type=MESH)
+
+    def run(self, step):
+        waits, starts = [
+            ((), (0, 1, 2)),
+            ((0, 1, 2), (3, 4, 5)),
+            ((3, 4), (6, 7, 8, 9)),
+            ((6, 7), (10, 11)),
+            ((5, 8, 9, 10, 11), ()),
+        ][step]
+        if step == 0:
+            self.own.start()
+        for k in waits:
+            self.copy(k).wait_recv()
+        if step == 1:
+            self.own.wait()
+        for k in starts:
+            self.copy(k).start()
+        if step == 4:
+            for k in range(12):
+                self.copy(k).wait_send()
+
+
+class Scatter:
+    COPIES = 8
+    STEPS = 5
+
+    def __init__(self, me, term, out, own, r0, r1, r2, r3, send, recv, local):
+        self.me, self.out, self.own, self.r = me, out, own, (r0, r1, r2, r3)
+        self.send, self.recv = send, recv
+        self.width = own.shape[-1]
+        self.cut = (self.width // 256 + self.width // 128 % 2) * 128
+        y, x, z, c = me.y, me.x, me.z, me.c
+        left, right = pl.ds(0, self.cut), pl.ds(self.cut, self.width - self.cut)
+        self.mine = pltpu.make_async_copy(term.at[ALL, ALL, ALL, c], own, local)
+        self.left, self.right = left, right
+        self.plan = [
+            (term.at[ALL, ALL, ALL, 1 - c], me.to_core, r0),
+            (own.at[1 - y, ALL, ALL, ALL, left], me.to_y, r1.at[ALL, ALL, ALL, left]),
+            (own.at[ALL, 1 - x, ALL, ALL, right], me.to_x, r1.at[ALL, ALL, ALL, right]),
+            (own.at[y, 1 - x, ALL, ALL, left], me.to_x, r2.at[ALL, ALL, left]),
+            (own.at[1 - y, x, ALL, ALL, right], me.to_y, r2.at[ALL, ALL, right]),
+        ] + [(own.at[y, x, me.zs[j]], me.to_z[j], r3.at[j]) for j in range(3)]
+
+    def copy(self, k):
+        src, peer, dst = self.plan[k]
+        return pltpu.make_async_remote_copy(
+            src_ref=src, dst_ref=dst, send_sem=self.send.at[k], recv_sem=self.recv.at[k],
+            device_id=peer, device_id_type=MESH)
+
+    def run(self, step):
+        y, x, z = self.me.y, self.me.x, self.me.z
+        own, (r0, r1, r2, r3) = self.own, self.r
+        left, right = self.left, self.right
+        if step == 0:
+            self.mine.start()
+            self.copy(0).start()
+        elif step == 1:
+            self.mine.wait()
+            self.copy(0).wait_recv()
+
+            @pl.loop(0, 4)
+            def _(k):
+                for a in range(2):
+                    for b in range(2):
+                        own[a, b, k] = own[a, b, k] + r0[a, b, k]
+
+            self.copy(1).start()
+            self.copy(2).start()
+        elif step == 2:
+            self.copy(1).wait_recv()
+            self.copy(2).wait_recv()
+
+            @pl.loop(0, 4)
+            def _(k):
+                for a in range(2):
+                    own[y, a, k, :, left] = own[y, a, k, :, left] + r1[a, k, :, left]
+                    own[a, x, k, :, right] = own[a, x, k, :, right] + r1[a, k, :, right]
+
+            self.copy(3).start()
+            self.copy(4).start()
+        elif step == 3:
+            self.copy(3).wait_recv()
+            self.copy(4).wait_recv()
+
+            @pl.loop(0, 4)
+            def _(k):
+                own[y, x, k] = own[y, x, k] + r2[k]
+
+            for k in (5, 6, 7):
+                self.copy(k).start()
+        else:
+            total = own[y, x, z].astype(F32)
+            for k in (5, 6, 7):
+                self.copy(k).wait_recv()
+                total = total + r3[k - 5].astype(F32)
+            self.out[...] = total
+            for k in range(8):
+                self.copy(k).wait_send()
+
+
+def host_specs(kind, arrays):
+    n = len(arrays)
+    sems = [pltpu.SemaphoreType.DMA((n, kind.COPIES)), pltpu.SemaphoreType.DMA((n, kind.COPIES)),
+            pltpu.SemaphoreType.DMA((n,))]
+    if kind is Gather:
+        ins = [pl.BlockSpec(memory_space=pltpu.VMEM)] * n
+        outs = [pl.BlockSpec(memory_space=pl.ANY)] * n
+        shapes = [jax.ShapeDtypeStruct((2, 2, 4, 2) + a.shape, a.dtype) for a in arrays]
+        return ins, outs, shapes, sems
+    ins = [pl.BlockSpec(memory_space=pl.ANY)] * n
+    outs = [pl.BlockSpec(memory_space=pltpu.VMEM)] * n
+    shapes = [jax.ShapeDtypeStruct(a.shape[4:], F32) for a in arrays]
+    scratch = []
+    for a in arrays:
+        tail = a.shape[4:]
+        for lead in ((2, 2, 4), (2, 2, 4), (2, 4), (4,), (3,)):
+            scratch.append(pltpu.VMEM(lead + tail, a.dtype))
+    return ins, outs, shapes, scratch + sems
+
+
+def host_build(kind, ins, outs, scratch):
+    me = Place()
+    send, recv, local = scratch[-3:]
+    jobs = []
+    for i in range(len(ins)):
+        extra = scratch[5 * i : 5 * i + 5] if kind is Scatter else ()
+        jobs.append(kind(me, ins[i], outs[i], *extra, send.at[i], recv.at[i], local.at[i]))
+    return me, jobs
+
+
+def in_order(count, steps):
+    return [(i, t - i) for t in range(count + steps - 1) for i in range(count) if 0 <= t - i < steps]
+
+
+def comm_kernel(*refs, kind, n):
+    me, jobs = host_build(kind, refs[:n], refs[n : 2 * n], refs[2 * n :])
+    me.greet()
+    for i in range(n):
+        jobs[i].run(0)
+    for i, t in in_order(n, kind.STEPS):
+        if t > 0:
+            jobs[i].run(t)
+
+
+def exchange(kind, arrays, ident, name):
+    n = len(arrays)
+    ins, outs, shapes, scratch = host_specs(kind, arrays)
+    return pl.pallas_call(
+        functools.partial(comm_kernel, kind=kind, n=n),
+        in_specs=ins, out_specs=outs, out_shape=shapes, scratch_shapes=scratch,
+        compiler_params=pltpu.CompilerParams(
+            collective_id=ident, has_side_effects=True, vmem_limit_bytes=48 << 20),
+        name=name)(*arrays)
+
+
+def gather_all(shards, ident):
     if not block_mesh():
-        whole = lax.all_gather(shard, AX, axis=0, tiled=True)
-        out = []
-        start = 0
-        for width in widths:
-            out.append(whole[:, start : start + width])
-            start += width
-        return out
-    second = XBIT + YBIT - first
-    column = place_column(shard, [swap(shard, 2 * j) for j in range(1, 4)])
-    near = swap(column, first)
-    far = [swap(column, second), swap(near, second)]
-    if first == XBIT:
-        mine = [column, near, far[0], far[1]]
-    else:
-        mine = [column, far[0], near, far[1]]
-    theirs = [swap(part, CORE) for part in mine]
-    return assemble(mine + theirs, widths)
-
-
-def scatter_rows(term, first):
-    rows = term.shape[0]
-    count = lax.axis_size(AX)
-    r = rows // count
+        return [lax.all_gather(a, AX, axis=0, tiled=True) for a in shards]
+    wide = exchange(Gather, shards, ident, "gather")
+    return [w.reshape(-1, w.shape[-1]) for w in wide]
+
+
+def scatter_all(terms, ident):
     if not block_mesh():
-        return lax.psum_scatter(term.astype(F32), AX, scatter_dimension=0, tiled=True)
-    width = term.shape[1]
-    f = lax.axis_index("fsdp")
-    d = lax.axis_index("dp")
-    core, z = lax.rem(f, 2), f // 2
-    xbit, ybit = lax.rem(d, 2), d // 2
-
-    def fold(value, axis, bit, mask):
-        kept = lax.dynamic_index_in_dim(value, bit, axis, keepdims=False)
-        sent = lax.dynamic_index_in_dim(value, 1 - bit, axis, keepdims=False)
-        return (kept.astype(F32) + swap(sent, mask).astype(F32)).astype(BF)
-
-    value = term.reshape(2, 2, 4, 2, r, width)
-    value = fold(value, 3, core, CORE)
-    if first == XBIT:
-        value = fold(value, 0, ybit, YBIT)
-        value = fold(value, 0, xbit, XBIT)
-    else:
-        value = fold(value, 1, xbit, XBIT)
-        value = fold(value, 0, ybit, YBIT)
-    total = lax.dynamic_index_in_dim(value, z, 0, keepdims=False).astype(F32)
-    for j in range(1, 4):
-        other = lax.dynamic_index_in_dim(value, z ^ j, 0, keepdims=False)
-        total = total + swap(other, 2 * j).astype(F32)
-    return total
+        return [lax.psum_scatter(t.astype(F32), AX, scatter_dimension=0, tiled=True) for t in terms]
+    return exchange(Scatter, [t.reshape(2, 2, 4, 2, -1, t.shape[-1]) for t in terms], ident, "scatter")
 
 
 def layer_norm(values, gain, shift):
@@ -296,24 +402,18 @@
     return [turned[i] for i in range(vector_count)], wide
 
 
-def gather_use(local, layer):
+def local_shards(local):
     (ga, sa, hw, qb, vb, mw, mb, gf, sf, ew, eb, sw, sb) = local
     small = pack_columns([ga, sa, qb, vb, mb, gf, sf, sb], eb, 1)
-    width = hw.shape[1]
-    if layer == 0:
-        half = width // 2
-        wa, sm = gather_rows(jnp.concatenate([hw[:, :half], small], axis=1), XBIT, [half, LANES])
-        (wb,) = gather_rows(hw[:, half:], YBIT, [width - half])
-        heads = jnp.concatenate([wa, wb], axis=1)
-    else:
-        heads, sm = gather_rows(jnp.concatenate([hw, small], axis=1), XBIT, [width, LANES])
-    (mix,) = gather_rows(mw, YBIT, [mw.shape[1]])
-    (expand,) = gather_rows(ew, XBIT, [ew.shape[1]])
-    (shrink,) = gather_rows(sw, YBIT, [sw.shape[1]])
-    vecs, wide = unpack_columns(sm, 8, eb.shape[0] // ga.shape[0], lax.axis_size(AX))
+    return [jnp.concatenate([hw, small], axis=1), mw, ew, sw]
+
+
+def as_weights(whole, width, ways):
+    heads, mix, expand, shrink = whole
+    vecs, wide = unpack_columns(heads[:, 3 * width :], 8, ways, lax.axis_size(AX))
     vecs = [v.astype(F32) for v in vecs]
     return dict(zip(("ga", "sa", "qb", "vb", "mb", "gf", "sf", "sb"), vecs), eb=wide.astype(F32),
-                heads=heads, mix=mix, expand=expand, shrink=shrink)
+                heads=heads[:, : 3 * width], mix=mix, expand=expand, shrink=shrink)
 
 
 def forward_use(hidden, w, first_len):
@@ -331,21 +431,19 @@
 
 def backward_use(grad_out, kept, w, first_len):
     hidden, normed, qkv, attended, lse, middle, normed_two, activated, slope = kept
-    width = hidden.shape[1]
     count = lax.axis_size(AX)
     grad_low = grad_out.astype(BF)
     shrink_term = inner_rows(activated, grad_low).astype(BF)
-    shrink_share = scatter_rows(shrink_term, YBIT)
     sb = column_sums(grad_low)
     dz = (times_transposed(grad_low, w["shrink"]) * slope.astype(F32)).astype(BF)
-    expand_share = scatter_rows(inner_rows(normed_two, dz).astype(BF), XBIT)
+    expand_term = inner_rows(normed_two, dz).astype(BF)
     eb = column_sums(dz)
     dc = times_transposed(dz, w["expand"])
     unused, norm_back = jax.vjp(layer_norm, middle, w["gf"], w["sf"])
     middle_norm, gf, sf = norm_back(dc)
     dm = grad_out + middle_norm
     dmb = dm.astype(BF)
-    mix_share = scatter_rows(inner_rows(attended, dmb).astype(BF), YBIT)
+    mix_term = inner_rows(attended, dmb).astype(BF)
     mb = column_sums(dmb)
     do = times_transposed(dmb, w["mix"]).astype(BF)
     dq, dk, dv = attend_bwd(qkv, do, lse, first_len)
@@ -356,14 +454,14 @@
     da = times_transposed(dqkv, w["heads"])
     unused, first_back = jax.vjp(layer_norm, hidden, w["ga"], w["sa"])
     hidden_norm, ga, sa = first_back(da)
-    small = pack_columns([ga, sa, qb, vb, mb, gf, sf, sb], eb, count).astype(BF)
-    heads_share = scatter_rows(jnp.concatenate([heads_term, small], axis=1), XBIT)
-    vecs, wide = unpack_columns(heads_share[:, 3 * width :], 8, eb.shape[0] // width, 1)
+    small = pack_columns([ga, sa, qb, vb, mb, gf, sf, sb], eb, count)
+    return dm + hidden_norm, (shrink_term, expand_term, mix_term, heads_term), small
+
+
+def as_shares(shrink, expand, mix, heads, small):
+    vecs, wide = unpack_columns(small, 8, shrink.shape[0] // heads.shape[0], 1)
     ga, sa, qb, vb, mb, gf, sf, sb = vecs
-    return dm + hidden_norm, (
-        ga, sa, heads_share[:, : 3 * width], qb, vb, mix_share, mb, gf, sf, expand_share, wide,
-        shrink_share, sb,
-    )
+    return ga, sa, heads, qb, vb, mix, mb, gf, sf, expand, wide, shrink, sb
 
 
 def pick_shards(stacks, source):
@@ -384,16 +482,23 @@
 
 def body(tokens, cotangent, tie_map, first_length, *stacks):
     hidden = tokens.astype(F32)
+    width = hidden.shape[1]
     sources = [tie_map[i] for i in range(LAYERS)]
-    weights = [gather_use(pick_shards(stacks, s), i) for i, s in enumerate(sources)]
+    shards = [local_shards(pick_shards(stacks, s)) for s in sources]
+    ways = shards[0][3].shape[0] // shards[0][0].shape[0]
+    whole = gather_all(shards[0] + shards[1], 0)
+    weights = [as_weights(whole[4 * i : 4 * i + 4], width, ways) for i in range(LAYERS)]
     kept = []
     for i in range(LAYERS):
         hidden, saved = forward_use(hidden, weights[i], first_length)
         kept.append(saved)
     grad = cotangent.astype(F32)
-    shares = [None] * LAYERS
+    terms, small = [None] * LAYERS, [None] * LAYERS
     for i in reversed(range(LAYERS)):
-        grad, shares[i] = backward_use(grad, kept[i], weights[i], first_length)
+        grad, terms[i], small[i] = backward_use(grad, kept[i], weights[i], first_length)
+    late = scatter_all(list(terms[1]), 1)
+    early = scatter_all(list(terms[0]) + [jnp.concatenate(small, axis=1)], 2)
+    shares = [as_shares(*early[:4], early[4][:, :LANES]), as_shares(*late, early[4][:, LANES:])]
     return (hidden.astype(BF), grad.astype(BF), *place_terms(sources, shares))
 
 

time: 833 us -> 719 us (0.86)
  Pallas kernels: 139 us -> 423 us
  waiting for transfers between devices: 176 us -> 0 us
  starting transfers between devices: 147 us -> 0 us
  local copies, waits for them, and re-layouts: 107 us -> 55.2 us
  other arithmetic: 71.1 us -> 39.7 us
    pallas_call x9 -> x3, Pallas kernels: 32.9 us -> 317 us  [exchange(): pl.pallas_call(functools.partial(comm_kernel, kind=kind, n=n), in_specs=i...]
    ppermute x138 -> x0, waiting for transfers between devices: 176 us -> none  [swap(): return lax.ppermute(x, AX, [(i, i ^ mask) for i in range(count)])]
    ppermute x138 -> x0, starting transfers between devices: 147 us -> none  [swap(): return lax.ppermute(x, AX, [(i, i ^ mask) for i in range(count)])]
    squeeze x32 -> x0, local copies, waits for them, and re-layouts: 23.6 us -> none  [the longest x24 23.3 us: fold(): sent = lax.dynamic_index_in_dim(value, 1 - bit, axis, keepdims=False)]
    convert_element_type x26 -> x2, other arithmetic: 19.7 us -> 0.01 us  [as_weights(): wide.astype(F32)]
    another operation x36, local copies, waits for them, and re-layouts: 17.9 us -> 4.69 us  [pack_columns(): block = jnp.concatenate([jnp.stack(vectors, axis=1), spread], axis=1)]
    dot_general x8, matrix products: 53.5 us -> 63.2 us  [inner_rows(): lax.dot_general(left, right, (((0,), (0,)), ((), ())), preferred_element_...]
    unnamed x296 -> x146, local copies, waits for them, and re-layouts: 28.6 us -> 23.6 us
  transfers between devices with their start and end apart: 138 -> 0, of which waited for: 42 -> 0; matrix products, arithmetic and copies ran while one was open for 22% -> 0% of each run, Pallas kernels for 10% -> 0%
where the time goes in v2:
time: 719 us; the launch traced here: 710 us
  Pallas kernels  423 us (59%)
  matrix products  186 us (26%)
  local copies, waits for them, and re-layouts  55.2 us (8%)
  other arithmetic  39.7 us (6%)
    pallas_call x3, Pallas kernels, exchange(): pl.pallas_call(functools.partial(comm_kernel, kind=kind, n=n), in_specs=i...  317 us
    dot_general x8, matrix products, times_transposed(): lax.dot_general(left, right, (((1,), (1,)), ((), ())), preferred_element_...  67 us
    dot_general x8, matrix products, inner_rows(): lax.dot_general(left, right, (((0,), (0,)), ((), ())), preferred_element_...  63.2 us
    pallas_call x2, Pallas kernels, attend_bwd(): pl.pallas_call(functools.partial(bwd_kernel, bq=bq), grid_spec=pltpu.Pref...  54.3 us
    pallas_call x2, Pallas kernels, attend_fwd(): pl.pallas_call(functools.partial(fwd_kernel, bq=bq), grid_spec=pltpu.Pref...  51.6 us
    unnamed x146, local copies, waits for them, and re-layouts  23.6 us
    dot_general x2, matrix products, forward_use(): jnp.dot(activated, w['shrink'], preferred_element_type=F32)  21.1 us
    dot_general x2, matrix products, forward_use(): jnp.dot(normed_two, w['expand'], preferred_element_type=F32) + w['eb']  16.8 us

profile of v2, /device:TPU:0, one launch (start us, length us, event | category | flops | bytes accessed | tf_op | source)
XLA Modules:
  0.0 710.2 jit_solution(16077730926665717566)
XLA Ops:
  23.6 138.8 %gather.1 = (bf16[2,2,4,2,24,2432]{5,4,3,2,1,0:T(8,128)(2,1)}, bf16[2,2,4,2,24,768]{5,4,3,2,1,0:T(8,128)(2,1)S(1)}, bf16[2,2,4,2,24,3072]{5,4,3,2,1,0:T(8,128)(2...) custom-call(bf16[24,2432]{1,0:T(8,128)(2,1)S(1)} %fusion.36.refs_0_,, ...), custom_call_target="tpu_custom_call" | custom-call | tf_op jit(solution)/shard_map/gather/pallas_call | solution.py:342
  165.7 8.7 %add_convert_fusion.1.q_ref.k_ref.v_ref = bf16[1024,2304]{1,0:T(8,128)(2,1)} fusion(f32[2304]{0:T(1024)S(1)} %get-tuple-element.178, bf16[768,2432]{1,0:T(8,128)(2,1)} %bitcast.153, bf16[1024,768]{0,1:T(8,128)(2,1)} %copy-done.5, f32[768]{0:T(1024)S(1)} %get-tuple-element.136, f32[768]{0:T(1024)S(1)} %get-tuple-element.137, f32[1024]{0:T(1024)S(1)} %fusion.40, ...), kind=kOutput, calls=%fused_computation.24 | convolution fusion | flops 3633315840 | bytes 9853952 | tf_op jit(solution)/shard_map/dot_general | solution.py:422
  174.4 25.9 %attend_fwd.2 = (bf16[1024,768]{1,0:T(8,128)(2,1)S(1)}, f32[6,2,1024]{2,1,0:T(2,128)S(1)}) custom-call(s32[1]{0:T(128)S(6)} %copy.169.fl_ref, bf16[1024,2304]{1,0:T(8,128)(2,1)} %add_convert_fusion.1.q_ref.k_ref.v_ref, bf16[1024,2304]{1,0:T(8,128)(2,1)} %add_convert_fusion.1.q_ref.k_ref.v_ref, bf16[1024,2304]{1,0:T(8,128)(2,1)} %add_convert_fusion.1.q_ref.k_ref.v_ref), custom_call_target="tpu_custom_call" | custom-call | flops 6442450944 | bytes 6291456 | tf_op jit(solution)/shard_map/attend_fwd/pallas_call | solution.py:65
  204.0 8.3 %fusion.83 = f32[1024,3072]{1,0:T(8,128)} fusion(bf16[768,3072]{1,0:T(8,128)(2,1)S(1)} %bitcast.131, f32[1024,768]{0,1:T(8,128)S(1)} %get-tuple-element.206, f32[768]{0:T(1024)S(1)} %get-tuple-element.132, f32[768]{0:T(1024)S(1)} %get-tuple-element.130, f32[1024]{0:T(1024)S(1)} %fusion.41, f32[1024]{0:T(1024)S(1)} %broadcast_multiply_fusion.2), kind=kOutput, calls=%fused_computation.242 | convolution fusion | flops 4835770368 | bytes 20461568 | tf_op jit(solution)/shard_map/dot_general | solution.py:426
  212.3 10.9 %fusion.91 = (f32[1024]{0:T(1024)S(1)}, f32[1024,768]{0,1:T(8,128)S(1)}) fusion(f32[768]{0:T(1024)S(1)} %get-tuple-element.131, f32[1024,768]{0,1:T(8,128)S(1)} %get-tuple-element.206, bf16[3072,768]{1,0:T(8,128)(2,1)} %bitcast.160, f32[1024,3072]{1,0:T(8,128)} %fusion.83, f32[3072]{0:T(1024)S(1)} %reshape.367), kind=kOutput, calls=%fused_computation.248 | convolution fusion | flops 4865653760 | bytes 23612416 | tf_op jit(solution)/shard_map/dot_general | solution.py:428
  223.7 5.8 add_convert_fusion.q_ref.k_ref.v_ref
  229.5 25.8 %attend_fwd.3 = (bf16[1024,768]{1,0:T(8,128)(2,1)S(1)}, f32[6,2,1024]{2,1,0:T(2,128)S(1)}) custom-call(s32[1]{0:T(128)S(6)} %copy.169.fl_ref, bf16[1024,2304]{1,0:T(8,128)(2,1)} %add_convert_fusion.q_ref.k_ref.v_ref, bf16[1024,2304]{1,0:T(8,128)(2,1)} %add_convert_fusion.q_ref.k_ref.v_ref, bf16[1024,2304]{1,0:T(8,128)(2,1)} %add_convert_fusion.q_ref.k_ref.v_ref), custom_call_target="tpu_custom_call" | custom-call | flops 6442450944 | bytes 6291456 | tf_op jit(solution)/shard_map/attend_fwd/pallas_call | solution.py:65
  257.6 8.5 %fusion.84 = f32[1024,3072]{1,0:T(8,128)} fusion(bf16[768,3072]{1,0:T(8,128)(2,1)S(1)} %bitcast.139, f32[1024,768]{0,1:T(8,128)S(1)} %get-tuple-element.210, f32[768]{0:T(1024)S(1)} %get-tuple-element.124, f32[768]{0:T(1024)S(1)} %get-tuple-element.122, f32[1024]{0:T(1024)S(1)} %fusion.43, f32[1024]{0:T(1024)S(1)} %broadcast_multiply_fusion), kind=kOutput, calls=%fused_computation.243 | convolution fusion | flops 4835770368 | bytes 20461568 | tf_op jit(solution)/shard_map/dot_general | solution.py:426
  266.0 10.2 %add_convert_fusion.3 = bf16[1024,768]{0,1:T(8,128)(2,1)} fusion(f32[1024,768]{0,1:T(8,128)S(1)} %get-tuple-element.210, bf16[3072,768]{1,0:T(8,128)(2,1)S(1)} %bitcast.165, f32[768]{0:T(1024)S(1)} %get-tuple-element.123, f32[1024,3072]{1,0:T(8,128)} %fusion.84, f32[3072]{0:T(1024)S(1)} %reshape.376), kind=kOutput, calls=%fused_computation.68 | convolution fusion | flops 4865654784 | bytes 22035456 | tf_op jit(solution)/shard_map/dot_general | solution.py:428
  278.8 18.4 %convert_reduce_fusion = (f32[3072]{0:T(1024)S(1)}, bf16[1024,3072]{1,0:T(8,128)(2,1)S(1)}) fusion(f32[1024,3072]{1,0:T(8,128)} %fusion.84, f32[3072]{0:T(1024)S(1)} %reshape.376, bf16[3072,768]{1,0:T(8,128)(2,1)} %bitcast.162, bf16[1024,768]{1,0:T(8,128)(2,1)} %param.18), kind=kOutput, calls=%fused_computation.18 | convolution fusion | flops 4907332608 | bytes 25190400 | tf_op jit(solution)/shard_map/dot_general | solution.py:374
  297.2 14.6 %convolution_convert_fusion.1 = bf16[3072,768]{1,0:T(8,128)(2,1)} fusion(bf16[1024,768]{1,0:T(8,128)(2,1)S(1)} %copy-done.28, f32[1024,3072]{1,0:T(8,128)} %fusion.84, f32[3072]{0:T(1024)S(1)} %reshape.376), kind=kOutput, calls=%fused_computation.26 | convolution fusion | flops 4865654784 | bytes 18886656 | tf_op jit(solution)/shard_map/dot_general | solution.py:370
  311.9 9.1 %fusion.94 = (f32[768]{0:T(1024)S(1)}, f32[1024,768]{1,0:T(8,128)}) fusion(bf16[1024,3072]{1,0:T(8,128)(2,1)S(1)} %get-tuple-element.216, bf16[768,3072]{1,0:T(8,128)(2,1)} %bitcast.136), kind=kOutput, calls=%fused_computation.251 | convolution fusion | flops 4832623616 | bytes 14158848 | tf_op jit(solution)/shard_map/dot_general | solution.py:374
  321.2 3.6 copy.146
  324.7 3.9 multiply_reduce_fusion
  328.7 9.9 %convolution_convert_fusion = bf16[768,3072]{1,0:T(8,128)(2,1)} fusion(bf16[1024,3072]{1,0:T(8,128)(2,1)} %copy-done.58, f32[1024,768]{0,1:T(8,128)S(1)} %copy-done.15, f32[768]{0:T(1024)S(1)} %get-tuple-element.124, f32[768]{0:T(1024)S(1)} %get-tuple-element.122, f32[1024]{0:T(1024)S(1)} %fusion.43, f32[1024]{0:T(1024)S(1)} %broadcast_multiply_fusion), kind=kOutput, calls=%fused_computation.25 | convolution fusion | flops 4838129664 | bytes 14170112 | tf_op jit(solution)/shard_map/dot_general | solution.py:370
  345.2 27.2 %attend_bwd.2 = (bf16[1024,768]{1,0:T(8,128)(2,1)S(1)}, bf16[1024,768]{1,0:T(8,128)(2,1)S(1)}, bf16[1024,768]{1,0:T(8,128)(2,1)S(1)}) custom-call(s32[1]{0:T(128)S(6)} %copy.169.fl_ref, bf16[1024,2304]{1,0:T(8,128)(2,1)} %add_convert_fusion.q_ref.k_ref.v_ref, bf16[1024,2304]{1,0:T(8,128)(2,1)} %add_convert_fusion.q_ref.k_ref.v_ref, ...), custom_call_target="tpu_custom_call" | custom-call | flops 16106127360 | bytes 12582912 | tf_op jit(solution)/shard_map/attend_bwd/pallas_call | solution.py:125
  375.1 5.5 fusion.93
  380.6 4.4 convolution_convert_fusion.4
  385.0 91.5 %scatter.3 = (f32[96,768]{1,0:T(8,128)S(1)}, f32[24,3072]{1,0:T(8,128)S(1)}, f32[24,768]{1,0:T(8,128)S(1)}, f32[24,2304]{1,0:T(8,128)S(1)}) custom-call(bf16[2,2,4,2,96,768]{5,4,3,2,1,0:T(8,128)(2,1)} %bitcast.141, bf16[2,2,4,2,24,3072]{5,4,3,2,1,0:T(8,128)(2,1)} %bitcast.142, bf16[2,2,4,2,24,768]{5,4,3,2,1,0:T(8,128)(2,1)S(1)} %bitcast.124, ...), custom_call_target="tpu_custom_call" | custom-call | tf_op jit(solution)/shard_map/scatter/pallas_call | solution.py:342
  476.6 3.9 copy.147
  490.9 16.5 %convert_reduce_fusion.1 = (f32[3072]{0:T(1024)S(1)}, bf16[1024,3072]{1,0:T(8,128)(2,1)S(1)}) fusion(f32[1024,3072]{1,0:T(8,128)} %fusion.83, f32[3072]{0:T(1024)S(1)} %copy-done.52, bf16[3072,768]{1,0:T(8,128)(2,1)} %bitcast.161, f32[1024,768]{0,1:T(8,128)} %get-tuple-element.157), kind=kOutput, calls=%fused_computation.19 | convolution fusion | flops 4908119040 | bytes 26763264 | tf_op jit(solution)/shard_map/dot_general | solution.py:374
  507.4 15.4 %convolution_convert_fusion.3 = bf16[3072,768]{1,0:T(8,128)(2,1)} fusion(f32[1024,768]{0,1:T(8,128)S(1)} %copy-done.18, f32[1024,3072]{1,0:T(8,128)} %fusion.83, f32[3072]{0:T(1024)S(1)} %copy-done.52), kind=kOutput, calls=%fused_computation.28 | convolution fusion | flops 4866441216 | bytes 20459520 | tf_op jit(solution)/shard_map/dot_general | solution.py:370
  522.8 6.8 fusion.96
  529.9 3.5 copy.148
  533.4 3.9 multiply_reduce_fusion.2
  537.4 10.1 %convolution_convert_fusion.2 = bf16[768,3072]{1,0:T(8,128)(2,1)} fusion(bf16[1024,3072]{1,0:T(8,128)(2,1)} %copy-done.59, f32[1024,768]{0,1:T(8,128)S(1)} %copy-done.10, f32[768]{0:T(1024)S(1)} %copy-done.36, f32[768]{0:T(1024)S(1)} %copy-done.32, f32[1024]{0:T(1024)S(1)} %copy-done.34, f32[1024]{0:T(1024)S(1)} %copy-done.30), kind=kOutput, calls=%fused_computation.27 | convolution fusion | flops 4838129664 | bytes 14170112 | tf_op jit(solution)/shard_map/dot_general | solution.py:370
  555.3 27.0 %attend_bwd.3 = (bf16[1024,768]{1,0:T(8,128)(2,1)S(1)}, bf16[1024,768]{1,0:T(8,128)(2,1)S(1)}, bf16[1024,768]{1,0:T(8,128)(2,1)S(1)}) custom-call(s32[1]{0:T(128)S(6)} %copy.169.fl_ref, bf16[1024,2304]{1,0:T(8,128)(2,1)} %add_convert_fusion.1.q_ref.k_ref.v_ref, bf16[1024,2304]{1,0:T(8,128)(2,1)} %add_convert_fusion.1.q_ref.k_ref.v_ref, ...), custom_call_target="tpu_custom_call" | custom-call | flops 16106127360 | bytes 12582912 | tf_op jit(solution)/shard_map/attend_bwd/pallas_call | solution.py:125
  585.1 5.6 fusion.95
  590.7 6.0 convolution_convert_fusion.5
  596.6 3.5 copy.149
  605.3 4.5 add_convert_fusion.2
  614.9 86.5 %scatter.2 = (f32[96,768]{1,0:T(8,128)S(1)}, f32[24,3072]{1,0:T(8,128)S(1)}, f32[24,768]{1,0:T(8,128)S(1)}, f32[24,2304]{1,0:T(8,128)S(1)}, f32[24,256]{1,0:T(8,128)S(1)}) custom-call(bf16[2,2,4,2,96,768]{5,4,3,2,1,0:T(8,128)(2,1)} %bitcast.135, bf16[2,2,4,2,24,3072]{5,4,3,2,1,0:T(8,128)(2,1)} %bitcast.140, bf16[2,2,4,2,24,768]{5,4,3,2,1,0:T(8,128)(2,1)S(1)} %bitcast.123, ...), custom_call_target="tpu_custom_call" | custom-call | tf_op jit(solution)/shard_map/scatter/pallas_call | solution.py:342
  (282 shorter events, 79.2 us)
Async XLA Ops:
  20.1 145.5 %copy-start.37 = (f32[1024]{0:T(1024)}, f32[1024]{0:T(1024)S(1)}, u32[]{:S(2)}) copy-start(f32[1024]{0:T(1024)S(1)} %broadcast_multiply_fusion.3) | copy-start | bytes 12292
  20.6 143.2 %copy-start.43 = (f32[1024]{0:T(1024)}, f32[1024]{0:T(1024)S(1)}, u32[]{:S(2)}) copy-start(f32[1024]{0:T(1024)S(1)} %fusion.22) | copy-start | bytes 12292
  21.0 153.4 %copy-start.41 = (f32[1024]{0:T(1024)}, f32[1024]{0:T(1024)S(1)}, u32[]{:S(2)}) copy-start(f32[1024]{0:T(1024)S(1)} %fusion.40) | copy-start | bytes 12292
  162.5 37.8 %copy-start.1 = (bf16[2,2,4,2,24,768]{5,4,3,2,1,0:T(8,128)(2,1)}, bf16[2,2,4,2,24,768]{5,4,3,2,1,0:T(8,128)(2,1)S(1)}, u32[]{:S(2)}) copy-start(bf16[2,2,4,2,24,768]{5,4,3,2,1,0:T(8,128)(2,1)S(1)} %get-tuple-element.44) | copy-start | bytes 3538948
  163.9 10.5 %copy-start.39 = (f32[768]{0:T(1024)}, f32[768]{0:T(1024)S(1)}, u32[]{:S(2)}) copy-start(f32[768]{0:T(1024)S(1)} %get-tuple-element.137) | copy-start | bytes 9220
  163.9 10.5 %copy-start.56 = (f32[768]{0:T(1024)}, f32[768]{0:T(1024)S(1)}, u32[]{:S(2)}) copy-start(f32[768]{0:T(1024)S(1)} %get-tuple-element.136) | copy-start | bytes 9220
  163.9 38.4 %copy-start.31 = (f32[768]{0:T(1024)}, f32[768]{0:T(1024)S(1)}, u32[]{:S(2)}) copy-start(f32[768]{0:T(1024)S(1)} %get-tuple-element.130) | copy-start | bytes 9220
  163.9 38.4 %copy-start.35 = (f32[768]{0:T(1024)}, f32[768]{0:T(1024)S(1)}, u32[]{:S(2)}) copy-start(f32[768]{0:T(1024)S(1)} %get-tuple-element.132) | copy-start | bytes 9220
  164.2 48.1 %copy-start.51 = (f32[3072]{0:T(1024)}, f32[3072]{0:T(1024)S(1)}, u32[]{:S(2)}) copy-start(f32[3072]{0:T(1024)S(1)} %reshape.367) | copy-start | bytes 36868
  174.4 25.9 %copy-start.6 = (bf16[1024,768]{0,1:T(8,128)(2,1)S(1)}, bf16[1024,768]{0,1:T(8,128)(2,1)}, u32[]{:S(2)}) copy-start(bf16[1024,768]{0,1:T(8,128)(2,1)} %copy-done.5) | copy-start | bytes 4718596
  201.9 10.4 %copy-start.9 = (f32[1024,768]{0,1:T(8,128)}, f32[1024,768]{0,1:T(8,128)S(1)}, u32[]{:S(2)}) copy-start(f32[1024,768]{0,1:T(8,128)S(1)} %get-tuple-element.206) | copy-start | bytes 9437188
  201.9 10.3 %copy-start.29 = (f32[1024]{0:T(1024)}, f32[1024]{0:T(1024)S(1)}, u32[]{:S(2)}) copy-start(f32[1024]{0:T(1024)S(1)} %broadcast_multiply_fusion.2) | copy-start | bytes 12292
  202.3 10.0 %copy-start.45 = (f32[1024]{0:T(1024)}, f32[1024]{0:T(1024)S(1)}, u32[]{:S(2)}) copy-start(f32[1024]{0:T(1024)S(1)} %multiply_reduce_fusion.8) | copy-start | bytes 12292
  204.0 8.3 %copy-start.33 = (f32[1024]{0:T(1024)}, f32[1024]{0:T(1024)S(1)}, u32[]{:S(2)}) copy-start(f32[1024]{0:T(1024)S(1)} %fusion.41) | copy-start | bytes 12292
  212.3 11.3 %copy-start.54 = (bf16[2,2,4,2,24,2432]{5,4,3,2,1,0:T(8,128)(2,1)S(1)}, bf16[2,2,4,2,24,2432]{5,4,3,2,1,0:T(8,128)(2,1)}, u32[]{:S(2)}) copy-start(bf16[2,2,4,2,24,2432]{5,4,3,2,1,0:T(8,128)(2,1)} %get-tuple-element.47) | copy-start | bytes 11206660
  223.2 32.0 %copy-start.11 = (f32[1024,768]{0,1:T(8,128)}, f32[1024,768]{0,1:T(8,128)S(1)}, u32[]{:S(2)}) copy-start(f32[1024,768]{0,1:T(8,128)S(1)} %get-tuple-element.208) | copy-start | bytes 9437188
  223.6 5.9 copy-start.47
  256.8 9.2 %copy-start.14 = (f32[1024,768]{0,1:T(8,128)}, f32[1024,768]{0,1:T(8,128)S(1)}, u32[]{:S(2)}) copy-start(f32[1024,768]{0,1:T(8,128)S(1)} %get-tuple-element.210) | copy-start | bytes 9437188
  256.8 9.2 %slice-start.6 = ((s8[4718592]{0:T(1024)(128)(4,1)}), s8[4194304]{0:T(1024)(128)(4,1)S(1)}, s32[]{:S(2)}) async-start(s8[4718592]{0:T(1024)(128)(4,1)} %bitcast.163), calls=%async_computation.6 | async-start | bytes 8388608
  257.6 8.5 %slice-start.7 = ((s8[4718592]{0:T(1024)(128)(4,1)}), s8[524288]{0:T(1024)(128)(4,1)S(1)}, s32[]{:S(2)}) async-start(s8[4718592]{0:T(1024)(128)(4,1)} %bitcast.163), calls=%async_computation.7 | async-start | bytes 1048576
  278.8 18.4 %copy-start.28 = (bf16[1024,768]{1,0:T(8,128)(2,1)S(1)}, bf16[1024,768]{1,0:T(8,128)(2,1)}, u32[]{:S(2)}) copy-start(bf16[1024,768]{1,0:T(8,128)(2,1)} %param.18) | copy-start | bytes 4718596
  297.2 14.6 %copy-start.58 = (bf16[1024,3072]{1,0:T(8,128)(2,1)}, bf16[1024,3072]{1,0:T(8,128)(2,1)S(1)}, u32[]{:S(2)}) copy-start(bf16[1024,3072]{1,0:T(8,128)(2,1)S(1)} %get-tuple-element.216) | copy-start | bytes 18874372
  328.7 9.9 %copy-start.24 = (f32[1024,768]{0,1:T(8,128)S(1)}, f32[1024,768]{0,1:T(8,128)}, u32[]{:S(2)}) copy-start(f32[1024,768]{0,1:T(8,128)} %copy.146) | copy-start | bytes 9437188
  487.6 35.2 %slice-start.2 = ((s8[4718592]{0:T(1024)(128)(4,1)}), s8[524288]{0:T(1024)(128)(4,1)S(1)}, s32[]{:S(2)}) async-start(s8[4718592]{0:T(1024)(128)(4,1)} %bitcast.132), calls=%async_computation.2 | async-start | bytes 1048576
  490.9 16.5 %copy-start.18 = (f32[1024,768]{0,1:T(8,128)S(1)}, f32[1024,768]{0,1:T(8,128)}, u32[]{:S(2)}) copy-start(f32[1024,768]{0,1:T(8,128)} %get-tuple-element.157) | copy-start | bytes 9437188
  490.9 31.9 %slice-start.3 = ((s8[4718592]{0:T(1024)(128)(4,1)}), s8[4194304]{0:T(1024)(128)(4,1)S(1)}, s32[]{:S(2)}) async-start(s8[4718592]{0:T(1024)(128)(4,1)} %bitcast.132), calls=%async_computation.3 | async-start | bytes 8388608
  507.4 15.4 %copy-start.59 = (bf16[1024,3072]{1,0:T(8,128)(2,1)}, bf16[1024,3072]{1,0:T(8,128)(2,1)S(1)}, u32[]{:S(2)}) copy-start(bf16[1024,3072]{1,0:T(8,128)(2,1)S(1)} %get-tuple-element.222) | copy-start | bytes 18874372
  537.4 10.2 %copy-start.46 = (f32[1024]{0:T(1024)S(1)}, f32[1024]{0:T(1024)}, u32[]{:S(2)}) copy-start(f32[1024]{0:T(1024)} %copy-done.45) | copy-start | bytes 12292
  537.4 10.2 %copy-start.25 = (f32[1024,768]{0,1:T(8,128)S(1)}, f32[1024,768]{0,1:T(8,128)}, u32[]{:S(2)}) copy-start(f32[1024,768]{0,1:T(8,128)} %copy.148) | copy-start | bytes 9437188
  585.1 5.6 copy-start.57
  614.8 88.3 %copy-start.49 = (pred[4]{0:T(512)(128)(4,1)S(1)}, pred[4]{0:T(512)(128)(4,1)}, u32[]{:S(2)}) copy-start(pred[4]{0:T(512)(128)(4,1)} %get-tuple-element.231) | copy-start | bytes 16
  614.8 88.3 %copy-start.50 = (pred[4]{0:T(512)(128)(4,1)S(1)}, pred[4]{0:T(512)(128)(4,1)}, u32[]{:S(2)}) copy-start(pred[4]{0:T(512)(128)(4,1)} %get-tuple-element.232) | copy-start | bytes 16
  (36 other events, 110.7 us)

commit v3 on v2

--- a/solution.py
+++ b/solution.py
@@ -23,7 +23,10 @@
     z=jnp.zeros_like(x)
     return jnp.where(lane<64,x,z), jnp.where(lane<64,z,x)
 
-def fwd_kernel(fl_ref,q_ref,k_ref,v_ref,o_ref,lse_ref,*,bq):
+def fwd_kernel(fl_ref,q_ref,k_ref,v_ref,*rest,bq,host):
+    n=host.count
+    o_ref,lse_ref=rest[n:n+2]
+    jobs=host.enter(rest[:n],rest[n+2:2*n+2],rest[2*n+2:])
     L=q_ref.shape[0]; half=L//2
     second=fl_ref[pl.program_id(0)]<L
     shut=jnp.where(second,F32(1e9),F32(0.))
@@ -59,22 +62,28 @@
             acc=acc+oh*(1.0/l)
             lse_ref[0,h:h+1,lo:hi]=m+jnp.log(l)
         o_ref[lo:hi,:]=acc.T.astype(BF)
-
-def attend_fwd(qkv,fl,bq=256):
+    host.leave(jobs)
+
+def attend_fwd(qkv,fl,host,bq=256):
     N,C=qkv.shape; R=fl.shape[0]; L=N//R; D=C//3; G=D//128
-    return pl.pallas_call(functools.partial(fwd_kernel,bq=bq),
+    return pl.pallas_call(functools.partial(fwd_kernel,bq=bq,host=host),
         grid_spec=pltpu.PrefetchScalarGridSpec(num_scalar_prefetch=1,grid=(R,G),
           in_specs=[pl.BlockSpec((L,128),lambda r,g,fl:(r,g)),
                     pl.BlockSpec((L,128),lambda r,g,fl:(r,G+g)),
-                    pl.BlockSpec((L,128),lambda r,g,fl:(r,2*G+g))],
+                    pl.BlockSpec((L,128),lambda r,g,fl:(r,2*G+g))]+host.ins,
           out_specs=[pl.BlockSpec((L,128),lambda r,g,fl:(r,g)),
-                     pl.BlockSpec((1,2,L),lambda r,g,fl:(r*G+g,0,0))]),
-        out_shape=[jax.ShapeDtypeStruct((N,D),BF),jax.ShapeDtypeStruct((R*G,2,L),F32)],
-        compiler_params=pltpu.CompilerParams(vmem_limit_bytes=48<<20),
+                     pl.BlockSpec((1,2,L),lambda r,g,fl:(r*G+g,0,0))]+host.outs,
+          scratch_shapes=host.scratch),
+        out_shape=[jax.ShapeDtypeStruct((N,D),BF),jax.ShapeDtypeStruct((R*G,2,L),F32)]+host.shapes,
+        compiler_params=host.params(),
         cost_estimate=pl.CostEstimate(flops=2*2*R*L*L*D*2,bytes_accessed=N*D*8,transcendentals=R*L*L*12//2),
-        name="attend_fwd")(fl,qkv,qkv,qkv)
-
-def bwd_kernel(fl_ref,q_ref,k_ref,v_ref,do_ref,lse_ref,dq_ref,dk_ref,dv_ref,dk_acc,dv_acc,*,bq):
+        name="attend_fwd")(fl,qkv,qkv,qkv,*host.arrays)
+
+def bwd_kernel(fl_ref,q_ref,k_ref,v_ref,do_ref,lse_ref,*rest,bq,host):
+    n=host.count
+    dq_ref,dk_ref,dv_ref=rest[n:n+3]
+    dk_acc,dv_acc=rest[2*n+3:2*n+5]
+    jobs=host.enter(rest[:n],rest[n+3:2*n+3],rest[2*n+5:])
     L=q_ref.shape[0]; half=L//2
     second=fl_ref[pl.program_id(0)]<L
     shut=jnp.where(second,F32(1e9),F32(0.))
@@ -118,19 +127,20 @@
             dk_acc[:hi]+=dkp; dv_acc[:hi]+=dvp
         dq_ref[lo:hi,:]=(dqT.T*0.125).astype(BF)
     dk_ref[...]=dk_acc[...].astype(BF); dv_ref[...]=dv_acc[...].astype(BF)
-
-def attend_bwd(qkv,do,lse,fl,bq=256):
+    host.leave(jobs)
+
+def attend_bwd(qkv,do,lse,fl,host,bq=256):
     N,C=qkv.shape; R=fl.shape[0]; L=N//R; D=C//3; G=D//128
     blk=lambda off: pl.BlockSpec((L,128),lambda r,g,fl:(r,off*G+g))
-    return pl.pallas_call(functools.partial(bwd_kernel,bq=bq),
+    return pl.pallas_call(functools.partial(bwd_kernel,bq=bq,host=host),
         grid_spec=pltpu.PrefetchScalarGridSpec(num_scalar_prefetch=1,grid=(R,G),
-          in_specs=[blk(0),blk(1),blk(2),blk(0),pl.BlockSpec((1,2,L),lambda r,g,fl:(r*G+g,0,0))],
-          out_specs=[blk(0),blk(0),blk(0)],
-          scratch_shapes=[pltpu.VMEM((L,128),F32),pltpu.VMEM((L,128),F32)]),
-        out_shape=[jax.ShapeDtypeStruct((N,D),BF)]*3,
-        compiler_params=pltpu.CompilerParams(vmem_limit_bytes=48<<20),
+          in_specs=[blk(0),blk(1),blk(2),blk(0),pl.BlockSpec((1,2,L),lambda r,g,fl:(r*G+g,0,0))]+host.ins,
+          out_specs=[blk(0),blk(0),blk(0)]+host.outs,
+          scratch_shapes=[pltpu.VMEM((L,128),F32),pltpu.VMEM((L,128),F32)]+host.scratch),
+        out_shape=[jax.ShapeDtypeStruct((N,D),BF)]*3+host.shapes,
+        compiler_params=host.params(),
         cost_estimate=pl.CostEstimate(flops=5*2*R*L*L*D*2,bytes_accessed=N*D*16,transcendentals=R*L*L*12//2),
-        name="attend_bwd")(fl,qkv,qkv,qkv,do,lse)
+        name="attend_bwd")(fl,qkv,qkv,qkv,do,lse,*host.arrays)
 
 
 MESH = pl.DeviceIdType.MESH
@@ -326,38 +336,83 @@
     return [(i, t - i) for t in range(count + steps - 1) for i in range(count) if 0 <= t - i < steps]
 
 
-def comm_kernel(*refs, kind, n):
-    me, jobs = host_build(kind, refs[:n], refs[n : 2 * n], refs[2 * n :])
-    me.greet()
-    for i in range(n):
-        jobs[i].run(0)
-    for i, t in in_order(n, kind.STEPS):
-        if t > 0:
-            jobs[i].run(t)
+class Host:
+    def __init__(self, kind=None, arrays=(), ident=None, plan=None, axis=1):
+        self.kind, self.ident, self.plan, self.axis = kind, ident, plan, axis
+        self.used = bool(arrays) and block_mesh()
+        self.source = list(arrays)
+        self.arrays, self.ins, self.outs, self.shapes, self.scratch = [], [], [], [], []
+        if self.used:
+            if kind is Scatter:
+                arrays = [a.reshape(2, 2, 4, 2, -1, a.shape[-1]) for a in arrays]
+            self.arrays = list(arrays)
+            self.ins, self.outs, self.shapes, self.scratch = host_specs(kind, self.arrays)
+        self.count = len(self.arrays)
+
+    def params(self):
+        if not self.used:
+            return pltpu.CompilerParams(vmem_limit_bytes=48 << 20)
+        return pltpu.CompilerParams(
+            collective_id=self.ident, has_side_effects=True, vmem_limit_bytes=56 << 20)
+
+    def enter(self, ins, outs, scratch):
+        if not self.used:
+            return None
+        me, jobs = host_build(self.kind, ins, outs, scratch)
+        now = pl.program_id(self.axis)
+
+        @pl.when(now == 0)
+        def _():
+            me.greet()
+            for job in jobs:
+                job.run(0)
+
+        for g, todo in enumerate(self.plan[:-1]):
+            if todo:
+                @pl.when(now == g)
+                def _():
+                    for i, t in todo:
+                        jobs[i].run(t)
+
+        return jobs
+
+    def leave(self, jobs):
+        if not self.used:
+            return
+        @pl.when(pl.program_id(self.axis) == len(self.plan) - 2)
+        def _():
+            for i, t in self.plan[-1]:
+                jobs[i].run(t)
+
+    def results(self, values):
+        if self.used and self.kind is Gather:
+            return [w.reshape(-1, w.shape[-1]) for w in values]
+        if self.used:
+            return list(values)
+        return plain(self.kind, self.source)
+
+
+def plain(kind, arrays):
+    if kind is Gather:
+        return [lax.all_gather(a, AX, axis=0, tiled=True) for a in arrays]
+    return [lax.psum_scatter(t.astype(F32), AX, scatter_dimension=0, tiled=True) for t in arrays]
+
+
+def alone_kernel(*refs, host):
+    n = host.count
+    jobs = host.enter(refs[:n], refs[n : 2 * n], refs[2 * n :])
+    host.leave(jobs)
 
 
 def exchange(kind, arrays, ident, name):
-    n = len(arrays)
-    ins, outs, shapes, scratch = host_specs(kind, arrays)
-    return pl.pallas_call(
-        functools.partial(comm_kernel, kind=kind, n=n),
-        in_specs=ins, out_specs=outs, out_shape=shapes, scratch_shapes=scratch,
-        compiler_params=pltpu.CompilerParams(
-            collective_id=ident, has_side_effects=True, vmem_limit_bytes=48 << 20),
-        name=name)(*arrays)
-
-
-def gather_all(shards, ident):
-    if not block_mesh():
-        return [lax.all_gather(a, AX, axis=0, tiled=True) for a in shards]
-    wide = exchange(Gather, shards, ident, "gather")
-    return [w.reshape(-1, w.shape[-1]) for w in wide]
-
-
-def scatter_all(terms, ident):
-    if not block_mesh():
-        return [lax.psum_scatter(t.astype(F32), AX, scatter_dimension=0, tiled=True) for t in terms]
-    return exchange(Scatter, [t.reshape(2, 2, 4, 2, -1, t.shape[-1]) for t in terms], ident, "scatter")
+    steps = [e for e in in_order(len(arrays), kind.STEPS) if e[1] > 0]
+    host = Host(kind, arrays, ident, [[], steps], axis=0)
+    if not host.used:
+        return plain(kind, arrays)
+    return host.results(pl.pallas_call(
+        functools.partial(alone_kernel, host=host), grid=(1,),
+        in_specs=host.ins, out_specs=host.outs, out_shape=host.shapes, scratch_shapes=host.scratch,
+        compiler_params=host.params(), name=name)(*host.arrays))
 
 
 def layer_norm(values, gain, shift):
@@ -408,28 +463,29 @@
     return [jnp.concatenate([hw, small], axis=1), mw, ew, sw]
 
 
-def as_weights(whole, width, ways):
-    heads, mix, expand, shrink = whole
+def use_heads(heads, width, ways):
     vecs, wide = unpack_columns(heads[:, 3 * width :], 8, ways, lax.axis_size(AX))
     vecs = [v.astype(F32) for v in vecs]
     return dict(zip(("ga", "sa", "qb", "vb", "mb", "gf", "sf", "sb"), vecs), eb=wide.astype(F32),
-                heads=heads[:, : 3 * width], mix=mix, expand=expand, shrink=shrink)
-
-
-def forward_use(hidden, w, first_len):
+                heads=heads[:, : 3 * width])
+
+
+def forward_use(hidden, w, first_len, host):
     normed = layer_norm(hidden, w["ga"], w["sa"]).astype(BF)
     bias = jnp.concatenate([w["qb"], jnp.zeros_like(w["qb"]), w["vb"]])
     qkv = (jnp.dot(normed, w["heads"], preferred_element_type=F32) + bias).astype(BF)
-    attended, lse = attend_fwd(qkv, first_len)
+    attended, lse, *more = attend_fwd(qkv, first_len, host)
+    more = host.results(more)
+    w.update(zip(("mix", "expand", "shrink"), more))
     middle = hidden + jnp.dot(attended, w["mix"], preferred_element_type=F32) + w["mb"]
     normed_two = layer_norm(middle, w["gf"], w["sf"]).astype(BF)
     expanded = jnp.dot(normed_two, w["expand"], preferred_element_type=F32) + w["eb"]
     activated, slope = gelu_pair(expanded)
     result = middle + jnp.dot(activated, w["shrink"], preferred_element_type=F32) + w["sb"]
-    return result, (hidden, normed, qkv, attended, lse, middle, normed_two, activated, slope)
-
-
-def backward_use(grad_out, kept, w, first_len):
+    return result, (hidden, normed, qkv, attended, lse, middle, normed_two, activated, slope), more[3:]
+
+
+def backward_use(grad_out, kept, w, first_len, carried, ident, plan):
     hidden, normed, qkv, attended, lse, middle, normed_two, activated, slope = kept
     count = lax.axis_size(AX)
     grad_low = grad_out.astype(BF)
@@ -446,7 +502,9 @@
     mix_term = inner_rows(attended, dmb).astype(BF)
     mb = column_sums(dmb)
     do = times_transposed(dmb, w["mix"]).astype(BF)
-    dq, dk, dv = attend_bwd(qkv, do, lse, first_len)
+    host = Host(Scatter, [shrink_term, expand_term, mix_term] + carried, ident, plan)
+    dq, dk, dv, *more = attend_bwd(qkv, do, lse, first_len, host)
+    more = host.results(more)
     dqkv = jnp.concatenate([dq, dk, dv], axis=1)
     heads_term = inner_rows(normed, dqkv).astype(BF)
     qb = column_sums(dq)
@@ -455,13 +513,27 @@
     unused, first_back = jax.vjp(layer_norm, hidden, w["ga"], w["sa"])
     hidden_norm, ga, sa = first_back(da)
     small = pack_columns([ga, sa, qb, vb, mb, gf, sf, sb], eb, count)
-    return dm + hidden_norm, (shrink_term, expand_term, mix_term, heads_term), small
+    return dm + hidden_norm, more, heads_term, small
 
 
 def as_shares(shrink, expand, mix, heads, small):
     vecs, wide = unpack_columns(small, 8, shrink.shape[0] // heads.shape[0], 1)
     ga, sa, qb, vb, mb, gf, sf, sb = vecs
     return ga, sa, heads, qb, vb, mix, mb, gf, sf, expand, wide, shrink, sb
+
+
+FORWARD_PLANS = (
+    [[], [(0, 1)], [(0, 2)], [(0, 3)], [(1, 1)], [(1, 2), (0, 4)],
+     [(2, 1), (1, 3), (3, 1), (2, 2), (3, 2), (2, 3), (3, 3), (1, 4), (2, 4), (3, 4)]],
+    [[], [(0, 1)], [(0, 2)], [(0, 3)], [(1, 1)], [(1, 2), (0, 4)],
+     [(2, 1), (1, 3), (2, 2), (2, 3), (1, 4), (2, 4)]],
+)
+BACKWARD_PLANS = (
+    [[], [(0, 1)], [(1, 1)], [(2, 1)], [(0, 2)], [(1, 2)],
+     [(0, 3), (2, 2), (1, 3), (2, 3), (0, 4), (1, 4), (2, 4)]],
+    [[], [(0, 1)], [(1, 1)], [(3, 1), (2, 1)], [(0, 2)], [(1, 2)],
+     [(0, 3), (3, 2), (2, 2), (1, 3), (3, 3), (2, 3), (0, 4), (1, 4), (3, 4), (2, 4)]],
+)
 
 
 def pick_shards(stacks, source):
@@ -486,19 +558,24 @@
     sources = [tie_map[i] for i in range(LAYERS)]
     shards = [local_shards(pick_shards(stacks, s)) for s in sources]
     ways = shards[0][3].shape[0] // shards[0][0].shape[0]
-    whole = gather_all(shards[0] + shards[1], 0)
-    weights = [as_weights(whole[4 * i : 4 * i + 4], width, ways) for i in range(LAYERS)]
-    kept = []
+    (heads,) = exchange(Gather, shards[0][:1], 0, "gather")
+    kept, weights = [], []
+    loads = [shards[0][1:] + shards[1][:1], shards[1][1:]]
     for i in range(LAYERS):
-        hidden, saved = forward_use(hidden, weights[i], first_length)
+        weights.append(use_heads(heads, width, ways))
+        host = Host(Gather, loads[i], 1 + i, FORWARD_PLANS[i])
+        hidden, saved, spare = forward_use(hidden, weights[i], first_length, host)
+        heads = spare[0] if spare else None
         kept.append(saved)
     grad = cotangent.astype(F32)
-    terms, small = [None] * LAYERS, [None] * LAYERS
-    for i in reversed(range(LAYERS)):
-        grad, terms[i], small[i] = backward_use(grad, kept[i], weights[i], first_length)
-    late = scatter_all(list(terms[1]), 1)
-    early = scatter_all(list(terms[0]) + [jnp.concatenate(small, axis=1)], 2)
-    shares = [as_shares(*early[:4], early[4][:, :LANES]), as_shares(*late, early[4][:, LANES:])]
+    grad, late, heads_late, small_late = backward_use(
+        grad, kept[1], weights[1], first_length, [], 3, BACKWARD_PLANS[0])
+    grad, early, heads_early, small_early = backward_use(
+        grad, kept[0], weights[0], first_length, [heads_late], 4, BACKWARD_PLANS[1])
+    heads_early, small = exchange(
+        Scatter, [heads_early, jnp.concatenate([small_early, small_late], axis=1)], 5, "scatter")
+    shares = [as_shares(*early[:3], heads_early, small[:, :LANES]),
+              as_shares(*late, early[3], small[:, LANES:])]
     return (hidden.astype(BF), grad.astype(BF), *place_terms(sources, shares))
 
 

time: 719 us -> 714 us (level)
  Pallas kernels: 423 us -> 406 us
  matrix products: 186 us -> 196 us
    pallas_call x7 -> x6, Pallas kernels: 423 us -> 406 us  [the longest x2 179 us: attend_bwd(): pl.pallas_call(functools.partial(bwd_kernel, bq=bq, host=host), grid_spec...]
    unnamed x146 -> x164, local copies, waits for them, and re-layouts: 23.6 us -> 21.2 us
where the time goes in v3:
time: 714 us; the launch traced here: 705 us
  Pallas kernels  406 us (57%)
  matrix products  196 us (27%)
  local copies, waits for them, and re-layouts  55.1 us (8%)
  other arithmetic  40.8 us (6%)
    pallas_call x2, Pallas kernels, attend_bwd(): pl.pallas_call(functools.partial(bwd_kernel, bq=bq, host=host), grid_spec...  179 us
    pallas_call x2, Pallas kernels, attend_fwd(): pl.pallas_call(functools.partial(fwd_kernel, bq=bq, host=host), grid_spec...  153 us
    pallas_call x2, Pallas kernels, exchange(): pl.pallas_call(functools.partial(alone_kernel, host=host), grid=(1,), in_...  74.6 us
    dot_general x8, matrix products, times_transposed(): lax.dot_general(left, right, (((1,), (1,)), ((), ())), preferred_element_...  69.3 us
    dot_general x8, matrix products, inner_rows(): lax.dot_general(left, right, (((0,), (0,)), ((), ())), preferred_element_...  63.5 us
    dot_general x2, matrix products, forward_use(): jnp.dot(activated, w['shrink'], preferred_element_type=F32)  22.6 us
    unnamed x164, local copies, waits for them, and re-layouts  21.2 us
    dot_general x2, matrix products, forward_use(): jnp.dot(normed_two, w['expand'], preferred_element_type=F32) + w['eb']  20.3 us

profile of v3, /device:TPU:0, one launch (start us, length us, event | category | flops | bytes accessed | tf_op | source)
XLA Modules:
  0.0 705.3 jit_solution(11336093784396657284)
XLA Ops:
  26.0 36.3 %gather.1 = bf16[2,2,4,2,24,2432]{5,4,3,2,1,0:T(8,128)(2,1)} custom-call(bf16[24,2432]{1,0:T(8,128)(2,1)} %fusion.36.refs_0_), custom_call_target="tpu_custom_call" | custom-call | tf_op jit(solution)/shard_map/gather/pallas_call | solution.py:412
  63.8 7.8 %add_convert_fusion.1.q_ref.k_ref.v_ref = bf16[1024,2304]{1,0:T(8,128)(2,1)} fusion(f32[2304]{0:T(1024)S(1)} %fusion.38, bf16[768,2432]{1,0:T(8,128)(2,1)} %bitcast.128, bf16[1024,768]{0,1:T(8,128)(2,1)S(1)} %copy.120, f32[768]{0:T(1024)S(1)} %get-tuple-element.134, f32[768]{0:T(1024)S(1)} %get-tuple-element.135, f32[1024]{0:T(1024)S(1)} %fusion.40, ...), kind=kOutput, calls=%fused_computation.24 | convolution fusion | flops 3633315840 | bytes 9853952 | tf_op jit(solution)/shard_map/dot_general | solution.py:476
  71.6 82.0 %attend_fwd.2 = (bf16[1024,768]{1,0:T(8,128)(2,1)}, f32[6,2,1024]{2,1,0:T(2,128)}, bf16[2,2,4,2,24,768]{5,4,3,2,1,0:T(8,128)(2,1)}, bf16[2,2,4,2,24,3072]{5,4,3,...) custom-call(s32[1]{0:T(128)S(6)} %copy.169.fl_ref, ...), custom_call_target="tpu_custom_call" | custom-call | flops 6442450944 | bytes 6291456 | tf_op jit(solution)/shard_map/attend_fwd/pallas_call | solution.py:69
  155.0 3.4 fusion.90
  159.9 11.7 %fusion.83 = f32[1024,3072]{1,0:T(8,128)} fusion(bf16[768,3072]{1,0:T(8,128)(2,1)} %bitcast.121, f32[1024,768]{0,1:T(8,128)S(1)} %get-tuple-element.202, f32[768]{0:T(1024)S(1)} %get-tuple-element.130, f32[768]{0:T(1024)S(1)} %get-tuple-element.128, f32[1024]{0:T(1024)S(1)} %fusion.41, f32[1024]{0:T(1024)S(1)} %broadcast_multiply_fusion.2), kind=kOutput, calls=%fused_computation.242 | convolution fusion | flops 4835770368 | bytes 20461568 | tf_op jit(solution)/shard_map/dot_general | solution.py:482
  171.6 12.4 %fusion.91 = (f32[1024]{0:T(1024)S(1)}, f32[1024,768]{0,1:T(8,128)S(1)}) fusion(f32[768]{0:T(1024)S(1)} %get-tuple-element.129, f32[1024,768]{0,1:T(8,128)S(1)} %get-tuple-element.202, bf16[3072,768]{1,0:T(8,128)(2,1)S(1)} %bitcast.148, f32[1024,3072]{1,0:T(8,128)} %fusion.83, f32[3072]{0:T(1024)S(1)} %reshape.367), kind=kOutput, calls=%fused_computation.248 | convolution fusion | flops 4865653760 | bytes 23612416 | tf_op jit(solution)/shard_map/dot_general | solution.py:484
  184.5 5.9 add_convert_fusion.q_ref.k_ref.v_ref
  190.4 70.9 %attend_fwd.3 = (bf16[1024,768]{1,0:T(8,128)(2,1)}, f32[6,2,1024]{2,1,0:T(2,128)}, bf16[2,2,4,2,24,768]{5,4,3,2,1,0:T(8,128)(2,1)}, bf16[2,2,4,2,24,3072]{5,4,3,...) custom-call(s32[1]{0:T(128)S(6)} %copy.169.fl_ref, bf16[1024,2304]{1,0:T(8,128)(2,1)} %add_convert_fusion.q_ref.k_ref.v_ref, ...), custom_call_target="tpu_custom_call" | custom-call | flops 6442450944 | bytes 6291456 | tf_op jit(solution)/shard_map/attend_fwd/pallas_call | solution.py:69
  261.2 3.5 fusion.92
  265.2 8.6 %fusion.84 = f32[1024,3072]{1,0:T(8,128)} fusion(bf16[768,3072]{1,0:T(8,128)(2,1)S(1)} %bitcast.126, f32[1024,768]{0,1:T(8,128)S(1)} %get-tuple-element.206, f32[768]{0:T(1024)S(1)} %get-tuple-element.122, f32[768]{0:T(1024)S(1)} %get-tuple-element.120, f32[1024]{0:T(1024)S(1)} %fusion.43, f32[1024]{0:T(1024)S(1)} %broadcast_multiply_fusion), kind=kOutput, calls=%fused_computation.243 | convolution fusion | flops 4835770368 | bytes 20461568 | tf_op jit(solution)/shard_map/dot_general | solution.py:482
  273.8 10.2 %add_convert_fusion.3 = bf16[1024,768]{0,1:T(8,128)(2,1)} fusion(f32[1024,768]{0,1:T(8,128)S(1)} %get-tuple-element.206, bf16[3072,768]{1,0:T(8,128)(2,1)S(1)} %bitcast.156, f32[768]{0:T(1024)S(1)} %get-tuple-element.121, f32[1024,3072]{1,0:T(8,128)} %fusion.84, f32[3072]{0:T(1024)S(1)} %reshape.376), kind=kOutput, calls=%fused_computation.68 | convolution fusion | flops 4865654784 | bytes 22035456 | tf_op jit(solution)/shard_map/dot_general | solution.py:484
  286.6 18.3 %convert_reduce_fusion = (f32[3072]{0:T(1024)S(1)}, bf16[1024,3072]{1,0:T(8,128)(2,1)S(1)}) fusion(f32[1024,3072]{1,0:T(8,128)} %fusion.84, f32[3072]{0:T(1024)S(1)} %reshape.376, bf16[3072,768]{1,0:T(8,128)(2,1)} %bitcast.153, bf16[1024,768]{1,0:T(8,128)(2,1)} %param.18), kind=kOutput, calls=%fused_computation.18 | convolution fusion | flops 4907332608 | bytes 25190400 | tf_op jit(solution)/shard_map/dot_general | solution.py:429
  304.9 14.7 %convolution_convert_fusion.3 = bf16[3072,768]{1,0:T(8,128)(2,1)} fusion(bf16[1024,768]{1,0:T(8,128)(2,1)S(1)} %copy-done.26, f32[1024,3072]{1,0:T(8,128)} %fusion.84, f32[3072]{0:T(1024)S(1)} %reshape.376), kind=kOutput, calls=%fused_computation.28 | convolution fusion | flops 4865654784 | bytes 18886656 | tf_op jit(solution)/shard_map/dot_general | solution.py:425
  319.6 9.1 %fusion.94 = (f32[768]{0:T(1024)S(1)}, f32[1024,768]{1,0:T(8,128)}) fusion(bf16[1024,3072]{1,0:T(8,128)(2,1)S(1)} %get-tuple-element.212, bf16[768,3072]{1,0:T(8,128)(2,1)} %bitcast.123), kind=kOutput, calls=%fused_computation.251 | convolution fusion | flops 4832623616 | bytes 14158848 | tf_op jit(solution)/shard_map/dot_general | solution.py:429
  328.9 3.5 copy.146
  332.4 3.9 multiply_reduce_fusion
  336.4 9.9 %convolution_convert_fusion.2 = bf16[768,3072]{1,0:T(8,128)(2,1)} fusion(bf16[1024,3072]{1,0:T(8,128)(2,1)} %copy-done.68, f32[1024,768]{0,1:T(8,128)S(1)} %copy-done.5, f32[768]{0:T(1024)S(1)} %get-tuple-element.122, f32[768]{0:T(1024)S(1)} %get-tuple-element.120, f32[1024]{0:T(1024)S(1)} %fusion.43, f32[1024]{0:T(1024)S(1)} %broadcast_multiply_fusion), kind=kOutput, calls=%fused_computation.27 | convolution fusion | flops 4838129664 | bytes 14170112 | tf_op jit(solution)/shard_map/dot_general | solution.py:425
  354.7 83.5 %attend_bwd.2 = (bf16[1024,768]{1,0:T(8,128)(2,1)}, bf16[1024,768]{1,0:T(8,128)(2,1)}, bf16[1024,768]{1,0:T(8,128)(2,1)}, f32[96,768]{1,0:T(8,128)}, f32[24,3072]{1,0:T(8,128)}, /*index=5*/f32[24,768]{1,0:T(8,128)}) custom-call(s32[1]{0:T(128)S(6)} %copy.169.fl_ref, bf16[1024,2304]{1,0:T(8,128)(2,1)} %add_convert_fusion.q_ref.k_ref.v_ref, ...), custom_call_target="tpu_custom_call" | custom-call | flops 16106127360 | bytes 12582912 | tf_op jit(solution)/shard_map/attend_bwd/pallas_call | solution.py:135
  444.3 5.5 fusion.93
  449.8 5.6 convolution_convert_fusion.5
  455.4 3.9 copy.147
  464.5 3.3 convert_reduce_fusion.7
  467.9 16.5 %convert_reduce_fusion.1 = (f32[3072]{0:T(1024)S(1)}, bf16[1024,3072]{1,0:T(8,128)(2,1)S(1)}) fusion(f32[1024,3072]{1,0:T(8,128)} %fusion.83, f32[3072]{0:T(1024)S(1)} %copy-done.59, bf16[3072,768]{1,0:T(8,128)(2,1)} %bitcast.145, f32[1024,768]{0,1:T(8,128)} %get-tuple-element.155), kind=kOutput, calls=%fused_computation.19 | convolution fusion | flops 4908119040 | bytes 26763264 | tf_op jit(solution)/shard_map/dot_general | solution.py:429
  484.4 15.4 %convolution_convert_fusion.1 = bf16[3072,768]{1,0:T(8,128)(2,1)} fusion(f32[1024,768]{0,1:T(8,128)S(1)} %copy-done.8, f32[1024,3072]{1,0:T(8,128)} %fusion.83, f32[3072]{0:T(1024)S(1)} %copy-done.59), kind=kOutput, calls=%fused_computation.26 | convolution fusion | flops 4866441216 | bytes 20459520 | tf_op jit(solution)/shard_map/dot_general | solution.py:425
  499.8 9.2 %fusion.96 = (f32[768]{0:T(1024)S(1)}, f32[1024,768]{1,0:T(8,128)}) fusion(bf16[1024,3072]{1,0:T(8,128)(2,1)S(1)} %get-tuple-element.218, bf16[768,3072]{1,0:T(8,128)(2,1)} %bitcast.122), kind=kOutput, calls=%fused_computation.253 | convolution fusion | flops 4832623616 | bytes 14158848 | tf_op jit(solution)/shard_map/dot_general | solution.py:429
  509.2 3.7 copy.148
  516.6 7.3 %convolution_convert_fusion = bf16[768,3072]{1,0:T(8,128)(2,1)} fusion(bf16[1024,3072]{1,0:T(8,128)(2,1)S(1)} %copy-done.70, f32[1024,768]{0,1:T(8,128)S(1)} %copy-done.3, f32[768]{0:T(1024)S(1)} %copy-done.36, f32[768]{0:T(1024)S(1)} %copy-done.32, f32[1024]{0:T(1024)S(1)} %copy-done.34, f32[1024]{0:T(1024)S(1)} %copy-done.30), kind=kOutput, calls=%fused_computation.25 | convolution fusion | flops 4838129664 | bytes 14170112 | tf_op jit(solution)/shard_map/dot_general | solution.py:425
  532.5 95.3 %attend_bwd.3 = (bf16[1024,768]{1,0:T(8,128)(2,1)}, bf16[1024,768]{1,0:T(8,128)(2,1)}, bf16[1024,768]{1,0:T(8,128)(2,1)}, f32[96,768]{1,0:T(8,128)}, f32[24,3072...) custom-call(s32[1]{0:T(128)S(6)} %copy.169.fl_ref, bf16[1024,2304]{1,0:T(8,128)(2,1)} %add_convert_fusion.1.q_ref.k_ref.v_ref, ...), custom_call_target="tpu_custom_call" | custom-call | flops 16106127360 | bytes 12582912 | tf_op jit(solution)/shard_map/attend_bwd/pallas_call | solution.py:135
  637.4 5.5 fusion.95
  642.9 5.7 convolution_convert_fusion.4
  648.6 3.5 copy.149
  661.4 38.3 %scatter.1 = (f32[24,2304]{1,0:T(8,128)}, f32[24,256]{1,0:T(8,128)}) custom-call(bf16[2,2,4,2,24,2304]{5,4,3,2,1,0:T(8,128)(2,1)} %bitcast.130, f32[2,2,4,2,24,256]{5,4,3,2,1,0:T(8,128)} %bitcast.131), custom_call_target="tpu_custom_call" | custom-call | tf_op jit(solution)/shard_map/scatter/pallas_call | solution.py:412
  (299 shorter events, 84.3 us)
Async XLA Ops:
  0.6 20.9 %copy-start.24 = (bf16[1024,768]{1,0:T(8,128)(2,1)S(1)}, bf16[1024,768]{1,0:T(8,128)(2,1)}, u32[]{:S(2)}) copy-start(bf16[1024,768]{1,0:T(8,128)(2,1)} %param.17) | copy-start | bytes 4718596
  22.3 132.7 %copy-start = (bf16[1024,768]{0,1:T(8,128)(2,1)}, bf16[1024,768]{0,1:T(8,128)(2,1)S(1)}, u32[]{:S(2)}) copy-start(bf16[1024,768]{0,1:T(8,128)(2,1)S(1)} %copy.120) | copy-start | bytes 4718596
  22.6 41.2 %copy-start.42 = (f32[1024]{0:T(1024)}, f32[1024]{0:T(1024)S(1)}, u32[]{:S(2)}) copy-start(f32[1024]{0:T(1024)S(1)} %broadcast_multiply_fusion.3) | copy-start | bytes 12292
  24.3 39.5 %copy-start.48 = (f32[1024]{0:T(1024)}, f32[1024]{0:T(1024)S(1)}, u32[]{:S(2)}) copy-start(f32[1024]{0:T(1024)S(1)} %fusion.40) | copy-start | bytes 12292
  63.5 8.1 %copy-start.46 = (f32[768]{0:T(1024)}, f32[768]{0:T(1024)S(1)}, u32[]{:S(2)}) copy-start(f32[768]{0:T(1024)S(1)} %get-tuple-element.135) | copy-start | bytes 9220
  63.5 8.1 %copy-start.62 = (f32[768]{0:T(1024)}, f32[768]{0:T(1024)S(1)}, u32[]{:S(2)}) copy-start(f32[768]{0:T(1024)S(1)} %get-tuple-element.134) | copy-start | bytes 9220
  63.5 95.4 %copy-start.31 = (f32[768]{0:T(1024)}, f32[768]{0:T(1024)S(1)}, u32[]{:S(2)}) copy-start(f32[768]{0:T(1024)S(1)} %get-tuple-element.128) | copy-start | bytes 9220
  63.5 95.4 %copy-start.35 = (f32[768]{0:T(1024)}, f32[768]{0:T(1024)S(1)}, u32[]{:S(2)}) copy-start(f32[768]{0:T(1024)S(1)} %get-tuple-element.130) | copy-start | bytes 9220
  63.8 107.7 %copy-start.58 = (f32[3072]{0:T(1024)}, f32[3072]{0:T(1024)S(1)}, u32[]{:S(2)}) copy-start(f32[3072]{0:T(1024)S(1)} %reshape.367) | copy-start | bytes 36868
  158.4 13.1 %copy-start.2 = (f32[1024,768]{0,1:T(8,128)}, f32[1024,768]{0,1:T(8,128)S(1)}, u32[]{:S(2)}) copy-start(f32[1024,768]{0,1:T(8,128)S(1)} %get-tuple-element.202) | copy-start | bytes 9437188
  158.5 13.1 %slice-start.2 = ((s8[4718592]{0:T(1024)(128)(4,1)}), s8[4194304]{0:T(1024)(128)(4,1)S(1)}, s32[]{:S(2)}) async-start(s8[4718592]{0:T(1024)(128)(4,1)} %bitcast.146), calls=%async_computation.2 | async-start | bytes 8388608
  158.9 12.7 %copy-start.52 = (f32[1024]{0:T(1024)}, f32[1024]{0:T(1024)S(1)}, u32[]{:S(2)}) copy-start(f32[1024]{0:T(1024)S(1)} %multiply_reduce_fusion.8) | copy-start | bytes 12292
  159.9 11.7 %slice-start.3 = ((s8[4718592]{0:T(1024)(128)(4,1)}), s8[524288]{0:T(1024)(128)(4,1)S(1)}, s32[]{:S(2)}) async-start(s8[4718592]{0:T(1024)(128)(4,1)} %bitcast.146), calls=%async_computation.3 | async-start | bytes 1048576
  171.6 12.9 %copy-start.60 = (bf16[2,2,4,2,24,2432]{5,4,3,2,1,0:T(8,128)(2,1)S(1)}, bf16[2,2,4,2,24,2432]{5,4,3,2,1,0:T(8,128)(2,1)}, u32[]{:S(2)}) copy-start(bf16[2,2,4,2,24,2432]{5,4,3,2,1,0:T(8,128)(2,1)} %get-tuple-element.45) | copy-start | bytes 11206660
  184.4 5.9 copy-start.54
  264.7 9.1 %copy-start.4 = (f32[1024,768]{0,1:T(8,128)}, f32[1024,768]{0,1:T(8,128)S(1)}, u32[]{:S(2)}) copy-start(f32[1024,768]{0,1:T(8,128)S(1)} %get-tuple-element.206) | copy-start | bytes 9437188
  264.8 9.0 %slice-start.4 = ((s8[4718592]{0:T(1024)(128)(4,1)}), s8[4194304]{0:T(1024)(128)(4,1)S(1)}, s32[]{:S(2)}) async-start(s8[4718592]{0:T(1024)(128)(4,1)} %bitcast.154), calls=%async_computation.4 | async-start | bytes 8388608
  265.2 8.6 %slice-start.5 = ((s8[4718592]{0:T(1024)(128)(4,1)}), s8[524288]{0:T(1024)(128)(4,1)S(1)}, s32[]{:S(2)}) async-start(s8[4718592]{0:T(1024)(128)(4,1)} %bitcast.154), calls=%async_computation.5 | async-start | bytes 1048576
  286.6 18.3 %copy-start.26 = (bf16[1024,768]{1,0:T(8,128)(2,1)S(1)}, bf16[1024,768]{1,0:T(8,128)(2,1)}, u32[]{:S(2)}) copy-start(bf16[1024,768]{1,0:T(8,128)(2,1)} %param.18) | copy-start | bytes 4718596
  304.9 14.7 %copy-start.68 = (bf16[1024,3072]{1,0:T(8,128)(2,1)}, bf16[1024,3072]{1,0:T(8,128)(2,1)S(1)}, u32[]{:S(2)}) copy-start(bf16[1024,3072]{1,0:T(8,128)(2,1)S(1)} %get-tuple-element.212) | copy-start | bytes 18874372
  336.3 10.0 %copy-start.15 = (f32[1024,768]{0,1:T(8,128)S(1)}, f32[1024,768]{0,1:T(8,128)}, u32[]{:S(2)}) copy-start(f32[1024,768]{0,1:T(8,128)} %copy.146) | copy-start | bytes 9437188
  467.9 16.5 %copy-start.8 = (f32[1024,768]{0,1:T(8,128)S(1)}, f32[1024,768]{0,1:T(8,128)}, u32[]{:S(2)}) copy-start(f32[1024,768]{0,1:T(8,128)} %get-tuple-element.155) | copy-start | bytes 9437188
  484.4 15.4 %copy-start.69 = (bf16[1024,3072]{1,0:T(8,128)(2,1)}, bf16[1024,3072]{1,0:T(8,128)(2,1)S(1)}, u32[]{:S(2)}) copy-start(bf16[1024,3072]{1,0:T(8,128)(2,1)S(1)} %get-tuple-element.218) | copy-start | bytes 18874372
  516.6 7.4 %copy-start.53 = (f32[1024]{0:T(1024)S(1)}, f32[1024]{0:T(1024)}, u32[]{:S(2)}) copy-start(f32[1024]{0:T(1024)} %copy-done.52) | copy-start | bytes 12292
  516.6 7.4 %copy-start.16 = (f32[1024,768]{0,1:T(8,128)S(1)}, f32[1024,768]{0,1:T(8,128)}, u32[]{:S(2)}) copy-start(f32[1024,768]{0,1:T(8,128)} %copy.148) | copy-start | bytes 9437188
  627.9 5.7 copy-start.37
  627.9 5.7 copy-start.39
  637.4 5.5 copy-start.47
  637.4 5.5 copy-start.49
  637.4 5.5 copy-start.63
  648.6 6.1 copy-start.51
  660.3 42.6 %copy-start.41 = (f32[24,2304]{1,0:T(8,128)S(1)}, f32[24,2304]{1,0:T(8,128)}, u32[]{:S(2)}) copy-start(f32[24,2304]{1,0:T(8,128)} %get-tuple-element.60) | copy-start | bytes 663556
  (45 other events, 131.9 us)

commit v4 on v3

--- a/solution.py
+++ b/solution.py
@@ -37,6 +37,7 @@
     qs=halves(q)
     tri=lax.broadcasted_iota(jnp.int32,(bq,bq),0)<=lax.broadcasted_iota(jnp.int32,(bq,bq),1)
     for j in range(L//bq):
+        host.tick(jobs,j)
         lo=j*bq; hi=lo+bq
         acc=jnp.zeros((128,bq),F32)
         for h in range(2):
@@ -95,6 +96,7 @@
     tri=lax.broadcasted_iota(jnp.int32,(bq,bq),0)<=lax.broadcasted_iota(jnp.int32,(bq,bq),1)
     nb=L//bq
     for j in reversed(range(nb)):
+        host.tick(jobs,nb-1-j)
         lo=j*bq; hi=lo+bq
         dqT=jnp.zeros((128,bq),F32)
         dkp=None; dvp=None
@@ -174,43 +176,36 @@
 
 
 class Gather:
-    COPIES = 12
+    COPIES = 8
     STEPS = 5
-
-    def __init__(self, me, shard, out, send, recv, local):
-        self.me, self.shard, self.out, self.send, self.recv = me, shard, out, send, recv
-        self.width = shard.shape[-1]
-        self.cut = (self.width // 256 + self.width // 128 % 2) * 128
+    LINKS = ((("z", 8), ), (("first", 8), ("core", 4)), (("second", 16), ("core", 4)), (("core", 8), ))
+
+    def __init__(self, me, shard, out, scratch, cols, x_first, send, recv, local):
+        self.send, self.recv = send, recv
         y, x, z, c = me.y, me.x, me.z, me.c
-        left, right = pl.ds(0, self.cut), pl.ds(self.cut, self.width - self.cut)
-        self.own = pltpu.make_async_copy(shard, out.at[y, x, z, c], local)
+        cols = pl.ds(*cols)
         o = out.at
-        self.plan = [(None, me.to_z[j], out.at[y, x, z, c]) for j in range(3)] + [
-            (None, me.to_x, o[y, x, ALL, c, ALL, left]),
-            (None, me.to_y, o[y, x, ALL, c, ALL, right]),
-            (None, me.to_core, o[y, x, ALL, c]),
-            (None, me.to_y, o[y, ALL, ALL, c, ALL, left]),
-            (None, me.to_x, o[ALL, x, ALL, c, ALL, right]),
-            (None, me.to_core, o[y, 1 - x, ALL, c, ALL, left]),
-            (None, me.to_core, o[1 - y, x, ALL, c, ALL, right]),
-            (None, me.to_core, o[1 - y, ALL, ALL, c, ALL, left]),
-            (None, me.to_core, o[ALL, 1 - x, ALL, c, ALL, right]),
-        ]
+        mine = o[y, x, z, c, :, cols]
+        self.shard = shard.at[:, cols]
+        self.own = pltpu.make_async_copy(self.shard, mine, local)
+        if x_first:
+            links, far, near, rest = (me.to_x, me.to_y), (y, ALL), (y, 1 - x), (1 - y, ALL)
+        else:
+            links, far, near, rest = (me.to_y, me.to_x), (ALL, x), (1 - y, x), (ALL, 1 - x)
+        tail = (ALL, c, ALL, cols)
+        self.plan = [(me.to_z[k], mine) for k in range(3)] + [
+            (links[0], o[(y, x) + tail]), (links[1], o[far + tail]), (me.to_core, o[(y, x) + tail]),
+            (me.to_core, o[near + tail]), (me.to_core, o[rest + tail])]
 
     def copy(self, k):
-        peer, ref = self.plan[k][1:]
+        peer, ref = self.plan[k]
         return pltpu.make_async_remote_copy(
             src_ref=self.shard if k < 3 else ref, dst_ref=ref, send_sem=self.send.at[k],
             recv_sem=self.recv.at[k], device_id=peer, device_id_type=MESH)
 
     def run(self, step):
         waits, starts = [
-            ((), (0, 1, 2)),
-            ((0, 1, 2), (3, 4, 5)),
-            ((3, 4), (6, 7, 8, 9)),
-            ((6, 7), (10, 11)),
-            ((5, 8, 9, 10, 11), ()),
-        ][step]
+            ((), (0, 1, 2)), ((0, 1, 2), (3, 5)), ((3,), (4, 6)), ((4,), (7,)), ((5, 6, 7), ())][step]
         if step == 0:
             self.own.start()
         for k in waits:
@@ -220,30 +215,29 @@
         for k in starts:
             self.copy(k).start()
         if step == 4:
-            for k in range(12):
+            for k in range(8):
                 self.copy(k).wait_send()
 
 
 class Scatter:
-    COPIES = 8
+    COPIES = 6
     STEPS = 5
-
-    def __init__(self, me, term, out, own, r0, r1, r2, r3, send, recv, local):
-        self.me, self.out, self.own, self.r = me, out, own, (r0, r1, r2, r3)
+    LINKS = ((("core", 16), ), (("first", 16), ), (("second", 8), ), (("z", 8), ))
+
+    def __init__(self, me, term, out, scratch, cols, x_first, send, recv, local):
+        self.me, self.out = me, out
+        self.own, self.r = scratch[0], scratch[1:]
         self.send, self.recv = send, recv
-        self.width = own.shape[-1]
-        self.cut = (self.width // 256 + self.width // 128 % 2) * 128
+        self.cols, self.x_first = pl.ds(*cols), x_first
+        own, (r0, r1, r2, r3) = self.own, self.r
         y, x, z, c = me.y, me.x, me.z, me.c
-        left, right = pl.ds(0, self.cut), pl.ds(self.cut, self.width - self.cut)
-        self.mine = pltpu.make_async_copy(term.at[ALL, ALL, ALL, c], own, local)
-        self.left, self.right = left, right
-        self.plan = [
-            (term.at[ALL, ALL, ALL, 1 - c], me.to_core, r0),
-            (own.at[1 - y, ALL, ALL, ALL, left], me.to_y, r1.at[ALL, ALL, ALL, left]),
-            (own.at[ALL, 1 - x, ALL, ALL, right], me.to_x, r1.at[ALL, ALL, ALL, right]),
-            (own.at[y, 1 - x, ALL, ALL, left], me.to_x, r2.at[ALL, ALL, left]),
-            (own.at[1 - y, x, ALL, ALL, right], me.to_y, r2.at[ALL, ALL, right]),
-        ] + [(own.at[y, x, me.zs[j]], me.to_z[j], r3.at[j]) for j in range(3)]
+        self.mine = pltpu.make_async_copy(term.at[ALL, ALL, ALL, c, :, self.cols], own, local)
+        if x_first:
+            pair = [(own.at[ALL, 1 - x], me.to_x, r1), (own.at[1 - y, x], me.to_y, r2)]
+        else:
+            pair = [(own.at[1 - y], me.to_y, r1), (own.at[y, 1 - x], me.to_x, r2)]
+        self.plan = [(term.at[ALL, ALL, ALL, 1 - c, :, self.cols], me.to_core, r0)] + pair + [
+            (own.at[y, x, me.zs[k]], me.to_z[k], r3.at[k]) for k in range(3)]
 
     def copy(self, k):
         src, peer, dst = self.plan[k]
@@ -254,7 +248,6 @@
     def run(self, step):
         y, x, z = self.me.y, self.me.x, self.me.z
         own, (r0, r1, r2, r3) = self.own, self.r
-        left, right = self.left, self.right
         if step == 0:
             self.mine.start()
             self.copy(0).start()
@@ -269,85 +262,126 @@
                         own[a, b, k] = own[a, b, k] + r0[a, b, k]
 
             self.copy(1).start()
-            self.copy(2).start()
         elif step == 2:
             self.copy(1).wait_recv()
-            self.copy(2).wait_recv()
 
             @pl.loop(0, 4)
             def _(k):
                 for a in range(2):
-                    own[y, a, k, :, left] = own[y, a, k, :, left] + r1[a, k, :, left]
-                    own[a, x, k, :, right] = own[a, x, k, :, right] + r1[a, k, :, right]
-
-            self.copy(3).start()
-            self.copy(4).start()
+                    if self.x_first:
+                        own[a, x, k] = own[a, x, k] + r1[a, k]
+                    else:
+                        own[y, a, k] = own[y, a, k] + r1[a, k]
+
+            self.copy(2).start()
         elif step == 3:
-            self.copy(3).wait_recv()
-            self.copy(4).wait_recv()
+            self.copy(2).wait_recv()
 
             @pl.loop(0, 4)
             def _(k):
                 own[y, x, k] = own[y, x, k] + r2[k]
 
-            for k in (5, 6, 7):
+            for k in (3, 4, 5):
                 self.copy(k).start()
         else:
             total = own[y, x, z].astype(F32)
-            for k in (5, 6, 7):
+            for k in (3, 4, 5):
                 self.copy(k).wait_recv()
-                total = total + r3[k - 5].astype(F32)
-            self.out[...] = total
-            for k in range(8):
+                total = total + r3[k - 3].astype(F32)
+            self.out[:, self.cols] = total
+            for k in range(6):
                 self.copy(k).wait_send()
 
 
-def host_specs(kind, arrays):
-    n = len(arrays)
-    sems = [pltpu.SemaphoreType.DMA((n, kind.COPIES)), pltpu.SemaphoreType.DMA((n, kind.COPIES)),
-            pltpu.SemaphoreType.DMA((n,))]
-    if kind is Gather:
-        ins = [pl.BlockSpec(memory_space=pltpu.VMEM)] * n
-        outs = [pl.BlockSpec(memory_space=pl.ANY)] * n
-        shapes = [jax.ShapeDtypeStruct((2, 2, 4, 2) + a.shape, a.dtype) for a in arrays]
-        return ins, outs, shapes, sems
-    ins = [pl.BlockSpec(memory_space=pl.ANY)] * n
-    outs = [pl.BlockSpec(memory_space=pltpu.VMEM)] * n
-    shapes = [jax.ShapeDtypeStruct(a.shape[4:], F32) for a in arrays]
-    scratch = []
-    for a in arrays:
-        tail = a.shape[4:]
-        for lead in ((2, 2, 4), (2, 2, 4), (2, 4), (4,), (3,)):
-            scratch.append(pltpu.VMEM(lead + tail, a.dtype))
-    return ins, outs, shapes, scratch + sems
-
-
-def host_build(kind, ins, outs, scratch):
-    me = Place()
-    send, recv, local = scratch[-3:]
+def cut_jobs(arrays, kind, pieces):
     jobs = []
-    for i in range(len(ins)):
-        extra = scratch[5 * i : 5 * i + 5] if kind is Scatter else ()
-        jobs.append(kind(me, ins[i], outs[i], *extra, send.at[i], recv.at[i], local.at[i]))
-    return me, jobs
-
-
-def in_order(count, steps):
-    return [(i, t - i) for t in range(count + steps - 1) for i in range(count) if 0 <= t - i < steps]
+    for i, a in enumerate(arrays):
+        units = a.shape[-1] // 128
+        n = min(pieces, units)
+        start = 0
+        for k in range(n):
+            width = 128 * (units // n + (1 if k < units % n else 0))
+            jobs.append((i, (start, width), len(jobs) % 2 == 0))
+            start += width
+    return jobs
+
+
+def plan_jobs(kind, jobs, rows, slots):
+    free = dict.fromkeys("xyzc", 0.0)
+    ready = {}
+
+    def start(i, step, now):
+        array, (unused, width), x_first = jobs[i]
+        done = now
+        names = {"z": "z", "core": "c", "first": "x" if x_first else "y", "second": "y" if x_first else "x"}
+        if step < len(kind.LINKS):
+            for link, blocks in kind.LINKS[step]:
+                name = names[link]
+                rate = 500e3 if name == "c" else 88e3
+                free[name] = max(free[name], now) + blocks * rows[array] * width * 2 / rate
+                if not (kind is Gather and name == "c" and step < 3):
+                    done = max(done, free[name])
+        if step < kind.STEPS - 1:
+            ready[i, step + 1] = done + 1.8
+
+    for i in range(len(jobs)):
+        start(i, 0, 0.0)
+    now, plan = 0.0, []
+    cost = 0.1 if kind is Gather else 0.5
+    for length in slots:
+        todo = []
+        while True:
+            can = sorted((e for e in ready if ready[e] <= now and e[1] < kind.STEPS - 1), key=lambda e: (-e[1], e[0]))
+            if not can:
+                break
+            ready.pop(can[0])
+            now += cost
+            start(*can[0], now)
+            todo.append(can[0])
+        plan.append(todo)
+        now += length
+    todo = []
+    while ready:
+        e = min(ready, key=lambda e: (max(ready[e], now), -e[1], e[0]))
+        now = max(ready.pop(e), now) + cost
+        start(*e, now)
+        todo.append(e)
+    return plan + [todo]
 
 
 class Host:
-    def __init__(self, kind=None, arrays=(), ident=None, plan=None, axis=1):
-        self.kind, self.ident, self.plan, self.axis = kind, ident, plan, axis
+    def __init__(self, kind=None, arrays=(), ident=None, slots=(), per=1, axis=1, pieces=2):
+        self.kind, self.ident, self.per, self.axis = kind, ident, per, axis
         self.used = bool(arrays) and block_mesh()
         self.source = list(arrays)
         self.arrays, self.ins, self.outs, self.shapes, self.scratch = [], [], [], [], []
         if self.used:
-            if kind is Scatter:
-                arrays = [a.reshape(2, 2, 4, 2, -1, a.shape[-1]) for a in arrays]
-            self.arrays = list(arrays)
-            self.ins, self.outs, self.shapes, self.scratch = host_specs(kind, self.arrays)
+            self.build(arrays, slots, pieces)
         self.count = len(self.arrays)
+
+    def build(self, arrays, slots, pieces):
+        kind = self.kind
+        if kind is Scatter:
+            arrays = [a.reshape(2, 2, 4, 2, -1, a.shape[-1]) for a in arrays]
+        self.arrays = arrays = list(arrays)
+        n = len(arrays)
+        self.jobs = jobs = cut_jobs(arrays, kind, pieces)
+        rows = [a.shape[-2] * a.dtype.itemsize // 2 for a in arrays]
+        self.plan = plan_jobs(kind, jobs, rows, slots)
+        m = len(jobs)
+        any_space, vmem = pl.BlockSpec(memory_space=pl.ANY), pl.BlockSpec(memory_space=pltpu.VMEM)
+        if kind is Gather:
+            self.ins, self.outs = [vmem] * n, [any_space] * n
+            self.shapes = [jax.ShapeDtypeStruct((2, 2, 4, 2) + a.shape, a.dtype) for a in arrays]
+        else:
+            self.ins, self.outs = [any_space] * n, [vmem] * n
+            self.shapes = [jax.ShapeDtypeStruct(a.shape[4:], F32) for a in arrays]
+            for i, (unused, width), unused in jobs:
+                for lead in ((2, 2, 4), (2, 2, 4), (2, 4), (4,), (3,)):
+                    self.scratch.append(pltpu.VMEM(lead + (arrays[i].shape[-2], width), arrays[i].dtype))
+        self.scratch = self.scratch + [
+            pltpu.SemaphoreType.DMA((m, kind.COPIES)), pltpu.SemaphoreType.DMA((m, kind.COPIES)),
+            pltpu.SemaphoreType.DMA((m,))]
 
     def params(self):
         if not self.used:
@@ -358,31 +392,41 @@
     def enter(self, ins, outs, scratch):
         if not self.used:
             return None
-        me, jobs = host_build(self.kind, ins, outs, scratch)
-        now = pl.program_id(self.axis)
-
-        @pl.when(now == 0)
+        me = Place()
+        send, recv, local = scratch[-3:]
+        work = []
+        for k, (i, cols, x_first) in enumerate(self.jobs):
+            own = scratch[5 * k : 5 * k + 5] if self.kind is Scatter else ()
+            work.append(self.kind(me, ins[i], outs[i], own, cols, x_first, send.at[k], recv.at[k], local.at[k]))
+        self.now = pl.program_id(self.axis)
+
+        @pl.when(self.now == 0)
         def _():
             me.greet()
-            for job in jobs:
+            for job in work:
                 job.run(0)
 
-        for g, todo in enumerate(self.plan[:-1]):
+        return work
+
+    def tick(self, work, at):
+        if not self.used:
+            return
+        for g in range((len(self.plan) - 1) // self.per):
+            todo = self.plan[g * self.per + at]
             if todo:
-                @pl.when(now == g)
+                @pl.when(self.now == g)
                 def _():
                     for i, t in todo:
-                        jobs[i].run(t)
-
-        return jobs
-
-    def leave(self, jobs):
+                        work[i].run(t)
+
+    def leave(self, work):
         if not self.used:
             return
-        @pl.when(pl.program_id(self.axis) == len(self.plan) - 2)
+
+        @pl.when(self.now == (len(self.plan) - 1) // self.per - 1)
         def _():
             for i, t in self.plan[-1]:
-                jobs[i].run(t)
+                work[i].run(t)
 
     def results(self, values):
         if self.used and self.kind is Gather:
@@ -404,9 +448,8 @@
     host.leave(jobs)
 
 
-def exchange(kind, arrays, ident, name):
-    steps = [e for e in in_order(len(arrays), kind.STEPS) if e[1] > 0]
-    host = Host(kind, arrays, ident, [[], steps], axis=0)
+def exchange(kind, arrays, ident, name, pieces):
+    host = Host(kind, arrays, ident, [0.0], axis=0, pieces=pieces)
     if not host.used:
         return plain(kind, arrays)
     return host.results(pl.pallas_call(
@@ -476,16 +519,16 @@
     qkv = (jnp.dot(normed, w["heads"], preferred_element_type=F32) + bias).astype(BF)
     attended, lse, *more = attend_fwd(qkv, first_len, host)
     more = host.results(more)
-    w.update(zip(("mix", "expand", "shrink"), more))
+    w.update(expand=more[0], shrink=more[1], mix=more[-1])
     middle = hidden + jnp.dot(attended, w["mix"], preferred_element_type=F32) + w["mb"]
     normed_two = layer_norm(middle, w["gf"], w["sf"]).astype(BF)
     expanded = jnp.dot(normed_two, w["expand"], preferred_element_type=F32) + w["eb"]
     activated, slope = gelu_pair(expanded)
     result = middle + jnp.dot(activated, w["shrink"], preferred_element_type=F32) + w["sb"]
-    return result, (hidden, normed, qkv, attended, lse, middle, normed_two, activated, slope), more[3:]
-
-
-def backward_use(grad_out, kept, w, first_len, carried, ident, plan):
+    return result, (hidden, normed, qkv, attended, lse, middle, normed_two, activated, slope), more[2:-1]
+
+
+def backward_use(grad_out, kept, w, first_len, carried, ident):
     hidden, normed, qkv, attended, lse, middle, normed_two, activated, slope = kept
     count = lax.axis_size(AX)
     grad_low = grad_out.astype(BF)
@@ -502,7 +545,7 @@
     mix_term = inner_rows(attended, dmb).astype(BF)
     mb = column_sums(dmb)
     do = times_transposed(dmb, w["mix"]).astype(BF)
-    host = Host(Scatter, [shrink_term, expand_term, mix_term] + carried, ident, plan)
+    host = Host(Scatter, [shrink_term, expand_term] + carried + [mix_term], ident, BACKWARD_SLOTS, per=4)
     dq, dk, dv, *more = attend_bwd(qkv, do, lse, first_len, host)
     more = host.results(more)
     dqkv = jnp.concatenate([dq, dk, dv], axis=1)
@@ -522,18 +565,8 @@
     return ga, sa, heads, qb, vb, mix, mb, gf, sf, expand, wide, shrink, sb
 
 
-FORWARD_PLANS = (
-    [[], [(0, 1)], [(0, 2)], [(0, 3)], [(1, 1)], [(1, 2), (0, 4)],
-     [(2, 1), (1, 3), (3, 1), (2, 2), (3, 2), (2, 3), (3, 3), (1, 4), (2, 4), (3, 4)]],
-    [[], [(0, 1)], [(0, 2)], [(0, 3)], [(1, 1)], [(1, 2), (0, 4)],
-     [(2, 1), (1, 3), (2, 2), (2, 3), (1, 4), (2, 4)]],
-)
-BACKWARD_PLANS = (
-    [[], [(0, 1)], [(1, 1)], [(2, 1)], [(0, 2)], [(1, 2)],
-     [(0, 3), (2, 2), (1, 3), (2, 3), (0, 4), (1, 4), (2, 4)]],
-    [[], [(0, 1)], [(1, 1)], [(3, 1), (2, 1)], [(0, 2)], [(1, 2)],
-     [(0, 3), (3, 2), (2, 2), (1, 3), (3, 3), (2, 3), (0, 4), (1, 4), (3, 4), (2, 4)]],
-)
+FORWARD_SLOTS = [0.43, 0.86, 1.29, 1.72] * 6
+BACKWARD_SLOTS = [1.8, 1.35, 0.9, 0.45] * 6
 
 
 def pick_shards(stacks, source):
@@ -558,24 +591,24 @@
     sources = [tie_map[i] for i in range(LAYERS)]
     shards = [local_shards(pick_shards(stacks, s)) for s in sources]
     ways = shards[0][3].shape[0] // shards[0][0].shape[0]
-    (heads,) = exchange(Gather, shards[0][:1], 0, "gather")
+    (heads,) = exchange(Gather, shards[0][:1], 0, "gather", 4)
     kept, weights = [], []
-    loads = [shards[0][1:] + shards[1][:1], shards[1][1:]]
+    loads = [shards[0][2:] + shards[1][:1] + shards[0][1:2], shards[1][2:] + shards[1][1:2]]
     for i in range(LAYERS):
         weights.append(use_heads(heads, width, ways))
-        host = Host(Gather, loads[i], 1 + i, FORWARD_PLANS[i])
+        host = Host(Gather, loads[i], 1 + i, FORWARD_SLOTS, per=4)
         hidden, saved, spare = forward_use(hidden, weights[i], first_length, host)
         heads = spare[0] if spare else None
         kept.append(saved)
     grad = cotangent.astype(F32)
     grad, late, heads_late, small_late = backward_use(
-        grad, kept[1], weights[1], first_length, [], 3, BACKWARD_PLANS[0])
+        grad, kept[1], weights[1], first_length, [], 3)
     grad, early, heads_early, small_early = backward_use(
-        grad, kept[0], weights[0], first_length, [heads_late], 4, BACKWARD_PLANS[1])
+        grad, kept[0], weights[0], first_length, [heads_late], 4)
     heads_early, small = exchange(
-        Scatter, [heads_early, jnp.concatenate([small_early, small_late], axis=1)], 5, "scatter")
-    shares = [as_shares(*early[:3], heads_early, small[:, :LANES]),
-              as_shares(*late, early[3], small[:, LANES:])]
+        Scatter, [heads_early, jnp.concatenate([small_early, small_late], axis=1)], 5, "scatter", 4)
+    shares = [as_shares(early[0], early[1], early[3], heads_early, small[:, :LANES]),
+              as_shares(*late, early[2], small[:, LANES:])]
     return (hidden.astype(BF), grad.astype(BF), *place_terms(sources, shares))
 
 

time: 714 us -> 712 us (level)
  no operation moved by 1% of the time
where the time goes in v4:
time: 712 us; the launch traced here: 703 us
  Pallas kernels  404 us (57%)
  matrix products  196 us (28%)
  local copies, waits for them, and re-layouts  55.1 us (8%)
  other arithmetic  40.8 us (6%)
    pallas_call x2, Pallas kernels, attend_bwd(): pl.pallas_call(functools.partial(bwd_kernel, bq=bq, host=host), grid_spec...  174 us
    pallas_call x2, Pallas kernels, attend_fwd(): pl.pallas_call(functools.partial(fwd_kernel, bq=bq, host=host), grid_spec...  160 us
    pallas_call x2, Pallas kernels, exchange(): pl.pallas_call(functools.partial(alone_kernel, host=host), grid=(1,), in_...  69.7 us
    dot_general x8, matrix products, times_transposed(): lax.dot_general(left, right, (((1,), (1,)), ((), ())), preferred_element_...  69.2 us
    dot_general x8, matrix products, inner_rows(): lax.dot_general(left, right, (((0,), (0,)), ((), ())), preferred_element_...  63.5 us
    dot_general x2, matrix products, forward_use(): jnp.dot(activated, w['shrink'], preferred_element_type=F32)  22.6 us
    unnamed x164, local copies, waits for them, and re-layouts  21.2 us
    dot_general x2, matrix products, forward_use(): jnp.dot(normed_two, w['expand'], preferred_element_type=F32) + w['eb']  20.3 us

profile of v4, /device:TPU:0, one launch (start us, length us, event | category | flops | bytes accessed | tf_op | source)
XLA Modules:
  0.0 702.8 jit_solution(12139341803920811873)
XLA Ops:
  26.0 33.8 %gather.1 = bf16[2,2,4,2,24,2432]{5,4,3,2,1,0:T(8,128)(2,1)} custom-call(bf16[24,2432]{1,0:T(8,128)(2,1)} %fusion.36.refs_0_), custom_call_target="tpu_custom_call" | custom-call | tf_op jit(solution)/shard_map/gather/pallas_call | solution.py:455
  61.3 7.8 %add_convert_fusion.1.q_ref.k_ref.v_ref = bf16[1024,2304]{1,0:T(8,128)(2,1)} fusion(f32[2304]{0:T(1024)S(1)} %fusion.38, bf16[768,2432]{1,0:T(8,128)(2,1)} %bitcast.128, bf16[1024,768]{0,1:T(8,128)(2,1)S(1)} %copy.120, f32[768]{0:T(1024)S(1)} %get-tuple-element.134, f32[768]{0:T(1024)S(1)} %get-tuple-element.135, f32[1024]{0:T(1024)S(1)} %fusion.40, ...), kind=kOutput, calls=%fused_computation.24 | convolution fusion | flops 3633315840 | bytes 9853952 | tf_op jit(solution)/shard_map/dot_general | solution.py:519
  69.1 86.5 %attend_fwd.2 = (bf16[1024,768]{1,0:T(8,128)(2,1)}, f32[6,2,1024]{2,1,0:T(2,128)}, bf16[2,2,4,2,24,3072]{5,4,3,2,1,0:T(8,128)(2,1)}, bf16[2,2,4,2,96,768]{5,4,3,...) custom-call(s32[1]{0:T(128)S(6)} %copy.169.fl_ref, ...), custom_call_target="tpu_custom_call" | custom-call | flops 6442450944 | bytes 6291456 | tf_op jit(solution)/shard_map/attend_fwd/pallas_call | solution.py:70
  157.1 3.4 fusion.90
  161.9 11.7 %fusion.83 = f32[1024,3072]{1,0:T(8,128)} fusion(bf16[768,3072]{1,0:T(8,128)(2,1)} %bitcast.121, f32[1024,768]{0,1:T(8,128)S(1)} %get-tuple-element.202, f32[768]{0:T(1024)S(1)} %get-tuple-element.130, f32[768]{0:T(1024)S(1)} %get-tuple-element.128, f32[1024]{0:T(1024)S(1)} %fusion.41, f32[1024]{0:T(1024)S(1)} %broadcast_multiply_fusion.2), kind=kOutput, calls=%fused_computation.242 | convolution fusion | flops 4835770368 | bytes 20461568 | tf_op jit(solution)/shard_map/dot_general | solution.py:525
  173.7 12.4 %fusion.91 = (f32[1024]{0:T(1024)S(1)}, f32[1024,768]{0,1:T(8,128)S(1)}) fusion(f32[768]{0:T(1024)S(1)} %get-tuple-element.129, f32[1024,768]{0,1:T(8,128)S(1)} %get-tuple-element.202, bf16[3072,768]{1,0:T(8,128)(2,1)S(1)} %bitcast.148, f32[1024,3072]{1,0:T(8,128)} %fusion.83, f32[3072]{0:T(1024)S(1)} %reshape.367), kind=kOutput, calls=%fused_computation.248 | convolution fusion | flops 4865653760 | bytes 23612416 | tf_op jit(solution)/shard_map/dot_general | solution.py:527
  186.5 5.9 add_convert_fusion.q_ref.k_ref.v_ref
  192.4 73.0 %attend_fwd.3 = (bf16[1024,768]{1,0:T(8,128)(2,1)}, f32[6,2,1024]{2,1,0:T(2,128)}, bf16[2,2,4,2,24,3072]{5,4,3,2,1,0:T(8,128)(2,1)}, bf16[2,2,4,2,96,768]{5,4,3,...) custom-call(s32[1]{0:T(128)S(6)} %copy.169.fl_ref, bf16[1024,2304]{1,0:T(8,128)(2,1)} %add_convert_fusion.q_ref.k_ref.v_ref, ...), custom_call_target="tpu_custom_call" | custom-call | flops 6442450944 | bytes 6291456 | tf_op jit(solution)/shard_map/attend_fwd/pallas_call | solution.py:70
  265.5 3.5 fusion.92
  269.5 8.6 %fusion.84 = f32[1024,3072]{1,0:T(8,128)} fusion(bf16[768,3072]{1,0:T(8,128)(2,1)S(1)} %bitcast.126, f32[1024,768]{0,1:T(8,128)S(1)} %get-tuple-element.206, f32[768]{0:T(1024)S(1)} %get-tuple-element.122, f32[768]{0:T(1024)S(1)} %get-tuple-element.120, f32[1024]{0:T(1024)S(1)} %fusion.43, f32[1024]{0:T(1024)S(1)} %broadcast_multiply_fusion), kind=kOutput, calls=%fused_computation.243 | convolution fusion | flops 4835770368 | bytes 20461568 | tf_op jit(solution)/shard_map/dot_general | solution.py:525
  278.1 10.2 %add_convert_fusion.3 = bf16[1024,768]{0,1:T(8,128)(2,1)} fusion(f32[1024,768]{0,1:T(8,128)S(1)} %get-tuple-element.206, bf16[3072,768]{1,0:T(8,128)(2,1)S(1)} %bitcast.156, f32[768]{0:T(1024)S(1)} %get-tuple-element.121, f32[1024,3072]{1,0:T(8,128)} %fusion.84, f32[3072]{0:T(1024)S(1)} %reshape.376), kind=kOutput, calls=%fused_computation.68 | convolution fusion | flops 4865654784 | bytes 22035456 | tf_op jit(solution)/shard_map/dot_general | solution.py:527
  290.8 18.3 %convert_reduce_fusion = (f32[3072]{0:T(1024)S(1)}, bf16[1024,3072]{1,0:T(8,128)(2,1)S(1)}) fusion(f32[1024,3072]{1,0:T(8,128)} %fusion.84, f32[3072]{0:T(1024)S(1)} %reshape.376, bf16[3072,768]{1,0:T(8,128)(2,1)} %bitcast.153, bf16[1024,768]{1,0:T(8,128)(2,1)} %param.18), kind=kOutput, calls=%fused_computation.18 | convolution fusion | flops 4907332608 | bytes 25190400 | tf_op jit(solution)/shard_map/dot_general | solution.py:472
  309.1 14.7 %convolution_convert_fusion.3 = bf16[3072,768]{1,0:T(8,128)(2,1)} fusion(bf16[1024,768]{1,0:T(8,128)(2,1)S(1)} %copy-done.26, f32[1024,3072]{1,0:T(8,128)} %fusion.84, f32[3072]{0:T(1024)S(1)} %reshape.376), kind=kOutput, calls=%fused_computation.28 | convolution fusion | flops 4865654784 | bytes 18886656 | tf_op jit(solution)/shard_map/dot_general | solution.py:468
  323.8 9.1 %fusion.94 = (f32[768]{0:T(1024)S(1)}, f32[1024,768]{1,0:T(8,128)}) fusion(bf16[1024,3072]{1,0:T(8,128)(2,1)S(1)} %get-tuple-element.212, bf16[768,3072]{1,0:T(8,128)(2,1)} %bitcast.123), kind=kOutput, calls=%fused_computation.251 | convolution fusion | flops 4832623616 | bytes 14158848 | tf_op jit(solution)/shard_map/dot_general | solution.py:472
  333.1 3.5 copy.146
  336.7 3.9 multiply_reduce_fusion
  340.6 9.9 %convolution_convert_fusion.2 = bf16[768,3072]{1,0:T(8,128)(2,1)} fusion(bf16[1024,3072]{1,0:T(8,128)(2,1)} %copy-done.68, f32[1024,768]{0,1:T(8,128)S(1)} %copy-done.5, f32[768]{0:T(1024)S(1)} %get-tuple-element.122, f32[768]{0:T(1024)S(1)} %get-tuple-element.120, f32[1024]{0:T(1024)S(1)} %fusion.43, f32[1024]{0:T(1024)S(1)} %broadcast_multiply_fusion), kind=kOutput, calls=%fused_computation.27 | convolution fusion | flops 4838129664 | bytes 14170112 | tf_op jit(solution)/shard_map/dot_general | solution.py:468
  358.9 80.6 %attend_bwd.2 = (bf16[1024,768]{1,0:T(8,128)(2,1)}, bf16[1024,768]{1,0:T(8,128)(2,1)}, bf16[1024,768]{1,0:T(8,128)(2,1)}, f32[96,768]{1,0:T(8,128)}, f32[24,3072]{1,0:T(8,128)}, /*index=5*/f32[24,768]{1,0:T(8,128)}) custom-call(s32[1]{0:T(128)S(6)} %copy.169.fl_ref, bf16[1024,2304]{1,0:T(8,128)(2,1)} %add_convert_fusion.q_ref.k_ref.v_ref, ...), custom_call_target="tpu_custom_call" | custom-call | flops 16106127360 | bytes 12582912 | tf_op jit(solution)/shard_map/attend_bwd/pallas_call | solution.py:137
  445.6 5.5 fusion.93
  451.1 5.6 convolution_convert_fusion.5
  456.8 3.9 copy.147
  465.8 3.3 convert_reduce_fusion.7
  469.2 16.5 %convert_reduce_fusion.1 = (f32[3072]{0:T(1024)S(1)}, bf16[1024,3072]{1,0:T(8,128)(2,1)S(1)}) fusion(f32[1024,3072]{1,0:T(8,128)} %fusion.83, f32[3072]{0:T(1024)S(1)} %copy-done.59, bf16[3072,768]{1,0:T(8,128)(2,1)} %bitcast.145, f32[1024,768]{0,1:T(8,128)} %get-tuple-element.155), kind=kOutput, calls=%fused_computation.19 | convolution fusion | flops 4908119040 | bytes 26763264 | tf_op jit(solution)/shard_map/dot_general | solution.py:472
  485.7 15.4 %convolution_convert_fusion.1 = bf16[3072,768]{1,0:T(8,128)(2,1)} fusion(f32[1024,768]{0,1:T(8,128)S(1)} %copy-done.8, f32[1024,3072]{1,0:T(8,128)} %fusion.83, f32[3072]{0:T(1024)S(1)} %copy-done.59), kind=kOutput, calls=%fused_computation.26 | convolution fusion | flops 4866441216 | bytes 20459520 | tf_op jit(solution)/shard_map/dot_general | solution.py:468
  501.1 9.2 %fusion.96 = (f32[768]{0:T(1024)S(1)}, f32[1024,768]{1,0:T(8,128)}) fusion(bf16[1024,3072]{1,0:T(8,128)(2,1)S(1)} %get-tuple-element.218, bf16[768,3072]{1,0:T(8,128)(2,1)} %bitcast.122), kind=kOutput, calls=%fused_computation.253 | convolution fusion | flops 4832623616 | bytes 14158848 | tf_op jit(solution)/shard_map/dot_general | solution.py:472
  510.5 3.7 copy.148
  518.0 7.3 %convolution_convert_fusion = bf16[768,3072]{1,0:T(8,128)(2,1)} fusion(bf16[1024,3072]{1,0:T(8,128)(2,1)S(1)} %copy-done.70, f32[1024,768]{0,1:T(8,128)S(1)} %copy-done.3, f32[768]{0:T(1024)S(1)} %copy-done.36, f32[768]{0:T(1024)S(1)} %copy-done.32, f32[1024]{0:T(1024)S(1)} %copy-done.34, f32[1024]{0:T(1024)S(1)} %copy-done.30), kind=kOutput, calls=%fused_computation.25 | convolution fusion | flops 4838129664 | bytes 14170112 | tf_op jit(solution)/shard_map/dot_general | solution.py:468
  533.8 93.9 %attend_bwd.3 = (bf16[1024,768]{1,0:T(8,128)(2,1)}, bf16[1024,768]{1,0:T(8,128)(2,1)}, bf16[1024,768]{1,0:T(8,128)(2,1)}, f32[96,768]{1,0:T(8,128)}, f32[24,3072...) custom-call(s32[1]{0:T(128)S(6)} %copy.169.fl_ref, bf16[1024,2304]{1,0:T(8,128)(2,1)} %add_convert_fusion.1.q_ref.k_ref.v_ref, ...), custom_call_target="tpu_custom_call" | custom-call | flops 16106127360 | bytes 12582912 | tf_op jit(solution)/shard_map/attend_bwd/pallas_call | solution.py:137
  637.3 5.5 fusion.95
  642.8 5.7 convolution_convert_fusion.4
  648.5 3.5 copy.149
  661.3 35.8 %scatter.1 = (f32[24,2304]{1,0:T(8,128)}, f32[24,256]{1,0:T(8,128)}) custom-call(bf16[2,2,4,2,24,2304]{5,4,3,2,1,0:T(8,128)(2,1)} %bitcast.130, f32[2,2,4,2,24,256]{5,4,3,2,1,0:T(8,128)} %bitcast.131), custom_call_target="tpu_custom_call" | custom-call | tf_op jit(solution)/shard_map/scatter/pallas_call | solution.py:455
  (299 shorter events, 84.3 us)
Async XLA Ops:
  0.6 20.9 %copy-start.24 = (bf16[1024,768]{1,0:T(8,128)(2,1)S(1)}, bf16[1024,768]{1,0:T(8,128)(2,1)}, u32[]{:S(2)}) copy-start(bf16[1024,768]{1,0:T(8,128)(2,1)} %param.17) | copy-start | bytes 4718596
  22.3 134.8 %copy-start = (bf16[1024,768]{0,1:T(8,128)(2,1)}, bf16[1024,768]{0,1:T(8,128)(2,1)S(1)}, u32[]{:S(2)}) copy-start(bf16[1024,768]{0,1:T(8,128)(2,1)S(1)} %copy.120) | copy-start | bytes 4718596
  22.6 38.7 %copy-start.42 = (f32[1024]{0:T(1024)}, f32[1024]{0:T(1024)S(1)}, u32[]{:S(2)}) copy-start(f32[1024]{0:T(1024)S(1)} %broadcast_multiply_fusion.3) | copy-start | bytes 12292
  24.3 37.0 %copy-start.48 = (f32[1024]{0:T(1024)}, f32[1024]{0:T(1024)S(1)}, u32[]{:S(2)}) copy-start(f32[1024]{0:T(1024)S(1)} %fusion.40) | copy-start | bytes 12292
  61.0 8.1 %copy-start.46 = (f32[768]{0:T(1024)}, f32[768]{0:T(1024)S(1)}, u32[]{:S(2)}) copy-start(f32[768]{0:T(1024)S(1)} %get-tuple-element.135) | copy-start | bytes 9220
  61.0 8.1 %copy-start.62 = (f32[768]{0:T(1024)}, f32[768]{0:T(1024)S(1)}, u32[]{:S(2)}) copy-start(f32[768]{0:T(1024)S(1)} %get-tuple-element.134) | copy-start | bytes 9220
  61.0 100.0 %copy-start.31 = (f32[768]{0:T(1024)}, f32[768]{0:T(1024)S(1)}, u32[]{:S(2)}) copy-start(f32[768]{0:T(1024)S(1)} %get-tuple-element.128) | copy-start | bytes 9220
  61.0 100.0 %copy-start.35 = (f32[768]{0:T(1024)}, f32[768]{0:T(1024)S(1)}, u32[]{:S(2)}) copy-start(f32[768]{0:T(1024)S(1)} %get-tuple-element.130) | copy-start | bytes 9220
  61.3 112.3 %copy-start.58 = (f32[3072]{0:T(1024)}, f32[3072]{0:T(1024)S(1)}, u32[]{:S(2)}) copy-start(f32[3072]{0:T(1024)S(1)} %reshape.367) | copy-start | bytes 36868
  160.5 13.1 %copy-start.2 = (f32[1024,768]{0,1:T(8,128)}, f32[1024,768]{0,1:T(8,128)S(1)}, u32[]{:S(2)}) copy-start(f32[1024,768]{0,1:T(8,128)S(1)} %get-tuple-element.202) | copy-start | bytes 9437188
  160.5 13.1 %slice-start.2 = ((s8[4718592]{0:T(1024)(128)(4,1)}), s8[4194304]{0:T(1024)(128)(4,1)S(1)}, s32[]{:S(2)}) async-start(s8[4718592]{0:T(1024)(128)(4,1)} %bitcast.146), calls=%async_computation.2 | async-start | bytes 8388608
  160.9 12.7 %copy-start.52 = (f32[1024]{0:T(1024)}, f32[1024]{0:T(1024)S(1)}, u32[]{:S(2)}) copy-start(f32[1024]{0:T(1024)S(1)} %multiply_reduce_fusion.8) | copy-start | bytes 12292
  161.9 11.7 %slice-start.3 = ((s8[4718592]{0:T(1024)(128)(4,1)}), s8[524288]{0:T(1024)(128)(4,1)S(1)}, s32[]{:S(2)}) async-start(s8[4718592]{0:T(1024)(128)(4,1)} %bitcast.146), calls=%async_computation.3 | async-start | bytes 1048576
  173.7 12.9 %copy-start.60 = (bf16[2,2,4,2,24,2432]{5,4,3,2,1,0:T(8,128)(2,1)S(1)}, bf16[2,2,4,2,24,2432]{5,4,3,2,1,0:T(8,128)(2,1)}, u32[]{:S(2)}) copy-start(bf16[2,2,4,2,24,2432]{5,4,3,2,1,0:T(8,128)(2,1)} %get-tuple-element.45) | copy-start | bytes 11206660
  186.5 5.9 copy-start.54
  269.0 9.1 %copy-start.4 = (f32[1024,768]{0,1:T(8,128)}, f32[1024,768]{0,1:T(8,128)S(1)}, u32[]{:S(2)}) copy-start(f32[1024,768]{0,1:T(8,128)S(1)} %get-tuple-element.206) | copy-start | bytes 9437188
  269.0 9.1 %slice-start.4 = ((s8[4718592]{0:T(1024)(128)(4,1)}), s8[4194304]{0:T(1024)(128)(4,1)S(1)}, s32[]{:S(2)}) async-start(s8[4718592]{0:T(1024)(128)(4,1)} %bitcast.154), calls=%async_computation.4 | async-start | bytes 8388608
  269.4 8.6 %slice-start.5 = ((s8[4718592]{0:T(1024)(128)(4,1)}), s8[524288]{0:T(1024)(128)(4,1)S(1)}, s32[]{:S(2)}) async-start(s8[4718592]{0:T(1024)(128)(4,1)} %bitcast.154), calls=%async_computation.5 | async-start | bytes 1048576
  290.8 18.3 %copy-start.26 = (bf16[1024,768]{1,0:T(8,128)(2,1)S(1)}, bf16[1024,768]{1,0:T(8,128)(2,1)}, u32[]{:S(2)}) copy-start(bf16[1024,768]{1,0:T(8,128)(2,1)} %param.18) | copy-start | bytes 4718596
  309.1 14.7 %copy-start.68 = (bf16[1024,3072]{1,0:T(8,128)(2,1)}, bf16[1024,3072]{1,0:T(8,128)(2,1)S(1)}, u32[]{:S(2)}) copy-start(bf16[1024,3072]{1,0:T(8,128)(2,1)S(1)} %get-tuple-element.212) | copy-start | bytes 18874372
  340.6 10.0 %copy-start.15 = (f32[1024,768]{0,1:T(8,128)S(1)}, f32[1024,768]{0,1:T(8,128)}, u32[]{:S(2)}) copy-start(f32[1024,768]{0,1:T(8,128)} %copy.146) | copy-start | bytes 9437188
  469.2 16.5 %copy-start.8 = (f32[1024,768]{0,1:T(8,128)S(1)}, f32[1024,768]{0,1:T(8,128)}, u32[]{:S(2)}) copy-start(f32[1024,768]{0,1:T(8,128)} %get-tuple-element.155) | copy-start | bytes 9437188
  485.7 15.4 %copy-start.69 = (bf16[1024,3072]{1,0:T(8,128)(2,1)}, bf16[1024,3072]{1,0:T(8,128)(2,1)S(1)}, u32[]{:S(2)}) copy-start(bf16[1024,3072]{1,0:T(8,128)(2,1)S(1)} %get-tuple-element.218) | copy-start | bytes 18874372
  517.9 7.4 %copy-start.53 = (f32[1024]{0:T(1024)S(1)}, f32[1024]{0:T(1024)}, u32[]{:S(2)}) copy-start(f32[1024]{0:T(1024)} %copy-done.52) | copy-start | bytes 12292
  518.0 7.4 %copy-start.16 = (f32[1024,768]{0,1:T(8,128)S(1)}, f32[1024,768]{0,1:T(8,128)}, u32[]{:S(2)}) copy-start(f32[1024,768]{0,1:T(8,128)} %copy.148) | copy-start | bytes 9437188
  627.8 5.7 copy-start.37
  627.8 5.7 copy-start.39
  637.3 5.5 copy-start.47
  637.3 5.5 copy-start.49
  637.3 5.5 copy-start.63
  648.5 6.1 copy-start.51
  660.2 40.2 %copy-start.41 = (f32[24,2304]{1,0:T(8,128)S(1)}, f32[24,2304]{1,0:T(8,128)}, u32[]{:S(2)}) copy-start(f32[24,2304]{1,0:T(8,128)} %get-tuple-element.60) | copy-start | bytes 663556
  (45 other events, 131.9 us)

commit v5 on v4

--- a/solution.py
+++ b/solution.py
@@ -176,53 +176,65 @@
 
 
 class Gather:
-    COPIES = 8
+    COPIES = 15
     STEPS = 5
-    LINKS = ((("z", 8), ), (("first", 8), ("core", 4)), (("second", 16), ("core", 4)), (("core", 8), ))
+    LINKS = (
+        (("z", 8, True), ("first", 2, False), ("second", 2, False)),
+        (("first", 6, True), ("second", 6, False), ("core", 4, False)),
+        (("second", 8, True), ("core", 4, False)),
+        (("core", 8, True),),
+    )
+    STARTS = ((0, 1, 2, 3, 4), (5, 6, 7, 8, 9, 10, 12), (11, 13), (14,), ())
+    WAITS = ((), (0, 1, 2), (3, 5, 6, 7), (4, 8, 9, 10, 11), (12, 13, 14))
 
     def __init__(self, me, shard, out, scratch, cols, x_first, send, recv, local):
         self.send, self.recv = send, recv
         y, x, z, c = me.y, me.x, me.z, me.c
         cols = pl.ds(*cols)
         o = out.at
+        tail = (ALL, c, ALL, cols)
         mine = o[y, x, z, c, :, cols]
         self.shard = shard.at[:, cols]
         self.own = pltpu.make_async_copy(self.shard, mine, local)
         if x_first:
-            links, far, near, rest = (me.to_x, me.to_y), (y, ALL), (y, 1 - x), (1 - y, ALL)
+            links, near, rest = (me.to_x, me.to_y), (y, 1 - x), (1 - y, ALL)
         else:
-            links, far, near, rest = (me.to_y, me.to_x), (ALL, x), (1 - y, x), (ALL, 1 - x)
-        tail = (ALL, c, ALL, cols)
-        self.plan = [(me.to_z[k], mine) for k in range(3)] + [
-            (links[0], o[(y, x) + tail]), (links[1], o[far + tail]), (me.to_core, o[(y, x) + tail]),
-            (me.to_core, o[near + tail]), (me.to_core, o[rest + tail])]
+            links, near, rest = (me.to_y, me.to_x), (1 - y, x), (ALL, 1 - x)
+        came = [o[y, x, zz, c, :, cols] for zz in me.zs]
+        self.plan = [(me.to_z[k], mine) for k in range(3)] + [(links[0], mine), (links[1], mine)]
+        self.plan += [(links[0], r) for r in came] + [(links[1], r) for r in came]
+        self.plan += [(links[1], o[near + tail]), (me.to_core, o[(y, x) + tail]),
+                      (me.to_core, o[near + tail]), (me.to_core, o[rest + tail])]
 
     def copy(self, k):
         peer, ref = self.plan[k]
         return pltpu.make_async_remote_copy(
-            src_ref=self.shard if k < 3 else ref, dst_ref=ref, send_sem=self.send.at[k],
+            src_ref=self.shard if k < 5 else ref, dst_ref=ref, send_sem=self.send.at[k],
             recv_sem=self.recv.at[k], device_id=peer, device_id_type=MESH)
 
     def run(self, step):
-        waits, starts = [
-            ((), (0, 1, 2)), ((0, 1, 2), (3, 5)), ((3,), (4, 6)), ((4,), (7,)), ((5, 6, 7), ())][step]
         if step == 0:
             self.own.start()
-        for k in waits:
+        for k in self.WAITS[step]:
             self.copy(k).wait_recv()
         if step == 1:
             self.own.wait()
-        for k in starts:
+        for k in self.STARTS[step]:
             self.copy(k).start()
         if step == 4:
-            for k in range(8):
+            for k in range(self.COPIES):
                 self.copy(k).wait_send()
 
 
 class Scatter:
-    COPIES = 6
+    COPIES = 7
     STEPS = 5
-    LINKS = ((("core", 16), ), (("first", 16), ), (("second", 8), ), (("z", 8), ))
+    LINKS = (
+        (("core", 16, True),),
+        (("first", 8, True), ("first", 8, False)),
+        (("second", 8, True),),
+        (("z", 8, True),),
+    )
 
     def __init__(self, me, term, out, scratch, cols, x_first, send, recv, local):
         self.me, self.out = me, out
@@ -233,10 +245,12 @@
         y, x, z, c = me.y, me.x, me.z, me.c
         self.mine = pltpu.make_async_copy(term.at[ALL, ALL, ALL, c, :, self.cols], own, local)
         if x_first:
-            pair = [(own.at[ALL, 1 - x], me.to_x, r1), (own.at[1 - y, x], me.to_y, r2)]
+            first, second, near, across = me.to_x, me.to_y, own.at[y, 1 - x], own.at[1 - y, x]
         else:
-            pair = [(own.at[1 - y], me.to_y, r1), (own.at[y, 1 - x], me.to_x, r2)]
-        self.plan = [(term.at[ALL, ALL, ALL, 1 - c, :, self.cols], me.to_core, r0)] + pair + [
+            first, second, near, across = me.to_y, me.to_x, own.at[1 - y, x], own.at[y, 1 - x]
+        self.plan = [
+            (term.at[ALL, ALL, ALL, 1 - c, :, self.cols], me.to_core, r0),
+            (own.at[1 - y, 1 - x], first, r1.at[0]), (near, first, r1.at[1]), (across, second, r2)] + [
             (own.at[y, x, me.zs[k]], me.to_z[k], r3.at[k]) for k in range(3)]
 
     def copy(self, k):
@@ -262,34 +276,34 @@
                         own[a, b, k] = own[a, b, k] + r0[a, b, k]
 
             self.copy(1).start()
+            self.copy(2).start()
         elif step == 2:
             self.copy(1).wait_recv()
+            ay, ax = (1 - y, x) if self.x_first else (y, 1 - x)
 
             @pl.loop(0, 4)
             def _(k):
-                for a in range(2):
-                    if self.x_first:
-                        own[a, x, k] = own[a, x, k] + r1[a, k]
-                    else:
-                        own[y, a, k] = own[y, a, k] + r1[a, k]
-
-            self.copy(2).start()
+                own[ay, ax, k] = own[ay, ax, k] + r1[0, k]
+
+            self.copy(3).start()
         elif step == 3:
             self.copy(2).wait_recv()
+            self.copy(3).wait_recv()
 
             @pl.loop(0, 4)
             def _(k):
-                own[y, x, k] = own[y, x, k] + r2[k]
-
-            for k in (3, 4, 5):
+                total = own[y, x, k].astype(F32) + r1[1, k].astype(F32) + r2[k].astype(F32)
+                own[y, x, k] = total.astype(own.dtype)
+
+            for k in (4, 5, 6):
                 self.copy(k).start()
         else:
             total = own[y, x, z].astype(F32)
-            for k in (3, 4, 5):
+            for k in (4, 5, 6):
                 self.copy(k).wait_recv()
-                total = total + r3[k - 3].astype(F32)
+                total = total + r3[k - 4].astype(F32)
             self.out[:, self.cols] = total
-            for k in range(6):
+            for k in range(self.COPIES):
                 self.copy(k).wait_send()
 
 
@@ -306,7 +320,7 @@
     return jobs
 
 
-def plan_jobs(kind, jobs, rows, slots):
+def plan_jobs(kind, jobs, rows, slots, window):
     free = dict.fromkeys("xyzc", 0.0)
     ready = {}
 
@@ -315,17 +329,19 @@
         done = now
         names = {"z": "z", "core": "c", "first": "x" if x_first else "y", "second": "y" if x_first else "x"}
         if step < len(kind.LINKS):
-            for link, blocks in kind.LINKS[step]:
+            for link, blocks, counts in kind.LINKS[step]:
                 name = names[link]
-                rate = 500e3 if name == "c" else 88e3
+                rate = {"c": 500e3, "z": 78e3}.get(name, 83e3)
                 free[name] = max(free[name], now) + blocks * rows[array] * width * 2 / rate
-                if not (kind is Gather and name == "c" and step < 3):
+                if counts:
                     done = max(done, free[name])
         if step < kind.STEPS - 1:
             ready[i, step + 1] = done + 1.8
-
-    for i in range(len(jobs)):
-        start(i, 0, 0.0)
+        if step == 1 and i + window < len(jobs):
+            ready[i + window, 0] = now
+
+    for i in range(min(window, len(jobs))):
+        ready[i, 0] = 0.0
     now, plan = 0.0, []
     cost = 0.1 if kind is Gather else 0.5
     for length in slots:
@@ -350,24 +366,25 @@
 
 
 class Host:
-    def __init__(self, kind=None, arrays=(), ident=None, slots=(), per=1, axis=1, pieces=2):
+    def __init__(self, kind=None, arrays=(), ident=None, slots=(), per=1, axis=1, pieces=None, window=None):
         self.kind, self.ident, self.per, self.axis = kind, ident, per, axis
         self.used = bool(arrays) and block_mesh()
         self.source = list(arrays)
         self.arrays, self.ins, self.outs, self.shapes, self.scratch = [], [], [], [], []
         if self.used:
-            self.build(arrays, slots, pieces)
+            self.build(arrays, slots, pieces, window)
         self.count = len(self.arrays)
 
-    def build(self, arrays, slots, pieces):
+    def build(self, arrays, slots, pieces, window):
         kind = self.kind
         if kind is Scatter:
             arrays = [a.reshape(2, 2, 4, 2, -1, a.shape[-1]) for a in arrays]
         self.arrays = arrays = list(arrays)
         n = len(arrays)
+        pieces = pieces or (2 if kind is Gather else 4)
         self.jobs = jobs = cut_jobs(arrays, kind, pieces)
         rows = [a.shape[-2] * a.dtype.itemsize // 2 for a in arrays]
-        self.plan = plan_jobs(kind, jobs, rows, slots)
+        self.plan = plan_jobs(kind, jobs, rows, slots, window or (8 if kind is Gather else 4))
         m = len(jobs)
         any_space, vmem = pl.BlockSpec(memory_space=pl.ANY), pl.BlockSpec(memory_space=pltpu.VMEM)
         if kind is Gather:
@@ -403,8 +420,6 @@
         @pl.when(self.now == 0)
         def _():
             me.greet()
-            for job in work:
-                job.run(0)
 
         return work
 
@@ -445,6 +460,7 @@
 def alone_kernel(*refs, host):
     n = host.count
     jobs = host.enter(refs[:n], refs[n : 2 * n], refs[2 * n :])
+    host.tick(jobs, 0)
     host.leave(jobs)
 
 

time: 712 us -> 671 us (0.942)
  Pallas kernels: 404 us -> 364 us
    pallas_call x2, Pallas kernels: 174 us -> 156 us  [attend_bwd(): pl.pallas_call(functools.partial(bwd_kernel, bq=bq, host=host), grid_spec...]
    pallas_call x2, Pallas kernels: 160 us -> 142 us  [attend_fwd(): pl.pallas_call(functools.partial(fwd_kernel, bq=bq, host=host), grid_spec...]
where the time goes in v5:
time: 671 us; the launch traced here: 662 us
  Pallas kernels  364 us (54%)
  matrix products  196 us (29%)
  local copies, waits for them, and re-layouts  55 us (8%)
  other arithmetic  40.8 us (6%)
  between operations  6.89 us (1%)
    pallas_call x2, Pallas kernels, attend_bwd(): pl.pallas_call(functools.partial(bwd_kernel, bq=bq, host=host), grid_spec...  156 us
    pallas_call x2, Pallas kernels, attend_fwd(): pl.pallas_call(functools.partial(fwd_kernel, bq=bq, host=host), grid_spec...  142 us
    dot_general x8, matrix products, times_transposed(): lax.dot_general(left, right, (((1,), (1,)), ((), ())), preferred_element_...  69.1 us
    pallas_call x2, Pallas kernels, exchange(): pl.pallas_call(functools.partial(alone_kernel, host=host), grid=(1,), in_...  65.4 us
    dot_general x8, matrix products, inner_rows(): lax.dot_general(left, right, (((0,), (0,)), ((), ())), preferred_element_...  63.4 us
    dot_general x2, matrix products, forward_use(): jnp.dot(activated, w['shrink'], preferred_element_type=F32)  22.8 us
    unnamed x164, local copies, waits for them, and re-layouts  21.2 us
    dot_general x2, matrix products, forward_use(): jnp.dot(normed_two, w['expand'], preferred_element_type=F32) + w['eb']  20.2 us

profile of v5, /device:TPU:0, one launch (start us, length us, event | category | flops | bytes accessed | tf_op | source)
XLA Modules:
  0.0 662.5 jit_solution(12868945716561139688)
XLA Ops:
  26.0 30.8 %gather.1 = bf16[2,2,4,2,24,2432]{5,4,3,2,1,0:T(8,128)(2,1)} custom-call(bf16[24,2432]{1,0:T(8,128)(2,1)} %fusion.36.refs_0_), custom_call_target="tpu_custom_call" | custom-call | tf_op jit(solution)/shard_map/gather/pallas_call | solution.py:471
  58.3 7.8 %add_convert_fusion.1.q_ref.k_ref.v_ref = bf16[1024,2304]{1,0:T(8,128)(2,1)} fusion(f32[2304]{0:T(1024)S(1)} %fusion.38, bf16[768,2432]{1,0:T(8,128)(2,1)} %bitcast.128, bf16[1024,768]{0,1:T(8,128)(2,1)S(1)} %copy.120, f32[768]{0:T(1024)S(1)} %get-tuple-element.134, f32[768]{0:T(1024)S(1)} %get-tuple-element.135, f32[1024]{0:T(1024)S(1)} %fusion.40, ...), kind=kOutput, calls=%fused_computation.24 | convolution fusion | flops 3633315840 | bytes 9853952 | tf_op jit(solution)/shard_map/dot_general | solution.py:535
  66.0 77.3 %attend_fwd.2 = (bf16[1024,768]{1,0:T(8,128)(2,1)}, f32[6,2,1024]{2,1,0:T(2,128)}, bf16[2,2,4,2,24,3072]{5,4,3,2,1,0:T(8,128)(2,1)}, bf16[2,2,4,2,96,768]{5,4,3,...) custom-call(s32[1]{0:T(128)S(6)} %copy.169.fl_ref, ...), custom_call_target="tpu_custom_call" | custom-call | flops 6442450944 | bytes 6291456 | tf_op jit(solution)/shard_map/attend_fwd/pallas_call | solution.py:70
  144.8 3.4 fusion.90
  149.7 11.6 %fusion.83 = f32[1024,3072]{1,0:T(8,128)} fusion(bf16[768,3072]{1,0:T(8,128)(2,1)} %bitcast.121, f32[1024,768]{0,1:T(8,128)S(1)} %get-tuple-element.202, f32[768]{0:T(1024)S(1)} %get-tuple-element.130, f32[768]{0:T(1024)S(1)} %get-tuple-element.128, f32[1024]{0:T(1024)S(1)} %fusion.41, f32[1024]{0:T(1024)S(1)} %broadcast_multiply_fusion.2), kind=kOutput, calls=%fused_computation.242 | convolution fusion | flops 4835770368 | bytes 20461568 | tf_op jit(solution)/shard_map/dot_general | solution.py:541
  161.4 12.4 %fusion.91 = (f32[1024]{0:T(1024)S(1)}, f32[1024,768]{0,1:T(8,128)S(1)}) fusion(f32[768]{0:T(1024)S(1)} %get-tuple-element.129, f32[1024,768]{0,1:T(8,128)S(1)} %get-tuple-element.202, bf16[3072,768]{1,0:T(8,128)(2,1)S(1)} %bitcast.148, f32[1024,3072]{1,0:T(8,128)} %fusion.83, f32[3072]{0:T(1024)S(1)} %reshape.367), kind=kOutput, calls=%fused_computation.248 | convolution fusion | flops 4865653760 | bytes 23612416 | tf_op jit(solution)/shard_map/dot_general | solution.py:543
  174.2 5.9 add_convert_fusion.q_ref.k_ref.v_ref
  180.1 64.5 %attend_fwd.3 = (bf16[1024,768]{1,0:T(8,128)(2,1)}, f32[6,2,1024]{2,1,0:T(2,128)}, bf16[2,2,4,2,24,3072]{5,4,3,2,1,0:T(8,128)(2,1)}, bf16[2,2,4,2,96,768]{5,4,3,...) custom-call(s32[1]{0:T(128)S(6)} %copy.169.fl_ref, bf16[1024,2304]{1,0:T(8,128)(2,1)} %add_convert_fusion.q_ref.k_ref.v_ref, ...), custom_call_target="tpu_custom_call" | custom-call | flops 6442450944 | bytes 6291456 | tf_op jit(solution)/shard_map/attend_fwd/pallas_call | solution.py:70
  244.7 3.5 fusion.92
  248.7 8.6 %fusion.84 = f32[1024,3072]{1,0:T(8,128)} fusion(bf16[768,3072]{1,0:T(8,128)(2,1)S(1)} %bitcast.126, f32[1024,768]{0,1:T(8,128)S(1)} %get-tuple-element.206, f32[768]{0:T(1024)S(1)} %get-tuple-element.122, f32[768]{0:T(1024)S(1)} %get-tuple-element.120, f32[1024]{0:T(1024)S(1)} %fusion.43, f32[1024]{0:T(1024)S(1)} %broadcast_multiply_fusion), kind=kOutput, calls=%fused_computation.243 | convolution fusion | flops 4835770368 | bytes 20461568 | tf_op jit(solution)/shard_map/dot_general | solution.py:541
  257.3 10.4 %add_convert_fusion.3 = bf16[1024,768]{0,1:T(8,128)(2,1)} fusion(f32[1024,768]{0,1:T(8,128)S(1)} %get-tuple-element.206, bf16[3072,768]{1,0:T(8,128)(2,1)S(1)} %bitcast.156, f32[768]{0:T(1024)S(1)} %get-tuple-element.121, f32[1024,3072]{1,0:T(8,128)} %fusion.84, f32[3072]{0:T(1024)S(1)} %reshape.376), kind=kOutput, calls=%fused_computation.68 | convolution fusion | flops 4865654784 | bytes 22035456 | tf_op jit(solution)/shard_map/dot_general | solution.py:543
  270.2 15.6 %convert_reduce_fusion = (f32[3072]{0:T(1024)S(1)}, bf16[1024,3072]{1,0:T(8,128)(2,1)S(1)}) fusion(f32[1024,3072]{1,0:T(8,128)} %fusion.84, f32[3072]{0:T(1024)S(1)} %reshape.376, bf16[3072,768]{1,0:T(8,128)(2,1)} %bitcast.153, bf16[1024,768]{1,0:T(8,128)(2,1)} %param.18), kind=kOutput, calls=%fused_computation.18 | convolution fusion | flops 4907332608 | bytes 25190400 | tf_op jit(solution)/shard_map/dot_general | solution.py:488
  285.9 14.5 %convolution_convert_fusion.3 = bf16[3072,768]{1,0:T(8,128)(2,1)} fusion(bf16[1024,768]{1,0:T(8,128)(2,1)S(1)} %copy-done.26, f32[1024,3072]{1,0:T(8,128)} %fusion.84, f32[3072]{0:T(1024)S(1)} %reshape.376), kind=kOutput, calls=%fused_computation.28 | convolution fusion | flops 4865654784 | bytes 18886656 | tf_op jit(solution)/shard_map/dot_general | solution.py:484
  300.4 9.1 %fusion.94 = (f32[768]{0:T(1024)S(1)}, f32[1024,768]{1,0:T(8,128)}) fusion(bf16[1024,3072]{1,0:T(8,128)(2,1)S(1)} %get-tuple-element.212, bf16[768,3072]{1,0:T(8,128)(2,1)} %bitcast.123), kind=kOutput, calls=%fused_computation.251 | convolution fusion | flops 4832623616 | bytes 14158848 | tf_op jit(solution)/shard_map/dot_general | solution.py:488
  309.7 3.5 copy.146
  313.2 3.9 multiply_reduce_fusion
  317.1 10.1 %convolution_convert_fusion.2 = bf16[768,3072]{1,0:T(8,128)(2,1)} fusion(bf16[1024,3072]{1,0:T(8,128)(2,1)} %copy-done.68, f32[1024,768]{0,1:T(8,128)S(1)} %copy-done.5, f32[768]{0:T(1024)S(1)} %get-tuple-element.122, f32[768]{0:T(1024)S(1)} %get-tuple-element.120, f32[1024]{0:T(1024)S(1)} %fusion.43, f32[1024]{0:T(1024)S(1)} %broadcast_multiply_fusion), kind=kOutput, calls=%fused_computation.27 | convolution fusion | flops 4838129664 | bytes 14170112 | tf_op jit(solution)/shard_map/dot_general | solution.py:484
  335.6 71.4 %attend_bwd.2 = (bf16[1024,768]{1,0:T(8,128)(2,1)}, bf16[1024,768]{1,0:T(8,128)(2,1)}, bf16[1024,768]{1,0:T(8,128)(2,1)}, f32[96,768]{1,0:T(8,128)}, f32[24,3072]{1,0:T(8,128)}, /*index=5*/f32[24,768]{1,0:T(8,128)}) custom-call(s32[1]{0:T(128)S(6)} %copy.169.fl_ref, bf16[1024,2304]{1,0:T(8,128)(2,1)} %add_convert_fusion.q_ref.k_ref.v_ref, ...), custom_call_target="tpu_custom_call" | custom-call | flops 16106127360 | bytes 12582912 | tf_op jit(solution)/shard_map/attend_bwd/pallas_call | solution.py:137
  413.2 5.5 fusion.93
  418.7 5.6 convolution_convert_fusion.5
  424.3 3.5 copy.147
  433.0 3.3 convert_reduce_fusion.7
  436.3 19.0 %convert_reduce_fusion.1 = (f32[3072]{0:T(1024)S(1)}, bf16[1024,3072]{1,0:T(8,128)(2,1)S(1)}) fusion(f32[1024,3072]{1,0:T(8,128)} %fusion.83, f32[3072]{0:T(1024)S(1)} %copy-done.59, bf16[3072,768]{1,0:T(8,128)(2,1)} %bitcast.145, f32[1024,768]{0,1:T(8,128)} %get-tuple-element.155), kind=kOutput, calls=%fused_computation.19 | convolution fusion | flops 4908119040 | bytes 26763264 | tf_op jit(solution)/shard_map/dot_general | solution.py:488
  455.4 15.5 %convolution_convert_fusion.1 = bf16[3072,768]{1,0:T(8,128)(2,1)} fusion(f32[1024,768]{0,1:T(8,128)S(1)} %copy-done.8, f32[1024,3072]{1,0:T(8,128)} %fusion.83, f32[3072]{0:T(1024)S(1)} %copy-done.59), kind=kOutput, calls=%fused_computation.26 | convolution fusion | flops 4866441216 | bytes 20459520 | tf_op jit(solution)/shard_map/dot_general | solution.py:484
  470.9 9.2 %fusion.96 = (f32[768]{0:T(1024)S(1)}, f32[1024,768]{1,0:T(8,128)}) fusion(bf16[1024,3072]{1,0:T(8,128)(2,1)S(1)} %get-tuple-element.218, bf16[768,3072]{1,0:T(8,128)(2,1)} %bitcast.122), kind=kOutput, calls=%fused_computation.253 | convolution fusion | flops 4832623616 | bytes 14158848 | tf_op jit(solution)/shard_map/dot_general | solution.py:488
  480.4 3.7 copy.148
  487.8 7.1 %convolution_convert_fusion = bf16[768,3072]{1,0:T(8,128)(2,1)} fusion(bf16[1024,3072]{1,0:T(8,128)(2,1)S(1)} %copy-done.70, f32[1024,768]{0,1:T(8,128)S(1)} %copy-done.3, f32[768]{0:T(1024)S(1)} %copy-done.36, f32[768]{0:T(1024)S(1)} %copy-done.32, f32[1024]{0:T(1024)S(1)} %copy-done.34, f32[1024]{0:T(1024)S(1)} %copy-done.30), kind=kOutput, calls=%fused_computation.25 | convolution fusion | flops 4838129664 | bytes 14170112 | tf_op jit(solution)/shard_map/dot_general | solution.py:484
  503.5 84.8 %attend_bwd.3 = (bf16[1024,768]{1,0:T(8,128)(2,1)}, bf16[1024,768]{1,0:T(8,128)(2,1)}, bf16[1024,768]{1,0:T(8,128)(2,1)}, f32[96,768]{1,0:T(8,128)}, f32[24,3072...) custom-call(s32[1]{0:T(128)S(6)} %copy.169.fl_ref, bf16[1024,2304]{1,0:T(8,128)(2,1)} %add_convert_fusion.1.q_ref.k_ref.v_ref, ...), custom_call_target="tpu_custom_call" | custom-call | flops 16106127360 | bytes 12582912 | tf_op jit(solution)/shard_map/attend_bwd/pallas_call | solution.py:137
  597.9 5.5 fusion.95
  603.4 5.7 convolution_convert_fusion.4
  609.1 3.8 copy.149
  622.2 34.6 %scatter.1 = (f32[24,2304]{1,0:T(8,128)}, f32[24,256]{1,0:T(8,128)}) custom-call(bf16[2,2,4,2,24,2304]{5,4,3,2,1,0:T(8,128)(2,1)} %bitcast.130, f32[2,2,4,2,24,256]{5,4,3,2,1,0:T(8,128)} %bitcast.131), custom_call_target="tpu_custom_call" | custom-call | tf_op jit(solution)/shard_map/scatter/pallas_call | solution.py:471
  (299 shorter events, 84.3 us)
Async XLA Ops:
  0.6 20.9 %copy-start.24 = (bf16[1024,768]{1,0:T(8,128)(2,1)S(1)}, bf16[1024,768]{1,0:T(8,128)(2,1)}, u32[]{:S(2)}) copy-start(bf16[1024,768]{1,0:T(8,128)(2,1)} %param.17) | copy-start | bytes 4718596
  22.3 122.5 %copy-start = (bf16[1024,768]{0,1:T(8,128)(2,1)}, bf16[1024,768]{0,1:T(8,128)(2,1)S(1)}, u32[]{:S(2)}) copy-start(bf16[1024,768]{0,1:T(8,128)(2,1)S(1)} %copy.120) | copy-start | bytes 4718596
  22.6 35.6 %copy-start.42 = (f32[1024]{0:T(1024)}, f32[1024]{0:T(1024)S(1)}, u32[]{:S(2)}) copy-start(f32[1024]{0:T(1024)S(1)} %broadcast_multiply_fusion.3) | copy-start | bytes 12292
  24.3 33.9 %copy-start.48 = (f32[1024]{0:T(1024)}, f32[1024]{0:T(1024)S(1)}, u32[]{:S(2)}) copy-start(f32[1024]{0:T(1024)S(1)} %fusion.40) | copy-start | bytes 12292
  57.9 8.1 %copy-start.46 = (f32[768]{0:T(1024)}, f32[768]{0:T(1024)S(1)}, u32[]{:S(2)}) copy-start(f32[768]{0:T(1024)S(1)} %get-tuple-element.135) | copy-start | bytes 9220
  57.9 8.1 %copy-start.62 = (f32[768]{0:T(1024)}, f32[768]{0:T(1024)S(1)}, u32[]{:S(2)}) copy-start(f32[768]{0:T(1024)S(1)} %get-tuple-element.134) | copy-start | bytes 9220
  57.9 90.8 %copy-start.31 = (f32[768]{0:T(1024)}, f32[768]{0:T(1024)S(1)}, u32[]{:S(2)}) copy-start(f32[768]{0:T(1024)S(1)} %get-tuple-element.128) | copy-start | bytes 9220
  58.0 90.8 %copy-start.35 = (f32[768]{0:T(1024)}, f32[768]{0:T(1024)S(1)}, u32[]{:S(2)}) copy-start(f32[768]{0:T(1024)S(1)} %get-tuple-element.130) | copy-start | bytes 9220
  58.3 103.0 %copy-start.58 = (f32[3072]{0:T(1024)}, f32[3072]{0:T(1024)S(1)}, u32[]{:S(2)}) copy-start(f32[3072]{0:T(1024)S(1)} %reshape.367) | copy-start | bytes 36868
  148.2 13.1 %copy-start.2 = (f32[1024,768]{0,1:T(8,128)}, f32[1024,768]{0,1:T(8,128)S(1)}, u32[]{:S(2)}) copy-start(f32[1024,768]{0,1:T(8,128)S(1)} %get-tuple-element.202) | copy-start | bytes 9437188
  148.3 13.0 %slice-start.2 = ((s8[4718592]{0:T(1024)(128)(4,1)}), s8[4194304]{0:T(1024)(128)(4,1)S(1)}, s32[]{:S(2)}) async-start(s8[4718592]{0:T(1024)(128)(4,1)} %bitcast.146), calls=%async_computation.2 | async-start | bytes 8388608
  148.7 12.6 %copy-start.52 = (f32[1024]{0:T(1024)}, f32[1024]{0:T(1024)S(1)}, u32[]{:S(2)}) copy-start(f32[1024]{0:T(1024)S(1)} %multiply_reduce_fusion.8) | copy-start | bytes 12292
  149.7 11.7 %slice-start.3 = ((s8[4718592]{0:T(1024)(128)(4,1)}), s8[524288]{0:T(1024)(128)(4,1)S(1)}, s32[]{:S(2)}) async-start(s8[4718592]{0:T(1024)(128)(4,1)} %bitcast.146), calls=%async_computation.3 | async-start | bytes 1048576
  161.3 12.9 %copy-start.60 = (bf16[2,2,4,2,24,2432]{5,4,3,2,1,0:T(8,128)(2,1)S(1)}, bf16[2,2,4,2,24,2432]{5,4,3,2,1,0:T(8,128)(2,1)}, u32[]{:S(2)}) copy-start(bf16[2,2,4,2,24,2432]{5,4,3,2,1,0:T(8,128)(2,1)} %get-tuple-element.45) | copy-start | bytes 11206660
  174.2 5.9 copy-start.54
  248.2 9.1 %copy-start.4 = (f32[1024,768]{0,1:T(8,128)}, f32[1024,768]{0,1:T(8,128)S(1)}, u32[]{:S(2)}) copy-start(f32[1024,768]{0,1:T(8,128)S(1)} %get-tuple-element.206) | copy-start | bytes 9437188
  248.2 9.1 %slice-start.4 = ((s8[4718592]{0:T(1024)(128)(4,1)}), s8[4194304]{0:T(1024)(128)(4,1)S(1)}, s32[]{:S(2)}) async-start(s8[4718592]{0:T(1024)(128)(4,1)} %bitcast.154), calls=%async_computation.4 | async-start | bytes 8388608
  248.6 8.6 %slice-start.5 = ((s8[4718592]{0:T(1024)(128)(4,1)}), s8[524288]{0:T(1024)(128)(4,1)S(1)}, s32[]{:S(2)}) async-start(s8[4718592]{0:T(1024)(128)(4,1)} %bitcast.154), calls=%async_computation.5 | async-start | bytes 1048576
  270.2 15.6 %copy-start.26 = (bf16[1024,768]{1,0:T(8,128)(2,1)S(1)}, bf16[1024,768]{1,0:T(8,128)(2,1)}, u32[]{:S(2)}) copy-start(bf16[1024,768]{1,0:T(8,128)(2,1)} %param.18) | copy-start | bytes 4718596
  285.9 14.5 %copy-start.68 = (bf16[1024,3072]{1,0:T(8,128)(2,1)}, bf16[1024,3072]{1,0:T(8,128)(2,1)S(1)}, u32[]{:S(2)}) copy-start(bf16[1024,3072]{1,0:T(8,128)(2,1)S(1)} %get-tuple-element.212) | copy-start | bytes 18874372
  317.1 10.1 %copy-start.15 = (f32[1024,768]{0,1:T(8,128)S(1)}, f32[1024,768]{0,1:T(8,128)}, u32[]{:S(2)}) copy-start(f32[1024,768]{0,1:T(8,128)} %copy.146) | copy-start | bytes 9437188
  436.3 19.0 %copy-start.8 = (f32[1024,768]{0,1:T(8,128)S(1)}, f32[1024,768]{0,1:T(8,128)}, u32[]{:S(2)}) copy-start(f32[1024,768]{0,1:T(8,128)} %get-tuple-element.155) | copy-start | bytes 9437188
  455.4 15.5 %copy-start.69 = (bf16[1024,3072]{1,0:T(8,128)(2,1)}, bf16[1024,3072]{1,0:T(8,128)(2,1)S(1)}, u32[]{:S(2)}) copy-start(bf16[1024,3072]{1,0:T(8,128)(2,1)S(1)} %get-tuple-element.218) | copy-start | bytes 18874372
  487.8 7.2 %copy-start.53 = (f32[1024]{0:T(1024)S(1)}, f32[1024]{0:T(1024)}, u32[]{:S(2)}) copy-start(f32[1024]{0:T(1024)} %copy-done.52) | copy-start | bytes 12292
  487.8 7.2 %copy-start.16 = (f32[1024,768]{0,1:T(8,128)S(1)}, f32[1024,768]{0,1:T(8,128)}, u32[]{:S(2)}) copy-start(f32[1024,768]{0,1:T(8,128)} %copy.148) | copy-start | bytes 9437188
  588.4 5.7 copy-start.37
  588.4 5.7 copy-start.39
  597.9 5.5 copy-start.47
  597.9 5.5 copy-start.49
  597.9 5.5 copy-start.63
  609.1 6.4 copy-start.51
  621.0 39.0 %copy-start.41 = (f32[24,2304]{1,0:T(8,128)S(1)}, f32[24,2304]{1,0:T(8,128)}, u32[]{:S(2)}) copy-start(f32[24,2304]{1,0:T(8,128)} %get-tuple-element.60) | copy-start | bytes 663556
  (45 other events, 131.9 us)

commit v6 on v5

--- a/solution.py
+++ b/solution.py
@@ -145,6 +145,73 @@
         name="attend_bwd")(fl,qkv,qkv,qkv,do,lse,*host.arrays)
 
 
+def tn(a,b): return lax.dot_general(a,b,(((0,),(0,)),((),())),preferred_element_type=F32)
+
+def feed_fwd_kernel(c_ref,e_ref,eb_ref,s_ref,m_ref,sb_ref,*rest,rows,host):
+    n=host.count
+    h_ref,u_ref,slope_ref=rest[n:n+3]
+    jobs=host.enter(rest[:n],rest[n+3:2*n+3],rest[2*n+3:])
+    N=c_ref.shape[0]
+    e=e_ref[...]; s=s_ref[...]; eb=eb_ref[...]
+    @pl.when(pl.program_id(0)==0)
+    def _(): h_ref[...]=m_ref[...]+sb_ref[...]
+    for j in range(N//rows):
+        host.tick(jobs,j)
+        at=slice(j*rows,(j+1)*rows)
+        u,slope=gelu_pair(nn(c_ref[at,:],e)+eb)
+        u_ref[at,:]=u; slope_ref[at,:]=slope
+        h_ref[at,:]+=nn(u,s)
+    host.leave(jobs)
+
+def feed_fwd(c,w,middle,host,tile=512,rows=256):
+    N,D=c.shape; F=w["expand"].shape[1]
+    fixed=lambda r: pl.BlockSpec((r,D),lambda t: (0,0))
+    return pl.pallas_call(functools.partial(feed_fwd_kernel,rows=rows,host=host),grid=(F//tile,),
+        in_specs=[fixed(N),pl.BlockSpec((D,tile),lambda t:(0,t)),pl.BlockSpec((1,tile),lambda t:(0,t)),
+                  pl.BlockSpec((tile,D),lambda t:(t,0)),fixed(N),fixed(1)]+host.ins,
+        out_specs=[fixed(N)]+[pl.BlockSpec((N,tile),lambda t:(0,t))]*2+host.outs,
+        out_shape=[jax.ShapeDtypeStruct((N,D),F32)]+[jax.ShapeDtypeStruct((N,F),BF)]*2+host.shapes,
+        scratch_shapes=host.scratch,compiler_params=host.params(),
+        cost_estimate=pl.CostEstimate(flops=4*N*D*F,bytes_accessed=4*N*F+4*D*F,transcendentals=N*F),
+        name="feed_fwd")(c,w["expand"],w["eb"][None],w["shrink"],middle,w["sb"][None],*host.arrays)
+
+def feed_bwd_kernel(g_ref,u_ref,slope_ref,c_ref,e_ref,s_ref,*rest,rows,host):
+    n=host.count
+    dc_ref,de_ref,ds_ref,eb_ref=rest[n:n+4]
+    dz_ref=rest[2*n+4]
+    jobs=host.enter(rest[:n],rest[n+4:2*n+4],rest[2*n+5:])
+    N=c_ref.shape[0]
+    e=e_ref[...]; s=s_ref[...]
+    @pl.when(pl.program_id(0)==0)
+    def _(): dc_ref[...]=jnp.zeros_like(dc_ref)
+    total=0.
+    for j in range(N//rows):
+        host.tick(jobs,j)
+        at=slice(j*rows,(j+1)*rows)
+        dz=(nt(g_ref[at,:],s)*slope_ref[at,:].astype(F32)).astype(BF)
+        dz_ref[at,:]=dz
+        total=total+jnp.sum(dz.astype(F32),axis=0,keepdims=True)
+        dc_ref[at,:]+=nt(dz,e)
+    eb_ref[...]=total
+    de_ref[...]=tn(c_ref[...],dz_ref[...]).astype(BF)
+    ds_ref[...]=tn(u_ref[...],g_ref[...]).astype(BF)
+    host.leave(jobs)
+
+def feed_bwd(g,u,slope,c,w,host,tile=512,rows=256):
+    N,D=c.shape; F=u.shape[1]
+    fixed=pl.BlockSpec((N,D),lambda t:(0,0))
+    wide=lambda r: pl.BlockSpec((r,tile),lambda t:(0,t))
+    tall=pl.BlockSpec((tile,D),lambda t:(t,0))
+    return pl.pallas_call(functools.partial(feed_bwd_kernel,rows=rows,host=host),grid=(F//tile,),
+        in_specs=[fixed,wide(N),wide(N),fixed,wide(D),tall]+host.ins,
+        out_specs=[fixed,wide(D),tall,wide(1)]+host.outs,
+        out_shape=[jax.ShapeDtypeStruct((N,D),F32),jax.ShapeDtypeStruct((D,F),BF),
+                   jax.ShapeDtypeStruct((F,D),BF),jax.ShapeDtypeStruct((1,F),F32)]+host.shapes,
+        scratch_shapes=[pltpu.VMEM((N,tile),BF)]+host.scratch,compiler_params=host.params(),
+        cost_estimate=pl.CostEstimate(flops=8*N*D*F,bytes_accessed=4*N*F+8*D*F,transcendentals=0),
+        name="feed_bwd")(g,u,slope,c,w["expand"],w["shrink"],*host.arrays)
+
+
 MESH = pl.DeviceIdType.MESH
 
 
@@ -448,7 +515,7 @@
             return [w.reshape(-1, w.shape[-1]) for w in values]
         if self.used:
             return list(values)
-        return plain(self.kind, self.source)
+        return plain(self.kind, self.source) if self.source else []
 
 
 def plain(kind, arrays):
@@ -529,7 +596,7 @@
                 heads=heads[:, : 3 * width])
 
 
-def forward_use(hidden, w, first_len, host):
+def forward_use(hidden, w, first_len, host, spare_host):
     normed = layer_norm(hidden, w["ga"], w["sa"]).astype(BF)
     bias = jnp.concatenate([w["qb"], jnp.zeros_like(w["qb"]), w["vb"]])
     qkv = (jnp.dot(normed, w["heads"], preferred_element_type=F32) + bias).astype(BF)
@@ -538,22 +605,20 @@
     w.update(expand=more[0], shrink=more[1], mix=more[-1])
     middle = hidden + jnp.dot(attended, w["mix"], preferred_element_type=F32) + w["mb"]
     normed_two = layer_norm(middle, w["gf"], w["sf"]).astype(BF)
-    expanded = jnp.dot(normed_two, w["expand"], preferred_element_type=F32) + w["eb"]
-    activated, slope = gelu_pair(expanded)
-    result = middle + jnp.dot(activated, w["shrink"], preferred_element_type=F32) + w["sb"]
-    return result, (hidden, normed, qkv, attended, lse, middle, normed_two, activated, slope), more[2:-1]
-
-
-def backward_use(grad_out, kept, w, first_len, carried, ident):
+    result, activated, slope, *spare = feed_fwd(normed_two, w, middle, spare_host)
+    kept = (hidden, normed, qkv, attended, lse, middle, normed_two, activated, slope)
+    return result, kept, spare_host.results(spare)
+
+
+def backward_use(grad_out, kept, w, first_len, carried, ident, spare_ident):
     hidden, normed, qkv, attended, lse, middle, normed_two, activated, slope = kept
     count = lax.axis_size(AX)
     grad_low = grad_out.astype(BF)
-    shrink_term = inner_rows(activated, grad_low).astype(BF)
     sb = column_sums(grad_low)
-    dz = (times_transposed(grad_low, w["shrink"]) * slope.astype(F32)).astype(BF)
-    expand_term = inner_rows(normed_two, dz).astype(BF)
-    eb = column_sums(dz)
-    dc = times_transposed(dz, w["expand"])
+    spare = Host(Scatter, carried, spare_ident, FEED_BACKWARD_SLOTS, per=4, axis=0)
+    dc, expand_term, shrink_term, eb, *carried = feed_bwd(grad_low, activated, slope, normed_two, w, spare)
+    carried = spare.results(carried)
+    eb = eb[0]
     unused, norm_back = jax.vjp(layer_norm, middle, w["gf"], w["sf"])
     middle_norm, gf, sf = norm_back(dc)
     dm = grad_out + middle_norm
@@ -561,7 +626,7 @@
     mix_term = inner_rows(attended, dmb).astype(BF)
     mb = column_sums(dmb)
     do = times_transposed(dmb, w["mix"]).astype(BF)
-    host = Host(Scatter, [shrink_term, expand_term] + carried + [mix_term], ident, BACKWARD_SLOTS, per=4)
+    host = Host(Scatter, [shrink_term, expand_term, mix_term], ident, BACKWARD_SLOTS, per=4)
     dq, dk, dv, *more = attend_bwd(qkv, do, lse, first_len, host)
     more = host.results(more)
     dqkv = jnp.concatenate([dq, dk, dv], axis=1)
@@ -572,7 +637,7 @@
     unused, first_back = jax.vjp(layer_norm, hidden, w["ga"], w["sa"])
     hidden_norm, ga, sa = first_back(da)
     small = pack_columns([ga, sa, qb, vb, mb, gf, sf, sb], eb, count)
-    return dm + hidden_norm, more, heads_term, small
+    return dm + hidden_norm, more, heads_term, small, carried
 
 
 def as_shares(shrink, expand, mix, heads, small):
@@ -583,6 +648,8 @@
 
 FORWARD_SLOTS = [0.43, 0.86, 1.29, 1.72] * 6
 BACKWARD_SLOTS = [1.8, 1.35, 0.9, 0.45] * 6
+FEED_FORWARD_SLOTS = [0.6, 0.6, 0.6, 0.6] * 6
+FEED_BACKWARD_SLOTS = [0.6, 0.6, 0.6, 2.9] * 6
 
 
 def pick_shards(stacks, source):
@@ -609,22 +676,23 @@
     ways = shards[0][3].shape[0] // shards[0][0].shape[0]
     (heads,) = exchange(Gather, shards[0][:1], 0, "gather", 4)
     kept, weights = [], []
-    loads = [shards[0][2:] + shards[1][:1] + shards[0][1:2], shards[1][2:] + shards[1][1:2]]
     for i in range(LAYERS):
         weights.append(use_heads(heads, width, ways))
-        host = Host(Gather, loads[i], 1 + i, FORWARD_SLOTS, per=4)
-        hidden, saved, spare = forward_use(hidden, weights[i], first_length, host)
+        host = Host(Gather, shards[i][2:] + shards[i][1:2], 1 + i, FORWARD_SLOTS, per=4)
+        later = shards[i + 1][:1] if i + 1 < LAYERS else []
+        spare_host = Host(Gather, later, 6, FEED_FORWARD_SLOTS, per=4, axis=0)
+        hidden, saved, spare = forward_use(hidden, weights[i], first_length, host, spare_host)
         heads = spare[0] if spare else None
         kept.append(saved)
     grad = cotangent.astype(F32)
-    grad, late, heads_late, small_late = backward_use(
-        grad, kept[1], weights[1], first_length, [], 3)
-    grad, early, heads_early, small_early = backward_use(
-        grad, kept[0], weights[0], first_length, [heads_late], 4)
+    grad, late, heads_late, small_late, unused = backward_use(
+        grad, kept[1], weights[1], first_length, [], 3, None)
+    grad, early, heads_early, small_early, (heads_late,) = backward_use(
+        grad, kept[0], weights[0], first_length, [heads_late], 4, 7)
     heads_early, small = exchange(
         Scatter, [heads_early, jnp.concatenate([small_early, small_late], axis=1)], 5, "scatter", 4)
-    shares = [as_shares(early[0], early[1], early[3], heads_early, small[:, :LANES]),
-              as_shares(*late, early[2], small[:, LANES:])]
+    shares = [as_shares(*early, heads_early, small[:, :LANES]),
+              as_shares(*late, heads_late, small[:, LANES:])]
     return (hidden.astype(BF), grad.astype(BF), *place_terms(sources, shares))
 
 

time: 671 us -> 603 us (0.90)
  matrix products: 196 us -> 55.1 us
  Pallas kernels: 364 us -> 466 us
  local copies, waits for them, and re-layouts: 55 us -> 31.7 us
    pallas_call x0 -> x4, Pallas kernels: none -> 134 us  [the longest x2 67.1 us: feed_fwd(): pl.pallas_call(functools.partial(feed_fwd_kernel, rows=rows, host=host),...]
    dot_general x8 -> x4, matrix products: 69.1 us -> 15.7 us  [times_transposed(): lax.dot_general(left, right, (((1,), (1,)), ((), ())), preferred_element_...]
    dot_general x8 -> x4, matrix products: 63.4 us -> 16.6 us  [inner_rows(): lax.dot_general(left, right, (((0,), (0,)), ((), ())), preferred_element_...]
    dot_general x4 -> x0, matrix products: 43.1 us -> none  [the longest x2 22.8 us: forward_use(): jnp.dot(activated, w['shrink'], preferred_element_type=F32)]
    pallas_call x2, Pallas kernels: 156 us -> 139 us  [attend_bwd(): pl.pallas_call(functools.partial(bwd_kernel, bq=bq, host=host), grid_spec...]
    dot_general x4 -> x0, local copies, waits for them, and re-layouts: 14.5 us -> none  [times_transposed(): lax.dot_general(left, right, (((1,), (1,)), ((), ())), preferred_element_...]
    pallas_call x2, Pallas kernels: 142 us -> 128 us  [attend_fwd(): pl.pallas_call(functools.partial(fwd_kernel, bq=bq, host=host), grid_spec...]
    unnamed x164 -> x106, local copies, waits for them, and re-layouts: 21.2 us -> 13.8 us
where the time goes in v6:
time: 603 us; the launch traced here: 599 us
  Pallas kernels  466 us (77%)
  matrix products  55.1 us (9%)
  other arithmetic  39.7 us (7%)
  local copies, waits for them, and re-layouts  31.7 us (5%)
  between operations  6.39 us (1%)
    pallas_call x2, Pallas kernels, attend_bwd(): pl.pallas_call(functools.partial(bwd_kernel, bq=bq, host=host), grid_spec...  139 us
    pallas_call x2, Pallas kernels, attend_fwd(): pl.pallas_call(functools.partial(fwd_kernel, bq=bq, host=host), grid_spec...  128 us
    pallas_call x2, Pallas kernels, feed_fwd(): pl.pallas_call(functools.partial(feed_fwd_kernel, rows=rows, host=host),...  67.1 us
    pallas_call x2, Pallas kernels, feed_bwd(): pl.pallas_call(functools.partial(feed_bwd_kernel, rows=rows, host=host),...  67.1 us
    pallas_call x2, Pallas kernels, exchange(): pl.pallas_call(functools.partial(alone_kernel, host=host), grid=(1,), in_...  65.7 us
    dot_general x4, matrix products, inner_rows(): lax.dot_general(left, right, (((0,), (0,)), ((), ())), preferred_element_...  16.6 us
    dot_general x2, matrix products, forward_use(): jnp.dot(normed, w['heads'], preferred_element_type=F32) + bias  16.3 us
    dot_general x4, matrix products, times_transposed(): lax.dot_general(left, right, (((1,), (1,)), ((), ())), preferred_element_...  15.7 us

profile of v6, /device:TPU:0, one launch (start us, length us, event | category | flops | bytes accessed | tf_op | source)
XLA Modules:
  0.0 599.3 jit_solution(8335997263929064132)
XLA Ops:
  12.5 30.8 %gather.1 = bf16[2,2,4,2,24,2432]{5,4,3,2,1,0:T(8,128)(2,1)} custom-call(bf16[24,2432]{1,0:T(8,128)(2,1)} %fusion.22.refs_0_), custom_call_target="tpu_custom_call" | custom-call | tf_op jit(solution)/shard_map/gather/pallas_call | solution.py:538
  46.1 8.5 %add_convert_fusion.1.q_ref.k_ref.v_ref = bf16[1024,2304]{1,0:T(8,128)(2,1)} fusion(f32[2304]{0:T(1024)S(1)} %fusion.24, bf16[768,2432]{1,0:T(8,128)(2,1)} %bitcast.104, bf16[1024,768]{1,0:T(8,128)(2,1)S(1)} %copy-done.12, f32[768]{0:T(1024)S(1)} %get-tuple-element.120, f32[768]{0:T(1024)S(1)} %get-tuple-element.121, f32[1024]{0:T(1024)S(1)} %fusion.26, ...), kind=kOutput, calls=%fused_computation.1 | convolution fusion | flops 3633315840 | bytes 9853952 | tf_op jit(solution)/shard_map/dot_general | solution.py:602
  56.7 64.1 %attend_fwd.2 = (bf16[1024,768]{1,0:T(8,128)(2,1)}, f32[6,2,1024]{2,1,0:T(2,128)}, bf16[2,2,4,2,24,3072]{5,4,3,2,1,0:T(8,128)(2,1)}, bf16[2,2,4,2,96,768]{5,4,3,...) custom-call(s32[1]{0:T(128)S(6)} %copy.135.fl_ref, bf16[1024,2304]{1,0:T(8,128)(2,1)} %add_convert_fusion.1.q_ref.k_ref.v_ref, ...), custom_call_target="tpu_custom_call" | custom-call | flops 6442450944 | bytes 6291456 | tf_op jit(solution)/shard_map/attend_fwd/pallas_call | solution.py:70
  120.8 3.3 fusion.72
  124.7 1.7 add_convert_fusion.5.c_ref
  129.6 44.7 %feed_fwd.2 = (f32[1024,768]{1,0:T(8,128)}, bf16[1024,3072]{1,0:T(8,128)(2,1)}, bf16[1024,3072]{1,0:T(8,128)(2,1)}, bf16[2,2,4,2,24,2432]{5,4,3,2,1,0:T(8,128)(2,1)}) custom-call(bf16[1024,768]{1,0:T(8,128)(2,1)} %add_convert_fusion.5.c_ref, bf16[768,3072]{1,0:T(8,128)(2,1)} %bitcast.123, f32[1,3072]{1,0:T(1,128)} %reshape.369.eb_ref, ...), custom_call_target="tpu_custom_call" | custom-call | flops 9663676416 | bytes 22020096 | tf_op jit(solution)/shard_map/feed_fwd/pallas_call | solution.py:169
  175.6 2.1 reduce_sum.287
  178.3 7.9 %add_convert_fusion.q_ref.k_ref.v_ref = bf16[1024,2304]{1,0:T(8,128)(2,1)} fusion(f32[2304]{0:T(1024)S(1)} %fusion.25, bf16[768,2432]{1,0:T(8,128)(2,1)} %bitcast.119, f32[1024,768]{1,0:T(8,128)S(1)} %copy-done.5, f32[768]{0:T(1024)S(1)} %get-tuple-element.113, f32[768]{0:T(1024)S(1)} %get-tuple-element.114, f32[1024]{0:T(1024)S(1)} %fusion.28, ...), kind=kOutput, calls=%fused_computation | convolution fusion | flops 3632529408 | bytes 11426816 | tf_op jit(solution)/shard_map/dot_general | solution.py:602
  186.1 63.5 %attend_fwd.3 = (bf16[1024,768]{1,0:T(8,128)(2,1)}, f32[6,2,1024]{2,1,0:T(2,128)}, bf16[2,2,4,2,24,3072]{5,4,3,2,1,0:T(8,128)(2,1)}, bf16[2,2,4,2,96,768]{5,4,3,...) custom-call(s32[1]{0:T(128)S(6)} %copy.135.fl_ref, bf16[1024,2304]{1,0:T(8,128)(2,1)} %add_convert_fusion.q_ref.k_ref.v_ref, ...), custom_call_target="tpu_custom_call" | custom-call | flops 6442450944 | bytes 6291456 | tf_op jit(solution)/shard_map/attend_fwd/pallas_call | solution.py:70
  249.6 3.3 fusion.73
  254.9 22.4 %feed_fwd.3 = (f32[1024,768]{1,0:T(8,128)S(1)}, bf16[1024,3072]{1,0:T(8,128)(2,1)}, bf16[1024,3072]{1,0:T(8,128)(2,1)}) custom-call(bf16[1024,768]{1,0:T(8,128)(2,1)S(1)} %add_convert_fusion.3.c_ref, bf16[768,3072]{1,0:T(8,128)(2,1)} %bitcast.131, f32[1,3072]{1,0:T(1,128)S(1)} %reshape.377.eb_ref, bf16[3072,768]{1,0:T(8,128)(2,1)} %bitcast.133, ...), custom_call_target="tpu_custom_call" | custom-call | flops 9663676416 | bytes 22020096 | tf_op jit(solution)/shard_map/feed_fwd/pallas_call | solution.py:169
  279.3 26.5 %feed_bwd.2 = (f32[1024,768]{1,0:T(8,128)}, bf16[768,3072]{1,0:T(8,128)(2,1)}, bf16[3072,768]{1,0:T(8,128)(2,1)}, f32[1,3072]{1,0:T(1,128)S(1)}) custom-call(bf16[1024,768]{1,0:T(8,128)(2,1)S(1)} %copy-done, bf16[1024,3072]{1,0:T(8,128)(2,1)} %get-tuple-element.66.u_ref, bf16[1024,3072]{1,0:T(8,128)(2,1)} %get-tuple-element.67.slope_ref, ...), custom_call_target="tpu_custom_call" | custom-call | flops 19327352832 | bytes 31457280 | tf_op jit(solution)/shard_map/feed_bwd/pallas_call | solution.py:205
  305.8 3.0 multiply_reduce_fusion
  308.8 1.9 fusion.70
  312.9 2.6 convolution_convert_fusion.3.do_ref
  315.5 2.5 convolution_convert_fusion.5
  318.0 69.2 %attend_bwd.2 = (bf16[1024,768]{1,0:T(8,128)(2,1)}, bf16[1024,768]{1,0:T(8,128)(2,1)}, bf16[1024,768]{1,0:T(8,128)(2,1)}, f32[96,768]{1,0:T(8,128)}, f32[24,3072]{1,0:T(8,128)}, /*index=5*/f32[24,768]{1,0:T(8,128)}) custom-call(s32[1]{0:T(128)S(6)} %copy.135.fl_ref, bf16[1024,2304]{1,0:T(8,128)(2,1)} %add_convert_fusion.q_ref.k_ref.v_ref, ...), custom_call_target="tpu_custom_call" | custom-call | flops 16106127360 | bytes 12582912 | tf_op jit(solution)/shard_map/attend_bwd/pallas_call | solution.py:137
  391.1 6.4 %multiply_reduce_fusion.1 = (f32[768]{0:T(1024)S(1)}, f32[1024]{0:T(1024)S(1)}, f32[768]{0:T(1024)S(1)}, f32[1024,768]{1,0:T(8,128)S(1)}) fusion(f32[1024,768]{1,0:T(8,128)S(1)} %copy-done.6, f32[1024]{0:T(1024)S(1)} %fusion.28, f32[1024]{0:T(1024)S(1)} %broadcast_multiply_fusion.1, f32[768]{0:T(1024)S(1)} %get-tuple-element.114, ...), kind=kOutput, calls=%fused_computation.29 | convolution fusion | flops 3630167552 | bytes 14570496 | tf_op jit(solution)/shard_map/dot_general | solution.py:555
  399.5 2.7 convert_reduce_fusion.5
  402.2 5.8 convolution_convert_fusion.1
  408.0 40.6 %feed_bwd.3 = (f32[1024,768]{1,0:T(8,128)}, bf16[768,3072]{1,0:T(8,128)(2,1)}, bf16[3072,768]{1,0:T(8,128)(2,1)}, f32[1,3072]{1,0:T(1,128)}, f32[24,2304]{1,0:T(8,128)}) custom-call(bf16[1024,768]{1,0:T(8,128)(2,1)} %get-tuple-element.141.g_ref, bf16[1024,3072]{1,0:T(8,128)(2,1)} %get-tuple-element.75.u_ref, bf16[1024,3072]{1,0:T(8,128)(2,1)} %get-tuple-element.76.slope_ref, ...), custom_call_target="tpu_custom_call" | custom-call | flops 19327352832 | bytes 31457280 | tf_op jit(solution)/shard_map/feed_bwd/pallas_call | solution.py:205
  448.7 3.1 multiply_reduce_fusion.2
  451.8 1.7 fusion.68
  455.9 2.6 convolution_convert_fusion.2.do_ref
  458.4 2.5 convolution_convert_fusion.4
  460.9 69.6 %attend_bwd.3 = (bf16[1024,768]{1,0:T(8,128)(2,1)}, bf16[1024,768]{1,0:T(8,128)(2,1)}, bf16[1024,768]{1,0:T(8,128)(2,1)}, f32[96,768]{1,0:T(8,128)}, f32[24,3072]{1,0:T(8,128)}, /*index=5*/f32[24,768]{1,0:T(8,128)}) custom-call(s32[1]{0:T(128)S(6)} %copy.135.fl_ref, bf16[1024,2304]{1,0:T(8,128)(2,1)} %add_convert_fusion.1.q_ref.k_ref.v_ref, ...), custom_call_target="tpu_custom_call" | custom-call | flops 16106127360 | bytes 12582912 | tf_op jit(solution)/shard_map/attend_bwd/pallas_call | solution.py:137
  535.1 4.1 fusion.65
  539.2 1.7 fusion.8
  541.0 2.4 add_convert_fusion.2
  543.5 5.8 convolution_convert_fusion
  554.3 34.9 %scatter.1 = (f32[24,2304]{1,0:T(8,128)}, f32[24,256]{1,0:T(8,128)}) custom-call(bf16[2,2,4,2,24,2304]{5,4,3,2,1,0:T(8,128)(2,1)} %bitcast.106, f32[2,2,4,2,24,256]{5,4,3,2,1,0:T(8,128)} %bitcast.107), custom_call_target="tpu_custom_call" | custom-call | tf_op jit(solution)/shard_map/scatter/pallas_call | solution.py:538
  592.6 2.0 select_add_fusion.2
  (233 shorter events, 49.1 us)
Async XLA Ops:
  0.6 44.5 %copy-start.12 = (bf16[1024,768]{1,0:T(8,128)(2,1)S(1)}, bf16[1024,768]{1,0:T(8,128)(2,1)}, u32[]{:S(2)}) copy-start(bf16[1024,768]{1,0:T(8,128)(2,1)} %param.17) | copy-start | bytes 4718596
  44.4 10.1 %copy-start.36 = (f32[768]{0:T(1024)}, f32[768]{0:T(1024)S(1)}, u32[]{:S(2)}) copy-start(f32[768]{0:T(1024)S(1)} %get-tuple-element.121) | copy-start | bytes 9220
  44.4 10.1 %copy-start.44 = (f32[768]{0:T(1024)}, f32[768]{0:T(1024)S(1)}, u32[]{:S(2)}) copy-start(f32[768]{0:T(1024)S(1)} %get-tuple-element.120) | copy-start | bytes 9220
  45.4 9.1 %copy-start.34 = (f32[1024]{0:T(1024)}, f32[1024]{0:T(1024)S(1)}, u32[]{:S(2)}) copy-start(f32[1024]{0:T(1024)S(1)} %broadcast_multiply_fusion.3) | copy-start | bytes 12292
  46.0 8.5 %copy-start.40 = (f32[1024]{0:T(1024)}, f32[1024]{0:T(1024)S(1)}, u32[]{:S(2)}) copy-start(f32[1024]{0:T(1024)S(1)} %fusion.9) | copy-start | bytes 12292
  46.1 8.5 %copy-start.38 = (f32[1024]{0:T(1024)}, f32[1024]{0:T(1024)S(1)}, u32[]{:S(2)}) copy-start(f32[1024]{0:T(1024)S(1)} %fusion.26) | copy-start | bytes 12292
  46.1 8.5 %copy-start.30 = (bf16[4,24,3072]{2,1,0:T(8,128)(2,1)S(1)}, bf16[4,24,3072]{2,1,0:T(8,128)(2,1)}, u32[]{:S(2)}) copy-start(bf16[4,24,3072]{2,1,0:T(8,128)(2,1)} %param.30) | copy-start | bytes 1769476
  46.1 9.3 %copy-start.31 = (bf16[4,96,768]{2,1,0:T(8,128)(2,1)S(1)}, bf16[4,96,768]{2,1,0:T(8,128)(2,1)}, u32[]{:S(2)}) copy-start(bf16[4,96,768]{2,1,0:T(8,128)(2,1)} %param.32) | copy-start | bytes 1769476
  46.1 10.0 %copy-start.42 = (bf16[4,24,768]{2,1,0:T(8,128)(2,1)S(1)}, bf16[4,24,768]{2,1,0:T(8,128)(2,1)}, u32[]{:S(2)}) copy-start(bf16[4,24,768]{2,1,0:T(8,128)(2,1)} %param.26) | copy-start | bytes 442372
  56.7 64.1 %copy-start.13 = (bf16[1024,768]{1,0:T(8,128)(2,1)S(1)}, bf16[1024,768]{1,0:T(8,128)(2,1)}, u32[]{:S(2)}) copy-start(bf16[1024,768]{1,0:T(8,128)(2,1)} %param.17) | copy-start | bytes 4718596
  174.3 3.4 copy-start.5
  279.3 26.5 %copy-start.4 = (f32[1024,768]{1,0:T(8,128)S(1)}, f32[1024,768]{1,0:T(8,128)}, u32[]{:S(2)}) copy-start(f32[1024,768]{1,0:T(8,128)} %copy-done.3) | copy-start | bytes 9437188
  305.8 3.0 copy-start.16
  312.9 2.6 copy-start.48
  408.0 40.6 %copy-start.2 = (f32[1024,768]{1,0:T(8,128)S(1)}, f32[1024,768]{1,0:T(8,128)}, u32[]{:S(2)}) copy-start(f32[1024,768]{1,0:T(8,128)} %copy-done.1) | copy-start | bytes 9437188
  448.7 3.1 copy-start.15
  455.9 2.6 copy-start.49
  532.4 2.6 copy-start.22
  532.4 2.6 copy-start.35
  532.4 2.6 copy-start.37
  535.1 4.1 copy-start.41
  535.1 4.1 copy-start.39
  543.5 5.8 copy-start.18
  549.2 2.5 copy-start.20
  549.3 2.8 copy-start.43
  553.1 39.4 %copy-start.29 = (f32[24,2304]{1,0:T(8,128)S(1)}, f32[24,2304]{1,0:T(8,128)}, u32[]{:S(2)}) copy-start(f32[24,2304]{1,0:T(8,128)} %get-tuple-element.88) | copy-start | bytes 663556
  554.3 40.3 %copy-start.32 = (f32[24,768]{1,0:T(8,128)S(1)}, f32[24,768]{1,0:T(8,128)}, u32[]{:S(2)}) copy-start(f32[24,768]{1,0:T(8,128)} %get-tuple-element.90) | copy-start | bytes 221188
  554.3 40.3 %copy-start.33 = (f32[24,768]{1,0:T(8,128)S(1)}, f32[24,768]{1,0:T(8,128)}, u32[]{:S(2)}) copy-start(f32[24,768]{1,0:T(8,128)} %get-tuple-element.89) | copy-start | bytes 221188
  554.3 41.1 %copy-start.26 = (f32[24,3072]{1,0:T(8,128)S(1)}, f32[24,3072]{1,0:T(8,128)}, u32[]{:S(2)}) copy-start(f32[24,3072]{1,0:T(8,128)} %get-tuple-element.92) | copy-start | bytes 884740
  554.3 41.1 %copy-start.28 = (f32[24,3072]{1,0:T(8,128)S(1)}, f32[24,3072]{1,0:T(8,128)}, u32[]{:S(2)}) copy-start(f32[24,3072]{1,0:T(8,128)} %get-tuple-element.91) | copy-start | bytes 884740
  554.3 43.5 %copy-start.25 = (f32[96,768]{1,0:T(8,128)S(1)}, f32[96,768]{1,0:T(8,128)}, u32[]{:S(2)}) copy-start(f32[96,768]{1,0:T(8,128)} %get-tuple-element.94) | copy-start | bytes 884740
  554.3 43.5 %copy-start.27 = (f32[96,768]{1,0:T(8,128)S(1)}, f32[96,768]{1,0:T(8,128)}, u32[]{:S(2)}) copy-start(f32[96,768]{1,0:T(8,128)} %get-tuple-element.93) | copy-start | bytes 884740
  (18 other events, 35.8 us)

commit v7 on v6

--- a/solution.py
+++ b/solution.py
@@ -23,11 +23,20 @@
     z=jnp.zeros_like(x)
     return jnp.where(lane<64,x,z), jnp.where(lane<64,z,x)
 
-def fwd_kernel(fl_ref,q_ref,k_ref,v_ref,*rest,bq,host):
+def fwd_kernel(fl_ref,hid_ref,ga_ref,sa_ref,wq_ref,wk_ref,wv_ref,qb_ref,vb_ref,*rest,bq,host):
     n=host.count
-    o_ref,lse_ref=rest[n:n+2]
-    jobs=host.enter(rest[:n],rest[n+2:2*n+2],rest[2*n+2:])
+    q_ref,k_ref,v_ref,normed_ref,o_ref,lse_ref=rest[n:n+6]
+    jobs=host.enter(rest[:n],rest[n+6:2*n+6],rest[2*n+6:])
     L=q_ref.shape[0]; half=L//2
+    @pl.when(pl.program_id(1)==0)
+    def _():
+        for lo in range(0,L,bq):
+            normed_ref[lo:lo+bq,:]=layer_norm(hid_ref[lo:lo+bq,:],ga_ref[...],sa_ref[...]).astype(BF)
+    w=jnp.concatenate([wq_ref[...],wk_ref[...],wv_ref[...]],axis=1)
+    qkv=nn(normed_ref[...],w)
+    q_ref[...]=(qkv[:,:128]+qb_ref[...]).astype(BF)
+    k_ref[...]=qkv[:,128:256].astype(BF)
+    v_ref[...]=(qkv[:,256:]+vb_ref[...]).astype(BF)
     second=fl_ref[pl.program_id(0)]<L
     shut=jnp.where(second,F32(1e9),F32(0.))
     q=q_ref[...]*BF(0.125); k=k_ref[...]; vT=v_ref[...].T
@@ -65,26 +74,29 @@
         o_ref[lo:hi,:]=acc.T.astype(BF)
     host.leave(jobs)
 
-def attend_fwd(qkv,fl,host,bq=256):
-    N,C=qkv.shape; R=fl.shape[0]; L=N//R; D=C//3; G=D//128
+def attend_fwd(hidden,w,fl,host,bq=256):
+    N,D=hidden.shape; R=fl.shape[0]; L=N//R; G=D//128
+    col=lambda off: pl.BlockSpec((D,128),lambda r,g,fl:(0,off*G+g))
+    blk=pl.BlockSpec((L,128),lambda r,g,fl:(r,g))
+    row=pl.BlockSpec((L,D),lambda r,g,fl:(r,0))
+    vec=pl.BlockSpec((1,D),lambda r,g,fl:(0,0)); part=pl.BlockSpec((1,128),lambda r,g,fl:(0,g))
+    narrow=jax.ShapeDtypeStruct((N,D),BF)
     return pl.pallas_call(functools.partial(fwd_kernel,bq=bq,host=host),
         grid_spec=pltpu.PrefetchScalarGridSpec(num_scalar_prefetch=1,grid=(R,G),
-          in_specs=[pl.BlockSpec((L,128),lambda r,g,fl:(r,g)),
-                    pl.BlockSpec((L,128),lambda r,g,fl:(r,G+g)),
-                    pl.BlockSpec((L,128),lambda r,g,fl:(r,2*G+g))]+host.ins,
-          out_specs=[pl.BlockSpec((L,128),lambda r,g,fl:(r,g)),
-                     pl.BlockSpec((1,2,L),lambda r,g,fl:(r*G+g,0,0))]+host.outs,
+          in_specs=[row,vec,vec,col(0),col(1),col(2),part,part]+host.ins,
+          out_specs=[blk,blk,blk,row,blk,pl.BlockSpec((1,2,L),lambda r,g,fl:(r*G+g,0,0))]+host.outs,
           scratch_shapes=host.scratch),
-        out_shape=[jax.ShapeDtypeStruct((N,D),BF),jax.ShapeDtypeStruct((R*G,2,L),F32)]+host.shapes,
+        out_shape=[narrow]*5+[jax.ShapeDtypeStruct((R*G,2,L),F32)]+host.shapes,
         compiler_params=host.params(),
-        cost_estimate=pl.CostEstimate(flops=2*2*R*L*L*D*2,bytes_accessed=N*D*8,transcendentals=R*L*L*12//2),
-        name="attend_fwd")(fl,qkv,qkv,qkv,*host.arrays)
-
-def bwd_kernel(fl_ref,q_ref,k_ref,v_ref,do_ref,lse_ref,*rest,bq,host):
+        cost_estimate=pl.CostEstimate(flops=2*2*R*L*L*D*2+6*N*D*D,bytes_accessed=N*D*14,transcendentals=R*L*L*12//2),
+        name="attend_fwd")(fl,hidden,w["ga"][None],w["sa"][None],w["heads"],w["heads"],w["heads"],
+                           w["qb"][None],w["vb"][None],*host.arrays)
+
+def bwd_kernel(fl_ref,q_ref,k_ref,v_ref,do_ref,lse_ref,normed_ref,wq_ref,wk_ref,wv_ref,*rest,bq,host):
     n=host.count
-    dq_ref,dk_ref,dv_ref=rest[n:n+3]
-    dk_acc,dv_acc=rest[2*n+3:2*n+5]
-    jobs=host.enter(rest[:n],rest[n+3:2*n+3],rest[2*n+5:])
+    gq_ref,gk_ref,gv_ref,da_ref,qb_ref,vb_ref=rest[n:n+6]
+    dk_acc,dv_acc,dqkv=rest[2*n+6:2*n+9]
+    jobs=host.enter(rest[:n],rest[n+6:2*n+6],rest[2*n+9:])
     L=q_ref.shape[0]; half=L//2
     second=fl_ref[pl.program_id(0)]<L
     shut=jnp.where(second,F32(1e9),F32(0.))
@@ -127,22 +139,38 @@
             dk_acc[...]=dkp; dv_acc[...]=dvp
         else:
             dk_acc[:hi]+=dkp; dv_acc[:hi]+=dvp
-        dq_ref[lo:hi,:]=(dqT.T*0.125).astype(BF)
-    dk_ref[...]=dk_acc[...].astype(BF); dv_ref[...]=dv_acc[...].astype(BF)
+        dqkv[lo:hi,:128]=(dqT.T*0.125).astype(BF)
+    dqkv[:,128:256]=dk_acc[...].astype(BF); dqkv[:,256:]=dv_acc[...].astype(BF)
+    d=dqkv[...]
+    qb_ref[0]=jnp.sum(d[:,:128].astype(F32),axis=0,keepdims=True)
+    vb_ref[0]=jnp.sum(d[:,256:].astype(F32),axis=0,keepdims=True)
+    terms=tn(normed_ref[...],d).astype(BF)
+    gq_ref[0]=terms[:,:128]; gk_ref[0]=terms[:,128:256]; gv_ref[0]=terms[:,256:]
+    da=nt(d,jnp.concatenate([wq_ref[...],wk_ref[...],wv_ref[...]],axis=1))
+    @pl.when(pl.program_id(1)==0)
+    def _(): da_ref[...]=da
+    @pl.when(pl.program_id(1)>0)
+    def _(): da_ref[...]+=da
     host.leave(jobs)
 
-def attend_bwd(qkv,do,lse,fl,host,bq=256):
-    N,C=qkv.shape; R=fl.shape[0]; L=N//R; D=C//3; G=D//128
-    blk=lambda off: pl.BlockSpec((L,128),lambda r,g,fl:(r,off*G+g))
-    return pl.pallas_call(functools.partial(bwd_kernel,bq=bq,host=host),
+def attend_bwd(q,k,v,do,lse,normed,w,fl,host,bq=256):
+    N,D=q.shape; R=fl.shape[0]; L=N//R; G=D//128
+    blk=pl.BlockSpec((L,128),lambda r,g,fl:(r,g))
+    row=pl.BlockSpec((L,D),lambda r,g,fl:(r,0))
+    col=lambda off: pl.BlockSpec((D,128),lambda r,g,fl:(0,off*G+g))
+    term=pl.BlockSpec((1,D,128),lambda r,g,fl:(r,0,g)); part=pl.BlockSpec((1,1,128),lambda r,g,fl:(r,0,g))
+    gq,gk,gv,da,qb,vb,*more=pl.pallas_call(functools.partial(bwd_kernel,bq=bq,host=host),
         grid_spec=pltpu.PrefetchScalarGridSpec(num_scalar_prefetch=1,grid=(R,G),
-          in_specs=[blk(0),blk(1),blk(2),blk(0),pl.BlockSpec((1,2,L),lambda r,g,fl:(r*G+g,0,0))]+host.ins,
-          out_specs=[blk(0),blk(0),blk(0)]+host.outs,
-          scratch_shapes=[pltpu.VMEM((L,128),F32),pltpu.VMEM((L,128),F32)]+host.scratch),
-        out_shape=[jax.ShapeDtypeStruct((N,D),BF)]*3+host.shapes,
+          in_specs=[blk]*4+[pl.BlockSpec((1,2,L),lambda r,g,fl:(r*G+g,0,0)),row,col(0),col(1),col(2)]+host.ins,
+          out_specs=[term]*3+[row,part,part]+host.outs,
+          scratch_shapes=[pltpu.VMEM((L,128),F32),pltpu.VMEM((L,128),F32),pltpu.VMEM((L,384),BF)]+host.scratch),
+        out_shape=[jax.ShapeDtypeStruct((R,D,D),BF)]*3+[jax.ShapeDtypeStruct((N,D),F32)]
+          +[jax.ShapeDtypeStruct((R,1,D),F32)]*2+host.shapes,
         compiler_params=host.params(),
-        cost_estimate=pl.CostEstimate(flops=5*2*R*L*L*D*2,bytes_accessed=N*D*16,transcendentals=R*L*L*12//2),
-        name="attend_bwd")(fl,qkv,qkv,qkv,do,lse,*host.arrays)
+        cost_estimate=pl.CostEstimate(flops=5*2*R*L*L*D*2+12*N*D*D,bytes_accessed=N*D*16,transcendentals=R*L*L*12//2),
+        name="attend_bwd")(fl,q,k,v,do,lse,normed,w["heads"],w["heads"],w["heads"],*host.arrays)
+    gq,gk,gv=[t[0] if R==1 else jnp.sum(t.astype(F32),axis=0).astype(BF) for t in (gq,gk,gv)]
+    return [gq,gk,gv],da,jnp.sum(qb,axis=(0,1)),jnp.sum(vb,axis=(0,1)),more
 
 
 def tn(a,b): return lax.dot_general(a,b,(((0,),(0,)),((),())),preferred_element_type=F32)
@@ -374,6 +402,12 @@
                 self.copy(k).wait_send()
 
 
+RATES = {"c": 500e3, "z": 78e3, "x": 83e3}
+DELAY = 2.0
+ENTRY = 0.0
+COST = {Gather: 0.1, Scatter: 0.2}
+
+
 def cut_jobs(arrays, kind, pieces):
     jobs = []
     for i, a in enumerate(arrays):
@@ -398,19 +432,19 @@
         if step < len(kind.LINKS):
             for link, blocks, counts in kind.LINKS[step]:
                 name = names[link]
-                rate = {"c": 500e3, "z": 78e3}.get(name, 83e3)
+                rate = RATES.get(name, RATES["x"])
                 free[name] = max(free[name], now) + blocks * rows[array] * width * 2 / rate
                 if counts:
                     done = max(done, free[name])
         if step < kind.STEPS - 1:
-            ready[i, step + 1] = done + 1.8
+            ready[i, step + 1] = done + DELAY
         if step == 1 and i + window < len(jobs):
             ready[i + window, 0] = now
 
     for i in range(min(window, len(jobs))):
         ready[i, 0] = 0.0
-    now, plan = 0.0, []
-    cost = 0.1 if kind is Gather else 0.5
+    now, plan = ENTRY, []
+    cost = COST[kind]
     for length in slots:
         todo = []
         while True:
@@ -593,20 +627,17 @@
     vecs, wide = unpack_columns(heads[:, 3 * width :], 8, ways, lax.axis_size(AX))
     vecs = [v.astype(F32) for v in vecs]
     return dict(zip(("ga", "sa", "qb", "vb", "mb", "gf", "sf", "sb"), vecs), eb=wide.astype(F32),
-                heads=heads[:, : 3 * width])
+                heads=heads)
 
 
 def forward_use(hidden, w, first_len, host, spare_host):
-    normed = layer_norm(hidden, w["ga"], w["sa"]).astype(BF)
-    bias = jnp.concatenate([w["qb"], jnp.zeros_like(w["qb"]), w["vb"]])
-    qkv = (jnp.dot(normed, w["heads"], preferred_element_type=F32) + bias).astype(BF)
-    attended, lse, *more = attend_fwd(qkv, first_len, host)
+    q, k, v, normed, attended, lse, *more = attend_fwd(hidden, w, first_len, host)
     more = host.results(more)
     w.update(expand=more[0], shrink=more[1], mix=more[-1])
     middle = hidden + jnp.dot(attended, w["mix"], preferred_element_type=F32) + w["mb"]
     normed_two = layer_norm(middle, w["gf"], w["sf"]).astype(BF)
     result, activated, slope, *spare = feed_fwd(normed_two, w, middle, spare_host)
-    kept = (hidden, normed, qkv, attended, lse, middle, normed_two, activated, slope)
+    kept = (hidden, normed, (q, k, v), attended, lse, middle, normed_two, activated, slope)
     return result, kept, spare_host.results(spare)
 
 
@@ -615,7 +646,7 @@
     count = lax.axis_size(AX)
     grad_low = grad_out.astype(BF)
     sb = column_sums(grad_low)
-    spare = Host(Scatter, carried, spare_ident, FEED_BACKWARD_SLOTS, per=4, axis=0)
+    spare = Host(Scatter, carried, spare_ident, FEED_BACKWARD_SLOTS, per=4, axis=0, pieces=2, window=2)
     dc, expand_term, shrink_term, eb, *carried = feed_bwd(grad_low, activated, slope, normed_two, w, spare)
     carried = spare.results(carried)
     eb = eb[0]
@@ -626,30 +657,27 @@
     mix_term = inner_rows(attended, dmb).astype(BF)
     mb = column_sums(dmb)
     do = times_transposed(dmb, w["mix"]).astype(BF)
-    host = Host(Scatter, [shrink_term, expand_term, mix_term], ident, BACKWARD_SLOTS, per=4)
-    dq, dk, dv, *more = attend_bwd(qkv, do, lse, first_len, host)
+    host = Host(Scatter, [shrink_term, mix_term, expand_term], ident, BACKWARD_SLOTS, per=4,
+                pieces=8, window=3)
+    heads_terms, da, qb, vb, more = attend_bwd(*qkv, do, lse, normed, w, first_len, host)
     more = host.results(more)
-    dqkv = jnp.concatenate([dq, dk, dv], axis=1)
-    heads_term = inner_rows(normed, dqkv).astype(BF)
-    qb = column_sums(dq)
-    vb = column_sums(dv)
-    da = times_transposed(dqkv, w["heads"])
     unused, first_back = jax.vjp(layer_norm, hidden, w["ga"], w["sa"])
     hidden_norm, ga, sa = first_back(da)
     small = pack_columns([ga, sa, qb, vb, mb, gf, sf, sb], eb, count)
-    return dm + hidden_norm, more, heads_term, small, carried
-
-
-def as_shares(shrink, expand, mix, heads, small):
-    vecs, wide = unpack_columns(small, 8, shrink.shape[0] // heads.shape[0], 1)
+    return dm + hidden_norm, more, heads_terms, small, carried
+
+
+def as_shares(shrink, mix, expand, heads, small):
+    heads = jnp.concatenate(heads, axis=1)
+    vecs, wide = unpack_columns(small, 8, shrink.shape[0] // mix.shape[0], 1)
     ga, sa, qb, vb, mb, gf, sf, sb = vecs
     return ga, sa, heads, qb, vb, mix, mb, gf, sf, expand, wide, shrink, sb
 
 
-FORWARD_SLOTS = [0.43, 0.86, 1.29, 1.72] * 6
-BACKWARD_SLOTS = [1.8, 1.35, 0.9, 0.45] * 6
-FEED_FORWARD_SLOTS = [0.6, 0.6, 0.6, 0.6] * 6
-FEED_BACKWARD_SLOTS = [0.6, 0.6, 0.6, 2.9] * 6
+FORWARD_SLOTS = [1.6, 0.86, 1.29, 1.72] * 6
+BACKWARD_SLOTS = [1.8, 1.35, 0.9, 2.9] * 6
+FEED_FORWARD_SLOTS = [0.95, 0.95, 0.95, 0.95] * 6
+FEED_BACKWARD_SLOTS = [0.7, 0.7, 0.7, 2.3] * 6
 
 
 def pick_shards(stacks, source):
@@ -678,19 +706,19 @@
     kept, weights = [], []
     for i in range(LAYERS):
         weights.append(use_heads(heads, width, ways))
-        host = Host(Gather, shards[i][2:] + shards[i][1:2], 1 + i, FORWARD_SLOTS, per=4)
+        host = Host(Gather, shards[i][2:] + shards[i][1:2], 1 + i, FORWARD_SLOTS, per=4, pieces=4, window=12)
         later = shards[i + 1][:1] if i + 1 < LAYERS else []
-        spare_host = Host(Gather, later, 6, FEED_FORWARD_SLOTS, per=4, axis=0)
+        spare_host = Host(Gather, later, 6, FEED_FORWARD_SLOTS, per=4, axis=0, pieces=5, window=4)
         hidden, saved, spare = forward_use(hidden, weights[i], first_length, host, spare_host)
         heads = spare[0] if spare else None
         kept.append(saved)
     grad = cotangent.astype(F32)
     grad, late, heads_late, small_late, unused = backward_use(
         grad, kept[1], weights[1], first_length, [], 3, None)
-    grad, early, heads_early, small_early, (heads_late,) = backward_use(
-        grad, kept[0], weights[0], first_length, [heads_late], 4, 7)
-    heads_early, small = exchange(
-        Scatter, [heads_early, jnp.concatenate([small_early, small_late], axis=1)], 5, "scatter", 4)
+    grad, early, heads_early, small_early, heads_late = backward_use(
+        grad, kept[0], weights[0], first_length, heads_late, 4, 7)
+    *heads_early, small = exchange(
+        Scatter, heads_early + [jnp.concatenate([small_early, small_late], axis=1)], 5, "scatter", 3)
     shares = [as_shares(*early, heads_early, small[:, :LANES]),
               as_shares(*late, heads_late, small[:, LANES:])]
     return (hidden.astype(BF), grad.astype(BF), *place_terms(sources, shares))

time: 603 us -> 560 us (0.929)
  matrix products: 55.1 us -> 16.6 us
  Pallas kernels: 466 us -> 452 us
  other arithmetic: 39.7 us -> 53.7 us
    dot_general x2 -> x0, matrix products: 16.3 us -> none  [forward_use(): jnp.dot(normed, w['heads'], preferred_element_type=F32) + bias]
    dot_general x4 -> x2, matrix products: 16.6 us -> 4.94 us  [inner_rows(): lax.dot_general(left, right, (((0,), (0,)), ((), ())), preferred_element_...]
    dot_general x4 -> x2, matrix products: 15.7 us -> 5.13 us  [times_transposed(): lax.dot_general(left, right, (((1,), (1,)), ((), ())), preferred_element_...]
    pallas_call x2, Pallas kernels: 67.1 us -> 58.1 us  [feed_fwd(): pl.pallas_call(functools.partial(feed_fwd_kernel, rows=rows, host=host),...]
    unnamed x106 -> x76, local copies, waits for them, and re-layouts: 13.8 us -> 5.58 us
    reduce_sum x3 -> x5, other arithmetic: 7.78 us -> 14 us  [layer_norm(): return centre * lax.rsqrt(spread + EPS) * gain + shift]
where the time goes in v7:
time: 560 us; the launch traced here: 556 us
  Pallas kernels  452 us (81%)
  other arithmetic  53.7 us (10%)
  local copies, waits for them, and re-layouts  28 us (5%)
  matrix products  16.6 us (3%)
  between operations  6.19 us (1%)
    pallas_call x2, Pallas kernels, attend_bwd(): pl.pallas_call(functools.partial(bwd_kernel, bq=bq, host=host), grid_spec...  140 us
    pallas_call x2, Pallas kernels, attend_fwd(): pl.pallas_call(functools.partial(fwd_kernel, bq=bq, host=host), grid_spec...  128 us
    pallas_call x2, Pallas kernels, feed_bwd(): pl.pallas_call(functools.partial(feed_bwd_kernel, rows=rows, host=host),...  62.8 us
    pallas_call x2, Pallas kernels, exchange(): pl.pallas_call(functools.partial(alone_kernel, host=host), grid=(1,), in_...  62.5 us
    pallas_call x2, Pallas kernels, feed_fwd(): pl.pallas_call(functools.partial(feed_fwd_kernel, rows=rows, host=host),...  58.1 us
    reduce_sum x5, other arithmetic, layer_norm(): return centre * lax.rsqrt(spread + EPS) * gain + shift  14 us

profile of v7, /device:TPU:0, one launch (start us, length us, event | category | flops | bytes accessed | tf_op | source)
XLA Modules:
  0.0 556.3 jit_solution(15915274671461378092)
XLA Ops:
  0.7 1.4 fusion.39
  12.5 30.8 %gather.1 = bf16[2,2,4,2,24,2432]{5,4,3,2,1,0:T(8,128)(2,1)} custom-call(bf16[24,2432]{1,0:T(8,128)(2,1)} %fusion.4.refs_0_), custom_call_target="tpu_custom_call" | custom-call | tf_op jit(solution)/shard_map/gather/pallas_call | solution.py:572
  45.8 2.0 convert_element_type.146.hid_ref
  51.0 1.7 dynamic-slice_bitcast_fusion.1
  52.7 1.7 dynamic-slice_bitcast_fusion
  55.0 64.9 %attend_fwd.2 = (bf16[1024,768]{1,0:T(8,128)(2,1)}, bf16[1024,768]{1,0:T(8,128)(2,1)}, bf16[1024,768]{1,0:T(8,128)(2,1)}, bf16[1024,768]{1,0:T(8,128)(2,1)}, bf1...) custom-call(s32[1]{0:T(128)S(6)} %copy.153.fl_ref, ...), custom_call_target="tpu_custom_call" | custom-call | flops 10066329600 | bytes 11010048 | tf_op jit(solution)/shard_map/attend_fwd/pallas_call | solution.py:84
  120.0 3.3 fusion.40
  123.8 1.7 add_convert_fusion.2.c_ref
  129.2 35.6 %feed_fwd.2 = (f32[1024,768]{1,0:T(8,128)}, bf16[1024,3072]{1,0:T(8,128)(2,1)}, bf16[1024,3072]{1,0:T(8,128)(2,1)}, bf16[2,2,4,2,24,2432]{5,4,3,2,1,0:T(8,128)(2,1)}) custom-call(bf16[1024,768]{1,0:T(8,128)(2,1)} %add_convert_fusion.2.c_ref, bf16[768,3072]{1,0:T(8,128)(2,1)} %bitcast.143, f32[1,3072]{1,0:T(1,128)} %reshape.355.eb_ref, ...), custom_call_target="tpu_custom_call" | custom-call | flops 9663676416 | bytes 22020096 | tf_op jit(solution)/shard_map/feed_fwd/pallas_call | solution.py:197
  169.4 63.5 %attend_fwd.3 = (bf16[1024,768]{1,0:T(8,128)(2,1)}, bf16[1024,768]{1,0:T(8,128)(2,1)}, bf16[1024,768]{1,0:T(8,128)(2,1)}, bf16[1024,768]{1,0:T(8,128)(2,1)}, bf1...) custom-call(s32[1]{0:T(128)S(6)} %copy.153.fl_ref, ...), custom_call_target="tpu_custom_call" | custom-call | flops 10066329600 | bytes 11010048 | tf_op jit(solution)/shard_map/attend_fwd/pallas_call | solution.py:84
  232.9 3.3 fusion.41
  238.5 22.4 %feed_fwd.3 = (f32[1024,768]{1,0:T(8,128)S(1)}, bf16[1024,3072]{1,0:T(8,128)(2,1)}, bf16[1024,3072]{1,0:T(8,128)(2,1)}) custom-call(bf16[1024,768]{1,0:T(8,128)(2,1)S(1)} %add_convert_fusion.1.c_ref, bf16[768,3072]{1,0:T(8,128)(2,1)} %bitcast.149, f32[1,3072]{1,0:T(1,128)S(1)} %reshape.359.eb_ref, bf16[3072,768]{1,0:T(8,128)(2,1)} %bitcast.151, ...), custom_call_target="tpu_custom_call" | custom-call | flops 9663676416 | bytes 22020096 | tf_op jit(solution)/shard_map/feed_fwd/pallas_call | solution.py:197
  263.0 27.0 %feed_bwd.2 = (f32[1024,768]{1,0:T(8,128)}, bf16[768,3072]{1,0:T(8,128)(2,1)}, bf16[3072,768]{1,0:T(8,128)(2,1)}, f32[1,3072]{1,0:T(1,128)S(1)}) custom-call(bf16[1024,768]{1,0:T(8,128)(2,1)S(1)} %copy-done, bf16[1024,3072]{1,0:T(8,128)(2,1)} %get-tuple-element.84.u_ref, bf16[1024,3072]{1,0:T(8,128)(2,1)} %get-tuple-element.85.slope_ref, ...), custom_call_target="tpu_custom_call" | custom-call | flops 19327352832 | bytes 31457280 | tf_op jit(solution)/shard_map/feed_bwd/pallas_call | solution.py:233
  290.0 2.9 multiply_reduce_fusion
  296.5 2.6 convolution_convert_fusion.1.do_ref
  299.1 2.5 convolution_convert_fusion.3
  301.6 70.1 %attend_bwd.2 = (bf16[1,768,768]{2,1,0:T(8,128)(2,1)}, bf16[1,768,768]{2,1,0:T(8,128)(2,1)}, bf16[1,768,768]{2,1,0:T(8,128)(2,1)}, f32[1024,768]{1,0:T(8,128)}, ...) custom-call(s32[1]{0:T(128)S(6)} %copy.153.fl_ref, ...), custom_call_target="tpu_custom_call" | custom-call | flops 23353884672 | bytes 12582912 | tf_op jit(solution)/shard_map/attend_bwd/pallas_call | solution.py:162
  371.7 2.1 reduce_sum.254
  373.8 2.5 multiply_reduce_fusion.8
  376.6 3.1 multiply_reduce_fusion.1
  379.7 1.5 fusion.35
  381.6 3.1 convert_reduce_fusion.2
  384.8 35.8 %feed_bwd.3 = (f32[1024,768]{1,0:T(8,128)}, bf16[768,3072]{1,0:T(8,128)(2,1)}, bf16[3072,768]{1,0:T(8,128)(2,1)}, f32[1,3072]{1,0:T(1,128)}, f32[24,768]{1,0:T(8...) custom-call(bf16[1024,768]{1,0:T(8,128)(2,1)} %get-tuple-element.172.g_ref, bf16[1024,3072]{1,0:T(8,128)(2,1)} %get-tuple-element.95.u_ref, ...), custom_call_target="tpu_custom_call" | custom-call | flops 19327352832 | bytes 31457280 | tf_op jit(solution)/shard_map/feed_bwd/pallas_call | solution.py:233
  420.6 3.0 multiply_reduce_fusion.2
  423.7 1.5 fusion.34
  427.6 2.6 convolution_convert_fusion.do_ref
  430.2 2.5 convolution_convert_fusion.2
  432.6 69.9 %attend_bwd.3 = (bf16[1,768,768]{2,1,0:T(8,128)(2,1)}, bf16[1,768,768]{2,1,0:T(8,128)(2,1)}, bf16[1,768,768]{2,1,0:T(8,128)(2,1)}, f32[1024,768]{1,0:T(8,128)}, ...) custom-call(s32[1]{0:T(128)S(6)} %copy.153.fl_ref, ...), custom_call_target="tpu_custom_call" | custom-call | flops 23353884672 | bytes 12582912 | tf_op jit(solution)/shard_map/attend_bwd/pallas_call | solution.py:162
  502.8 3.2 fusion.31
  506.1 1.7 multiply_reduce_fusion.3
  508.0 2.6 add_convert_fusion
  514.5 31.7 %scatter.1 = (f32[24,768]{1,0:T(8,128)}, f32[24,768]{1,0:T(8,128)}, f32[24,768]{1,0:T(8,128)}, f32[24,256]{1,0:T(8,128)}) custom-call(bf16[2,2,4,2,24,768]{5,4,3,2,1,0:T(8,128)(2,1)} %bitcast.121, bf16[2,2,4,2,24,768]{5,4,3,2,1,0:T(8,128)(2,1)} %bitcast.122, bf16[2,2,4,2,24,768]{5,4,3,2,1,0:T(8,128)(2,1)} %bitcast.123, f32[2,2,4,2,24,256]{5,4,3,2,1,0:T(8,128)} %bitcast.120), custom_call_target="tpu_custom_call" | custom-call | tf_op jit(solution)/shard_map/scatter/pallas_call | solution.py:572
  (203 shorter events, 45.9 us)
Async XLA Ops:
  0.6 45.1 %copy-start.7 = (bf16[1024,768]{1,0:T(8,128)(2,1)S(1)}, bf16[1024,768]{1,0:T(8,128)(2,1)}, u32[]{:S(2)}) copy-start(bf16[1024,768]{1,0:T(8,128)(2,1)} %param.17) | copy-start | bytes 4718596
  47.8 6.6 %copy-start.28 = (bf16[4,24,768]{2,1,0:T(8,128)(2,1)S(1)}, bf16[4,24,768]{2,1,0:T(8,128)(2,1)}, u32[]{:S(2)}) copy-start(bf16[4,24,768]{2,1,0:T(8,128)(2,1)} %param.26) | copy-start | bytes 442372
  123.3 2.3 copy-start.1
  169.4 63.5 %copy-start.3 = (f32[1024,768]{1,0:T(8,128)S(1)}, f32[1024,768]{1,0:T(8,128)}, u32[]{:S(2)}) copy-start(f32[1024,768]{1,0:T(8,128)} %get-tuple-element.77.hid_ref) | copy-start | bytes 9437188
  261.0 2.0 copy-start
  263.0 27.0 %copy-start.6 = (f32[1024,768]{1,0:T(8,128)S(1)}, f32[1024,768]{1,0:T(8,128)}, u32[]{:S(2)}) copy-start(f32[1024,768]{1,0:T(8,128)} %copy-done.5) | copy-start | bytes 9437188
  290.0 3.0 copy-start.17
  294.3 2.2 copy-start.35
  296.5 2.6 copy-start.36
  373.8 2.8 copy-start.4
  376.6 3.1 copy-start.15
  384.8 35.8 %copy-start.2 = (f32[1024,768]{1,0:T(8,128)S(1)}, f32[1024,768]{1,0:T(8,128)}, u32[]{:S(2)}) copy-start(f32[1024,768]{1,0:T(8,128)} %copy-done.1) | copy-start | bytes 9437188
  420.6 3.1 copy-start.16
  425.5 2.0 copy-start.34
  427.6 2.6 copy-start.37
  432.6 69.9 %copy-start.8 = (bf16[1024,768]{1,0:T(8,128)(2,1)S(1)}, bf16[1024,768]{1,0:T(8,128)(2,1)}, u32[]{:S(2)}) copy-start(bf16[1024,768]{1,0:T(8,128)(2,1)} %param.17) | copy-start | bytes 4718596
  432.6 70.2 %copy-start.27 = (f32[768]{0:T(1024)S(1)}, f32[768]{0:T(1024)}, u32[]{:S(2)}) copy-start(f32[768]{0:T(1024)} %get-tuple-element.145) | copy-start | bytes 9220
  502.5 3.6 copy-start.14
  507.9 4.1 copy-start.30
  507.9 4.1 copy-start.31
  507.9 4.3 copy-start.29
  507.9 5.2 copy-start.32
  507.9 5.2 copy-start.33
  513.3 36.3 %copy-start.23 = (f32[24,768]{1,0:T(8,128)S(1)}, f32[24,768]{1,0:T(8,128)}, u32[]{:S(2)}) copy-start(f32[24,768]{1,0:T(8,128)} %get-tuple-element.122) | copy-start | bytes 221188
  513.3 36.3 %copy-start.24 = (f32[24,768]{1,0:T(8,128)S(1)}, f32[24,768]{1,0:T(8,128)}, u32[]{:S(2)}) copy-start(f32[24,768]{1,0:T(8,128)} %get-tuple-element.123) | copy-start | bytes 221188
  513.3 36.3 %copy-start.25 = (f32[24,768]{1,0:T(8,128)S(1)}, f32[24,768]{1,0:T(8,128)}, u32[]{:S(2)}) copy-start(f32[24,768]{1,0:T(8,128)} %get-tuple-element.124) | copy-start | bytes 221188
  514.5 37.2 %copy-start.22 = (f32[24,768]{1,0:T(8,128)S(1)}, f32[24,768]{1,0:T(8,128)}, u32[]{:S(2)}) copy-start(f32[24,768]{1,0:T(8,128)} %get-tuple-element.126) | copy-start | bytes 221188
  514.5 37.2 %copy-start.26 = (f32[24,768]{1,0:T(8,128)S(1)}, f32[24,768]{1,0:T(8,128)}, u32[]{:S(2)}) copy-start(f32[24,768]{1,0:T(8,128)} %get-tuple-element.125) | copy-start | bytes 221188
  514.5 38.0 %copy-start.19 = (f32[24,3072]{1,0:T(8,128)S(1)}, f32[24,3072]{1,0:T(8,128)}, u32[]{:S(2)}) copy-start(f32[24,3072]{1,0:T(8,128)} %get-tuple-element.128) | copy-start | bytes 884740
  514.5 38.0 %copy-start.21 = (f32[24,3072]{1,0:T(8,128)S(1)}, f32[24,3072]{1,0:T(8,128)}, u32[]{:S(2)}) copy-start(f32[24,3072]{1,0:T(8,128)} %get-tuple-element.127) | copy-start | bytes 884740
  546.2 8.7 %copy-start.18 = (f32[96,768]{1,0:T(8,128)S(1)}, f32[96,768]{1,0:T(8,128)}, u32[]{:S(2)}) copy-start(f32[96,768]{1,0:T(8,128)} %get-tuple-element.130) | copy-start | bytes 884740
  546.2 8.7 %copy-start.20 = (f32[96,768]{1,0:T(8,128)S(1)}, f32[96,768]{1,0:T(8,128)}, u32[]{:S(2)}) copy-start(f32[96,768]{1,0:T(8,128)} %get-tuple-element.129) | copy-start | bytes 884740
  (6 other events, 10.7 us)

commit v8 on v7

--- a/solution.py
+++ b/solution.py
@@ -23,7 +23,7 @@
     z=jnp.zeros_like(x)
     return jnp.where(lane<64,x,z), jnp.where(lane<64,z,x)
 
-def fwd_kernel(fl_ref,hid_ref,ga_ref,sa_ref,wq_ref,wk_ref,wv_ref,qb_ref,vb_ref,*rest,bq,host):
+def fwd_kernel(fl_ref,hid_ref,vec_ref,wq_ref,wk_ref,wv_ref,part_ref,*rest,bq,host):
     n=host.count
     q_ref,k_ref,v_ref,normed_ref,o_ref,lse_ref=rest[n:n+6]
     jobs=host.enter(rest[:n],rest[n+6:2*n+6],rest[2*n+6:])
@@ -31,12 +31,12 @@
     @pl.when(pl.program_id(1)==0)
     def _():
         for lo in range(0,L,bq):
-            normed_ref[lo:lo+bq,:]=layer_norm(hid_ref[lo:lo+bq,:],ga_ref[...],sa_ref[...]).astype(BF)
+            normed_ref[lo:lo+bq,:]=layer_norm(hid_ref[lo:lo+bq,:].astype(F32),vec_ref[0:1,:],vec_ref[1:2,:]).astype(BF)
     w=jnp.concatenate([wq_ref[...],wk_ref[...],wv_ref[...]],axis=1)
     qkv=nn(normed_ref[...],w)
-    q_ref[...]=(qkv[:,:128]+qb_ref[...]).astype(BF)
+    q_ref[...]=(qkv[:,:128]+part_ref[2:3,:]).astype(BF)
     k_ref[...]=qkv[:,128:256].astype(BF)
-    v_ref[...]=(qkv[:,256:]+vb_ref[...]).astype(BF)
+    v_ref[...]=(qkv[:,256:]+part_ref[3:4,:]).astype(BF)
     second=fl_ref[pl.program_id(0)]<L
     shut=jnp.where(second,F32(1e9),F32(0.))
     q=q_ref[...]*BF(0.125); k=k_ref[...]; vT=v_ref[...].T
@@ -79,20 +79,19 @@
     col=lambda off: pl.BlockSpec((D,128),lambda r,g,fl:(0,off*G+g))
     blk=pl.BlockSpec((L,128),lambda r,g,fl:(r,g))
     row=pl.BlockSpec((L,D),lambda r,g,fl:(r,0))
-    vec=pl.BlockSpec((1,D),lambda r,g,fl:(0,0)); part=pl.BlockSpec((1,128),lambda r,g,fl:(0,g))
+    vec=pl.BlockSpec((8,D),lambda r,g,fl:(0,0)); part=pl.BlockSpec((8,128),lambda r,g,fl:(0,g))
     narrow=jax.ShapeDtypeStruct((N,D),BF)
     return pl.pallas_call(functools.partial(fwd_kernel,bq=bq,host=host),
         grid_spec=pltpu.PrefetchScalarGridSpec(num_scalar_prefetch=1,grid=(R,G),
-          in_specs=[row,vec,vec,col(0),col(1),col(2),part,part]+host.ins,
+          in_specs=[row,vec,col(0),col(1),col(2),part]+host.ins,
           out_specs=[blk,blk,blk,row,blk,pl.BlockSpec((1,2,L),lambda r,g,fl:(r*G+g,0,0))]+host.outs,
           scratch_shapes=host.scratch),
         out_shape=[narrow]*5+[jax.ShapeDtypeStruct((R*G,2,L),F32)]+host.shapes,
         compiler_params=host.params(),
         cost_estimate=pl.CostEstimate(flops=2*2*R*L*L*D*2+6*N*D*D,bytes_accessed=N*D*14,transcendentals=R*L*L*12//2),
-        name="attend_fwd")(fl,hidden,w["ga"][None],w["sa"][None],w["heads"],w["heads"],w["heads"],
-                           w["qb"][None],w["vb"][None],*host.arrays)
-
-def bwd_kernel(fl_ref,q_ref,k_ref,v_ref,do_ref,lse_ref,normed_ref,wq_ref,wk_ref,wv_ref,*rest,bq,host):
+        name="attend_fwd")(fl,hidden,w["vecs"],w["heads"],w["heads"],w["heads"],w["vecs"],*host.arrays)
+
+def bwd_kernel(fl_ref,q_ref,k_ref,v_ref,dm_ref,mix_ref,lse_ref,normed_ref,wq_ref,wk_ref,wv_ref,*rest,bq,host):
     n=host.count
     gq_ref,gk_ref,gv_ref,da_ref,qb_ref,vb_ref=rest[n:n+6]
     dk_acc,dv_acc,dqkv=rest[2*n+6:2*n+9]
@@ -100,7 +99,7 @@
     L=q_ref.shape[0]; half=L//2
     second=fl_ref[pl.program_id(0)]<L
     shut=jnp.where(second,F32(1e9),F32(0.))
-    q=q_ref[...]*BF(0.125); k=k_ref[...]; v=v_ref[...]; do=do_ref[...]
+    q=q_ref[...]*BF(0.125); k=k_ref[...]; v=v_ref[...]; do=nt(dm_ref[...],mix_ref[...]).astype(BF)
     kT=k.T
     sub=lax.broadcasted_iota(jnp.int32,kT.shape,0); zero=jnp.zeros_like(kT)
     kTs=(jnp.where(sub<64,kT,zero),jnp.where(sub<64,zero,kT))
@@ -153,7 +152,7 @@
     def _(): da_ref[...]+=da
     host.leave(jobs)
 
-def attend_bwd(q,k,v,do,lse,normed,w,fl,host,bq=256):
+def attend_bwd(q,k,v,dmb,lse,normed,w,fl,host,bq=256):
     N,D=q.shape; R=fl.shape[0]; L=N//R; G=D//128
     blk=pl.BlockSpec((L,128),lambda r,g,fl:(r,g))
     row=pl.BlockSpec((L,D),lambda r,g,fl:(r,0))
@@ -161,14 +160,14 @@
     term=pl.BlockSpec((1,D,128),lambda r,g,fl:(r,0,g)); part=pl.BlockSpec((1,1,128),lambda r,g,fl:(r,0,g))
     gq,gk,gv,da,qb,vb,*more=pl.pallas_call(functools.partial(bwd_kernel,bq=bq,host=host),
         grid_spec=pltpu.PrefetchScalarGridSpec(num_scalar_prefetch=1,grid=(R,G),
-          in_specs=[blk]*4+[pl.BlockSpec((1,2,L),lambda r,g,fl:(r*G+g,0,0)),row,col(0),col(1),col(2)]+host.ins,
+          in_specs=[blk]*3+[row,pl.BlockSpec((128,D),lambda r,g,fl:(g,0)),pl.BlockSpec((1,2,L),lambda r,g,fl:(r*G+g,0,0)),row,col(0),col(1),col(2)]+host.ins,
           out_specs=[term]*3+[row,part,part]+host.outs,
           scratch_shapes=[pltpu.VMEM((L,128),F32),pltpu.VMEM((L,128),F32),pltpu.VMEM((L,384),BF)]+host.scratch),
         out_shape=[jax.ShapeDtypeStruct((R,D,D),BF)]*3+[jax.ShapeDtypeStruct((N,D),F32)]
           +[jax.ShapeDtypeStruct((R,1,D),F32)]*2+host.shapes,
         compiler_params=host.params(),
         cost_estimate=pl.CostEstimate(flops=5*2*R*L*L*D*2+12*N*D*D,bytes_accessed=N*D*16,transcendentals=R*L*L*12//2),
-        name="attend_bwd")(fl,q,k,v,do,lse,normed,w["heads"],w["heads"],w["heads"],*host.arrays)
+        name="attend_bwd")(fl,q,k,v,dmb,w["mix"],lse,normed,w["heads"],w["heads"],w["heads"],*host.arrays)
     gq,gk,gv=[t[0] if R==1 else jnp.sum(t.astype(F32),axis=0).astype(BF) for t in (gq,gk,gv)]
     return [gq,gk,gv],da,jnp.sum(qb,axis=(0,1)),jnp.sum(vb,axis=(0,1)),more
 
@@ -182,7 +181,7 @@
     N=c_ref.shape[0]
     e=e_ref[...]; s=s_ref[...]; eb=eb_ref[...]
     @pl.when(pl.program_id(0)==0)
-    def _(): h_ref[...]=m_ref[...]+sb_ref[...]
+    def _(): h_ref[...]=m_ref[...]+sb_ref[7:8,:]
     for j in range(N//rows):
         host.tick(jobs,j)
         at=slice(j*rows,(j+1)*rows)
@@ -196,12 +195,12 @@
     fixed=lambda r: pl.BlockSpec((r,D),lambda t: (0,0))
     return pl.pallas_call(functools.partial(feed_fwd_kernel,rows=rows,host=host),grid=(F//tile,),
         in_specs=[fixed(N),pl.BlockSpec((D,tile),lambda t:(0,t)),pl.BlockSpec((1,tile),lambda t:(0,t)),
-                  pl.BlockSpec((tile,D),lambda t:(t,0)),fixed(N),fixed(1)]+host.ins,
+                  pl.BlockSpec((tile,D),lambda t:(t,0)),fixed(N),fixed(8)]+host.ins,
         out_specs=[fixed(N)]+[pl.BlockSpec((N,tile),lambda t:(0,t))]*2+host.outs,
         out_shape=[jax.ShapeDtypeStruct((N,D),F32)]+[jax.ShapeDtypeStruct((N,F),BF)]*2+host.shapes,
         scratch_shapes=host.scratch,compiler_params=host.params(),
         cost_estimate=pl.CostEstimate(flops=4*N*D*F,bytes_accessed=4*N*F+4*D*F,transcendentals=N*F),
-        name="feed_fwd")(c,w["expand"],w["eb"][None],w["shrink"],middle,w["sb"][None],*host.arrays)
+        name="feed_fwd")(c,w["expand"],w["eb"],w["shrink"],middle,w["vecs"],*host.arrays)
 
 def feed_bwd_kernel(g_ref,u_ref,slope_ref,c_ref,e_ref,s_ref,*rest,rows,host):
     n=host.count
@@ -617,23 +616,51 @@
     return [turned[i] for i in range(vector_count)], wide
 
 
-def local_shards(local):
-    (ga, sa, hw, qb, vb, mw, mb, gf, sf, ew, eb, sw, sb) = local
-    small = pack_columns([ga, sa, qb, vb, mb, gf, sf, sb], eb, 1)
-    return [jnp.concatenate([hw, small], axis=1), mw, ew, sw]
+def pick_kernel(tie_ref, *refs):
+    n = 5 * LAYERS
+    for i in range(LAYERS):
+        heads, small, mix, expand, shrink = refs[5 * i : 5 * i + 5]
+        outs = refs[n + 4 * i : n + 4 * i + 4]
+        width = heads.shape[-1]
+        outs[0][:, :width] = heads[0]
+        outs[0][:, width:] = small[0]
+        for out, ref in zip(outs[1:], (mix, expand, shrink)):
+            out[...] = ref[0]
+
+
+def pick_shards(tie_map, stacks):
+    (ga, sa, hw, qb, vb, mw, mb, gf, sf, ew, eb, sw, sb) = stacks
+    per = ga.shape[1]
+    small = jnp.stack([ga, sa, qb, vb, mb, gf, sf, sb], axis=1)
+    small = jnp.concatenate([small, eb.reshape(UNIQUE, -1, per)], axis=1).transpose(0, 2, 1)
+    small = jnp.pad(small, ((0, 0), (0, 0), (0, LANES - small.shape[2])))
+    arrays = [hw, small, mw, ew, sw]
+    shapes = [(per, hw.shape[2] + LANES), mw.shape[1:], ew.shape[1:], sw.shape[1:]] * LAYERS
+    specs = [pl.BlockSpec((1,) + a.shape[1:], lambda g, tie, use=i: (tie[use], 0, 0))
+             for i in range(LAYERS) for a in arrays]
+    outs = pl.pallas_call(
+        pick_kernel,
+        grid_spec=pltpu.PrefetchScalarGridSpec(
+            num_scalar_prefetch=1, grid=(1,), in_specs=specs,
+            out_specs=[pl.BlockSpec(shape, lambda g, tie: (0, 0)) for shape in shapes]),
+        out_shape=[jax.ShapeDtypeStruct(shape, BF) for shape in shapes],
+        name="pick")(tie_map, *(arrays * LAYERS))
+    return [outs[4 * i : 4 * i + 4] for i in range(LAYERS)]
 
 
 def use_heads(heads, width, ways):
-    vecs, wide = unpack_columns(heads[:, 3 * width :], 8, ways, lax.axis_size(AX))
-    vecs = [v.astype(F32) for v in vecs]
-    return dict(zip(("ga", "sa", "qb", "vb", "mb", "gf", "sf", "sb"), vecs), eb=wide.astype(F32),
-                heads=heads)
+    count = lax.axis_size(AX)
+    turned = heads[:, 3 * width : 3 * width + 8 + ways].T.astype(F32)
+    wide = turned[8:].reshape(ways, count, width // count).transpose(1, 0, 2).reshape(1, -1)
+    vecs = turned[:8]
+    return dict(vecs=vecs, ga=vecs[0], sa=vecs[1], mb=vecs[4], gf=vecs[5], sf=vecs[6], eb=wide, heads=heads)
 
 
 def forward_use(hidden, w, first_len, host, spare_host):
     q, k, v, normed, attended, lse, *more = attend_fwd(hidden, w, first_len, host)
     more = host.results(more)
     w.update(expand=more[0], shrink=more[1], mix=more[-1])
+    hidden = hidden.astype(F32)
     middle = hidden + jnp.dot(attended, w["mix"], preferred_element_type=F32) + w["mb"]
     normed_two = layer_norm(middle, w["gf"], w["sf"]).astype(BF)
     result, activated, slope, *spare = feed_fwd(normed_two, w, middle, spare_host)
@@ -656,10 +683,9 @@
     dmb = dm.astype(BF)
     mix_term = inner_rows(attended, dmb).astype(BF)
     mb = column_sums(dmb)
-    do = times_transposed(dmb, w["mix"]).astype(BF)
     host = Host(Scatter, [shrink_term, mix_term, expand_term], ident, BACKWARD_SLOTS, per=4,
                 pieces=8, window=3)
-    heads_terms, da, qb, vb, more = attend_bwd(*qkv, do, lse, normed, w, first_len, host)
+    heads_terms, da, qb, vb, more = attend_bwd(*qkv, dmb, lse, normed, w, first_len, host)
     more = host.results(more)
     unused, first_back = jax.vjp(layer_norm, hidden, w["ga"], w["sa"])
     hidden_norm, ga, sa = first_back(da)
@@ -678,10 +704,6 @@
 BACKWARD_SLOTS = [1.8, 1.35, 0.9, 2.9] * 6
 FEED_FORWARD_SLOTS = [0.95, 0.95, 0.95, 0.95] * 6
 FEED_BACKWARD_SLOTS = [0.7, 0.7, 0.7, 2.3] * 6
-
-
-def pick_shards(stacks, source):
-    return tuple(lax.dynamic_index_in_dim(stack, source, 0, keepdims=False) for stack in stacks)
 
 
 def place_terms(sources, shares):
@@ -697,10 +719,10 @@
 
 
 def body(tokens, cotangent, tie_map, first_length, *stacks):
-    hidden = tokens.astype(F32)
+    hidden = tokens
     width = hidden.shape[1]
     sources = [tie_map[i] for i in range(LAYERS)]
-    shards = [local_shards(pick_shards(stacks, s)) for s in sources]
+    shards = pick_shards(tie_map, stacks)
     ways = shards[0][3].shape[0] // shards[0][0].shape[0]
     (heads,) = exchange(Gather, shards[0][:1], 0, "gather", 4)
     kept, weights = [], []

time: 560 us -> 551 us (0.984)
  Pallas kernels: 452 us -> 464 us
  other arithmetic: 53.7 us -> 45.9 us
    pallas_call x2, Pallas kernels: 140 us -> 150 us  [attend_bwd(): pl.pallas_call(functools.partial(bwd_kernel, bq=bq, host=host), grid_spec...]
    another operation x0 -> x8, local copies, waits for them, and re-layouts: none -> 6.32 us  [pick_shards(): small = jnp.stack([ga, sa, qb, vb, mb, gf, sf, sb], axis=1)]
    convert_element_type x11 -> x2, other arithmetic: 7.68 us -> 1.91 us  [use_heads(): turned = heads[:, 3 * width:3 * width + 8 + ways].T.astype(F32)]
where the time goes in v8:
time: 551 us; the launch traced here: 548 us
  Pallas kernels  464 us (84%)
  other arithmetic  45.9 us (8%)
  local copies, waits for them, and re-layouts  23.6 us (4%)
  matrix products  11.5 us (2%)
    pallas_call x2, Pallas kernels, attend_bwd(): pl.pallas_call(functools.partial(bwd_kernel, bq=bq, host=host), grid_spec...  150 us
    pallas_call x2, Pallas kernels, attend_fwd(): pl.pallas_call(functools.partial(fwd_kernel, bq=bq, host=host), grid_spec...  128 us
    pallas_call x2, Pallas kernels, feed_bwd(): pl.pallas_call(functools.partial(feed_bwd_kernel, rows=rows, host=host),...  62.8 us
    pallas_call x2, Pallas kernels, exchange(): pl.pallas_call(functools.partial(alone_kernel, host=host), grid=(1,), in_...  62.3 us
    pallas_call x2, Pallas kernels, feed_fwd(): pl.pallas_call(functools.partial(feed_fwd_kernel, rows=rows, host=host),...  58.1 us
    reduce_sum x5, other arithmetic, layer_norm(): return centre * lax.rsqrt(spread + EPS) * gain + shift  13.9 us

profile of v8, /device:TPU:0, one launch (start us, length us, event | category | flops | bytes accessed | tf_op | source)
XLA Modules:
  0.0 547.6 jit_solution(9806875554375734763)
XLA Ops:
  8.6 2.9 pick.1
  11.5 30.8 %gather.1 = bf16[2,2,4,2,24,2432]{5,4,3,2,1,0:T(8,128)(2,1)} custom-call(bf16[24,2432]{1,0:T(8,128)(2,1)} %get-tuple-element.81.refs_0_), custom_call_target="tpu_custom_call" | custom-call | tf_op jit(solution)/shard_map/gather/pallas_call | solution.py:571
  45.7 64.7 %attend_fwd.2 = (bf16[1024,768]{1,0:T(8,128)(2,1)}, bf16[1024,768]{1,0:T(8,128)(2,1)}, bf16[1024,768]{1,0:T(8,128)(2,1)}, bf16[1024,768]{1,0:T(8,128)(2,1)}, bf1...) custom-call(s32[1]{0:T(128)S(6)} %copy.113.fl_ref, ...), custom_call_target="tpu_custom_call" | custom-call | flops 10066329600 | bytes 11010048 | tf_op jit(solution)/shard_map/attend_fwd/pallas_call | solution.py:84
  110.4 3.3 fusion.23
  114.3 1.7 add_convert_fusion.2.c_ref
  117.2 35.7 %feed_fwd.2 = (f32[1024,768]{1,0:T(8,128)}, bf16[1024,3072]{1,0:T(8,128)(2,1)}, bf16[1024,3072]{1,0:T(8,128)(2,1)}, bf16[2,2,4,2,24,2432]{5,4,3,2,1,0:T(8,128)(2,1)}) custom-call(bf16[1024,768]{1,0:T(8,128)(2,1)} %add_convert_fusion.2.c_ref, bf16[768,3072]{1,0:T(8,128)(2,1)} %bitcast.103, f32[1,3072]{1,0:T(1,128)} %reshape.289.eb_ref, ...), custom_call_target="tpu_custom_call" | custom-call | flops 9663676416 | bytes 22020096 | tf_op jit(solution)/shard_map/feed_fwd/pallas_call | solution.py:196
  155.4 63.5 %attend_fwd.3 = (bf16[1024,768]{1,0:T(8,128)(2,1)}, bf16[1024,768]{1,0:T(8,128)(2,1)}, bf16[1024,768]{1,0:T(8,128)(2,1)}, bf16[1024,768]{1,0:T(8,128)(2,1)}, bf1...) custom-call(s32[1]{0:T(128)S(6)} %copy.113.fl_ref, ...), custom_call_target="tpu_custom_call" | custom-call | flops 10066329600 | bytes 11010048 | tf_op jit(solution)/shard_map/attend_fwd/pallas_call | solution.py:84
  218.9 3.3 fusion.24
  224.4 22.4 %feed_fwd.3 = (f32[1024,768]{1,0:T(8,128)S(1)}, bf16[1024,3072]{1,0:T(8,128)(2,1)}, bf16[1024,3072]{1,0:T(8,128)(2,1)}) custom-call(bf16[1024,768]{1,0:T(8,128)(2,1)S(1)} %add_convert_fusion.1.c_ref, bf16[768,3072]{1,0:T(8,128)(2,1)} %bitcast.111, f32[1,3072]{1,0:T(1,128)S(1)} %reshape.295.eb_ref, bf16[3072,768]{1,0:T(8,128)(2,1)} %bitcast.113, ...), custom_call_target="tpu_custom_call" | custom-call | flops 9663676416 | bytes 22020096 | tf_op jit(solution)/shard_map/feed_fwd/pallas_call | solution.py:196
  246.9 1.3 convert_element_type.68
  248.8 27.0 %feed_bwd.2 = (f32[1024,768]{1,0:T(8,128)}, bf16[768,3072]{1,0:T(8,128)(2,1)}, bf16[3072,768]{1,0:T(8,128)(2,1)}, f32[1,3072]{1,0:T(1,128)S(1)}) custom-call(bf16[1024,768]{1,0:T(8,128)(2,1)S(1)} %copy-done, bf16[1024,3072]{1,0:T(8,128)(2,1)} %get-tuple-element.100.u_ref, bf16[1024,3072]{1,0:T(8,128)(2,1)} %get-tuple-element.101.slope_ref, ...), custom_call_target="tpu_custom_call" | custom-call | flops 19327352832 | bytes 31457280 | tf_op jit(solution)/shard_map/feed_bwd/pallas_call | solution.py:232
  275.9 2.9 multiply_reduce_fusion
  278.9 1.4 fusion.21
  282.8 2.5 convolution_convert_fusion.1
  285.3 75.3 %attend_bwd.2 = (bf16[1,768,768]{2,1,0:T(8,128)(2,1)}, bf16[1,768,768]{2,1,0:T(8,128)(2,1)}, bf16[1,768,768]{2,1,0:T(8,128)(2,1)}, f32[1024,768]{1,0:T(8,128)}, ...) custom-call(s32[1]{0:T(128)S(6)} %copy.113.fl_ref, ...), custom_call_target="tpu_custom_call" | custom-call | flops 23353884672 | bytes 12582912 | tf_op jit(solution)/shard_map/attend_bwd/pallas_call | solution.py:161
  360.5 2.1 reduce_sum.254
  362.7 2.5 multiply_reduce_fusion.5
  365.5 3.1 multiply_reduce_fusion.1
  368.6 1.5 fusion.20
  370.5 3.1 convert_reduce_fusion.3
  373.6 35.8 %feed_bwd.3 = (f32[1024,768]{1,0:T(8,128)}, bf16[768,3072]{1,0:T(8,128)(2,1)}, bf16[3072,768]{1,0:T(8,128)(2,1)}, f32[1,3072]{1,0:T(1,128)}, f32[24,768]{1,0:T(8...) custom-call(bf16[1024,768]{1,0:T(8,128)(2,1)} %get-tuple-element.186.g_ref, bf16[1024,3072]{1,0:T(8,128)(2,1)} %get-tuple-element.111.u_ref, ...), custom_call_target="tpu_custom_call" | custom-call | flops 19327352832 | bytes 31457280 | tf_op jit(solution)/shard_map/feed_bwd/pallas_call | solution.py:232
  409.5 3.0 multiply_reduce_fusion.2
  412.5 1.5 fusion.19
  416.5 2.5 convolution_convert_fusion
  418.9 74.7 %attend_bwd.3 = (bf16[1,768,768]{2,1,0:T(8,128)(2,1)}, bf16[1,768,768]{2,1,0:T(8,128)(2,1)}, bf16[1,768,768]{2,1,0:T(8,128)(2,1)}, f32[1024,768]{1,0:T(8,128)}, ...) custom-call(s32[1]{0:T(128)S(6)} %copy.113.fl_ref, ...), custom_call_target="tpu_custom_call" | custom-call | flops 23353884672 | bytes 12582912 | tf_op jit(solution)/shard_map/attend_bwd/pallas_call | solution.py:161
  493.7 3.2 fusion.16
  496.9 1.7 fusion.7
  498.8 2.6 add_convert_fusion
  505.4 31.5 %scatter.1 = (f32[24,768]{1,0:T(8,128)}, f32[24,768]{1,0:T(8,128)}, f32[24,768]{1,0:T(8,128)}, f32[24,256]{1,0:T(8,128)}) custom-call(bf16[2,2,4,2,24,768]{5,4,3,2,1,0:T(8,128)(2,1)} %bitcast.76, bf16[2,2,4,2,24,768]{5,4,3,2,1,0:T(8,128)(2,1)} %bitcast.77, bf16[2,2,4,2,24,768]{5,4,3,2,1,0:T(8,128)(2,1)} %bitcast.78, f32[2,2,4,2,24,256]{5,4,3,2,1,0:T(8,128)} %bitcast.73), custom_call_target="tpu_custom_call" | custom-call | tf_op jit(solution)/shard_map/scatter/pallas_call | solution.py:571
  538.9 1.3 iota_compare_fusion.2
  543.8 1.2 select_add_fusion.1
  546.2 1.2 select_add_fusion
  (163 shorter events, 34.1 us)
Async XLA Ops:
  45.7 64.7 %copy-start.14 = (bf16[1024,768]{1,0:T(8,128)(2,1)S(1)}, bf16[1024,768]{1,0:T(8,128)(2,1)}, u32[]{:S(2)}) copy-start(bf16[1024,768]{1,0:T(8,128)(2,1)} %hid_ref.1) | copy-start | bytes 4718596
  113.7 2.3 copy-start.2
  155.4 63.5 %copy-start.4 = (f32[1024,768]{1,0:T(8,128)S(1)}, f32[1024,768]{1,0:T(8,128)}, u32[]{:S(2)}) copy-start(f32[1024,768]{1,0:T(8,128)} %get-tuple-element.90.hid_ref) | copy-start | bytes 9437188
  246.8 2.0 copy-start
  248.8 27.0 %copy-start.7 = (f32[1024,768]{1,0:T(8,128)S(1)}, f32[1024,768]{1,0:T(8,128)}, u32[]{:S(2)}) copy-start(f32[1024,768]{1,0:T(8,128)} %copy-done.6) | copy-start | bytes 9437188
  275.9 3.0 copy-start.18
  280.2 2.5 copy-start.37
  282.0 3.3 copy-start.20
  362.6 2.8 copy-start.5
  365.5 3.1 copy-start.16
  368.6 1.9 copy-start.10
  373.6 35.8 %copy-start.3 = (f32[1024,768]{1,0:T(8,128)S(1)}, f32[1024,768]{1,0:T(8,128)}, u32[]{:S(2)}) copy-start(f32[1024,768]{1,0:T(8,128)} %copy-done.2) | copy-start | bytes 9437188
  409.4 3.0 copy-start.17
  412.5 2.4 copy-start.8
  415.7 3.3 copy-start.19
  418.9 74.8 %copy-start.30 = (f32[768]{0:T(1024)S(1)}, f32[768]{0:T(1024)}, u32[]{:S(2)}) copy-start(f32[768]{0:T(1024)} %get-tuple-element.161) | copy-start | bytes 9220
  493.7 3.2 copy-start.13
  498.8 4.2 copy-start.33
  498.8 4.2 copy-start.34
  498.8 4.3 copy-start.31
  498.8 5.2 copy-start.35
  498.8 5.2 copy-start.36
  504.2 34.1 %copy-start.32 = (s32[12]{0:T(128)S(1)}, s32[12]{0:T(128)}, u32[]{:S(2)}) copy-start(s32[12]{0:T(128)} %tie_ref.1) | copy-start | bytes 148
  504.2 36.7 %copy-start.26 = (f32[24,768]{1,0:T(8,128)S(1)}, f32[24,768]{1,0:T(8,128)}, u32[]{:S(2)}) copy-start(f32[24,768]{1,0:T(8,128)} %get-tuple-element.138) | copy-start | bytes 221188
  504.2 36.7 %copy-start.27 = (f32[24,768]{1,0:T(8,128)S(1)}, f32[24,768]{1,0:T(8,128)}, u32[]{:S(2)}) copy-start(f32[24,768]{1,0:T(8,128)} %get-tuple-element.139) | copy-start | bytes 221188
  504.2 36.7 %copy-start.28 = (f32[24,768]{1,0:T(8,128)S(1)}, f32[24,768]{1,0:T(8,128)}, u32[]{:S(2)}) copy-start(f32[24,768]{1,0:T(8,128)} %get-tuple-element.140) | copy-start | bytes 221188
  505.4 37.6 %copy-start.25 = (f32[24,768]{1,0:T(8,128)S(1)}, f32[24,768]{1,0:T(8,128)}, u32[]{:S(2)}) copy-start(f32[24,768]{1,0:T(8,128)} %get-tuple-element.142) | copy-start | bytes 221188
  505.4 37.6 %copy-start.29 = (f32[24,768]{1,0:T(8,128)S(1)}, f32[24,768]{1,0:T(8,128)}, u32[]{:S(2)}) copy-start(f32[24,768]{1,0:T(8,128)} %get-tuple-element.141) | copy-start | bytes 221188
  505.4 38.4 %copy-start.22 = (f32[24,3072]{1,0:T(8,128)S(1)}, f32[24,3072]{1,0:T(8,128)}, u32[]{:S(2)}) copy-start(f32[24,3072]{1,0:T(8,128)} %get-tuple-element.144) | copy-start | bytes 884740
  505.4 38.4 %copy-start.24 = (f32[24,3072]{1,0:T(8,128)S(1)}, f32[24,3072]{1,0:T(8,128)}, u32[]{:S(2)}) copy-start(f32[24,3072]{1,0:T(8,128)} %get-tuple-element.143) | copy-start | bytes 884740
  536.9 9.3 %copy-start.21 = (f32[96,768]{1,0:T(8,128)S(1)}, f32[96,768]{1,0:T(8,128)}, u32[]{:S(2)}) copy-start(f32[96,768]{1,0:T(8,128)} %get-tuple-element.146) | copy-start | bytes 884740
  536.9 9.3 %copy-start.23 = (f32[96,768]{1,0:T(8,128)S(1)}, f32[96,768]{1,0:T(8,128)}, u32[]{:S(2)}) copy-start(f32[96,768]{1,0:T(8,128)} %get-tuple-element.145) | copy-start | bytes 884740
  (7 other events, 11.8 us)
